TPU v7x, 32 devices: a whole 2x2x4 slice. The times are simulated.
32 devices in a mesh: phase: 2 (over core), dp: 16 (over z, y, x).
Axes of the slice: x: 2, y: 2, z: 4, core: 2. Of those that a mesh axis runs over, the one named last changes fastest.
Arguments:
- token_vectors: bfloat16 [2, 2, 4096, 1024], P('phase', None, 'dp'), may hold values from -6 to 6
- generation_result_adjoint: bfloat16 [2, 4096, 1024], P(None, 'dp'), may hold values from -6 to 6
- sequence_labels: int32 [2, 16, 256], P(None, 'dp'), may hold values from 0 to 3, never falling along the last dimension, each value on 1 to 192 neighbouring positions
- inquiry_vectors: bfloat16 [2, 2048, 768], P(None, 'dp'), may hold values from -6 to 6
- inquiry_token_spans: int32 [2, 16, 4], P(None, 'dp'), may hold values from 1 to 64, 128 in all within a row
- document_vectors: float32 [2, 256, 768], P(None, 'dp'), may hold values from -0.3 to 0.3
- document_slots: int32 [2, 64, 5], P(None, 'dp'), may hold values from 0 to 15
- relevance_adjoint: float32 [2, 64, 5], P(None, 'dp'), may hold values from -6 to 6
- softness_scalar: float32 [1], replicated, may hold values from 0.5 to 2
- intrinsic_triple_map: bfloat16 [2, 1024, 3072], P('phase', 'dp'), may hold values from -0.1875 to 0.1875
- intrinsic_probe_content_offset: bfloat16 [2, 2048], P('phase', 'dp'), may hold values from -0.59765625 to 0.59765625
- intrinsic_mixing_result_map: bfloat16 [2, 1024, 1024], P('phase', 'dp'), may hold values from -0.75 to 0.75
- intrinsic_mixing_result_offset: bfloat16 [2, 1024], P('phase', 'dp'), may hold values from -1.1953125 to 1.1953125
- perceptron_widen_map: bfloat16 [2, 1024, 4096], P('phase', 'dp'), may hold values from -0.1875 to 0.1875
- perceptron_widen_offset: bfloat16 [2, 4096], P('phase', 'dp'), may hold values from -1.1953125 to 1.1953125
- perceptron_narrow_map: bfloat16 [2, 4096, 1024], P('phase', 'dp'), may hold values from -0.125 to 0.125
- perceptron_narrow_offset: bfloat16 [2, 1024], P('phase', 'dp'), may hold values from -1.1953125 to 1.1953125
- standardize_scales: bfloat16 [2, 2, 1024], P('phase', None, 'dp'), may hold values from 0.5 to 1.5
- standardize_shifts: bfloat16 [2, 2, 1024], P('phase', None, 'dp'), may hold values from -1.1953125 to 1.1953125
- encoded_mixing_probe_map: bfloat16 [1024, 1024], P(('phase', 'dp')), may hold values from -0.1875 to 0.1875
- encoded_mixing_probe_offset: bfloat16 [1024], P(('phase', 'dp')), may hold values from -0.59765625 to 0.59765625
- encoded_lookup_content_map: bfloat16 [1024, 2048], P(('phase', 'dp')), may hold values from -0.1875 to 0.1875
- encoded_mixing_content_offset: bfloat16 [1024], P(('phase', 'dp')), may hold values from -0.59765625 to 0.59765625
- encoded_mixing_result_map: bfloat16 [1024, 1024], P(('phase', 'dp')), may hold values from -0.75 to 0.75
- encoded_mixing_result_offset: bfloat16 [1024], P(('phase', 'dp')), may hold values from -1.1953125 to 1.1953125
- encoded_mixing_scale_factor: bfloat16 [1024], P(('phase', 'dp')), may hold values from 0.5 to 1.5
- encoded_mixing_scale_shift: bfloat16 [1024], P(('phase', 'dp')), may hold values from -1.1953125 to 1.1953125
- retriever_triple_map: bfloat16 [768, 2304], P(('phase', 'dp')), may hold values from -0.21875 to 0.21875
- retriever_probe_content_offset: bfloat16 [1536], P(('phase', 'dp')), may hold values from -0.59765625 to 0.59765625
- retriever_mixing_result_map: bfloat16 [768, 768], P(('phase', 'dp')), may hold values from -0.875 to 0.875
- retriever_mixing_result_offset: bfloat16 [768], P(('phase', 'dp')), may hold values from -1.1953125 to 1.1953125
- retriever_widen_map: bfloat16 [768, 3072], P(('phase', 'dp')), may hold values from -0.21875 to 0.21875
- retriever_widen_offset: bfloat16 [3072], P(('phase', 'dp')), may hold values from -1.1953125 to 1.1953125
- retriever_narrow_map: bfloat16 [3072, 768], P(('phase', 'dp')), may hold values from -0.15625 to 0.15625
- retriever_narrow_offset: bfloat16 [768], P(('phase', 'dp')), may hold values from -1.1953125 to 1.1953125
- retriever_standardize_scales: bfloat16 [2, 768], P(None, ('phase', 'dp')), may hold values from 0.5 to 1.5
- retriever_standardize_shifts: bfloat16 [2, 768], P(None, ('phase', 'dp')), may hold values from -1.1953125 to 1.1953125
Outputs:
- layer_out: bfloat16 [2, 2, 4096, 1024], P('phase', None, 'dp')
- input_grad: float32 [2, 2, 4096, 1024], P('phase', None, 'dp')
- scores: float32 [2, 64, 5], P('phase', 'dp')
- question_grad: float32 [2, 2048, 768], P('phase', 'dp')
- temperature_grad: float32 [1], replicated
- self_qkv_grad: float32 [2, 1024, 3072], P('phase', 'dp')
- self_qv_bias_grad: float32 [2, 2048], P('phase', 'dp')
- self_out_grad: float32 [2, 1024, 1024], P('phase', 'dp')
- self_out_bias_grad: float32 [2, 1024], P('phase', 'dp')
- ffn_in_grad: float32 [2, 1024, 4096], P('phase', 'dp')
- ffn_in_bias_grad: float32 [2, 4096], P('phase', 'dp')
- ffn_out_grad: float32 [2, 4096, 1024], P('phase', 'dp')
- ffn_out_bias_grad: float32 [2, 1024], P('phase', 'dp')
- norm_gain_grad: float32 [2, 2, 1024], P('phase', None, 'dp')
- norm_bias_grad: float32 [2, 2, 1024], P('phase', None, 'dp')
- cross_q_grad: float32 [1024, 1024], P(('phase', 'dp'))
- cross_q_bias_grad: float32 [1024], P(('phase', 'dp'))
- cross_kv_grad: float32 [1024, 2048], P(('phase', 'dp'))
- cross_v_bias_grad: float32 [1024], P(('phase', 'dp'))
- cross_out_grad: float32 [1024, 1024], P(('phase', 'dp'))
- cross_out_bias_grad: float32 [1024], P(('phase', 'dp'))
- cross_norm_gain_grad: float32 [1024], P(('phase', 'dp'))
- cross_norm_bias_grad: float32 [1024], P(('phase', 'dp'))
- query_qkv_grad: float32 [768, 2304], P(('phase', 'dp'))
- query_qv_bias_grad: float32 [1536], P(('phase', 'dp'))
- query_out_grad: float32 [768, 768], P(('phase', 'dp'))
- query_out_bias_grad: float32 [768], P(('phase', 'dp'))
- query_ffn_in_grad: float32 [768, 3072], P(('phase', 'dp'))
- query_ffn_in_bias_grad: float32 [3072], P(('phase', 'dp'))
- query_ffn_out_grad: float32 [3072, 768], P(('phase', 'dp'))
- query_ffn_out_bias_grad: float32 [768], P(('phase', 'dp'))
- query_norm_gain_grad: float32 [2, 768], P(None, ('phase', 'dp'))
- query_norm_bias_grad: float32 [2, 768], P(None, ('phase', 'dp'))
Inputs may be any that keep to these rules, and one draw needn't show every extreme that they name: `sequence_labels`: in each block of 256 rows the numbers never fall, each of the 4 sequences has 1 to 192 rows, and one has exactly 192. `inquiry_token_spans`: the 4 lengths of a block sum to 128; the longest is exactly 64. `document_slots`: indices into the 16 passages of the same micro-batch and block.
All inputs are finite; a program needn't handle non-finite values.
Results may differ from a plain program's by a relative error of at most 0.025.
Values may be sent and summed in bfloat16 or wider, within the bound.
No kernel may reach another device: no remote copies, remote signals or barrier semaphores. Data moves between devices by JAX's collectives and lax.ppermute only.
A program may use at most 384 MiB of HBM per device.

v0:
```python
from functools import partial

import jax
import jax.numpy as jnp
from jax import lax
from jax.sharding import PartitionSpec as P

HEADS = 16
QHEADS = 12


NEG_FILL = -1e30
EPS_MODEL = 1e-05
EPS_QUERY = 1e-12


def as_sent(shard):

    def short(part):
        return part.astype(jnp.bfloat16) if part.dtype == jnp.float32 else part

    return jax.tree.map(short, shard)


def from_behind(value, axis, steps):
    count = lax.axis_size(axis)
    initial, last = (max(0, -steps), min(count, count - steps))
    return lax.ppermute(value, axis, [(source, source + steps) for source in range(initial, last)])


def matmul_plain(left, right):
    return jnp.dot(left, right, preferred_element_type=jnp.float32)


def matmul_left_t(left, right):
    return lax.dot_general(
        left, right, (((0,), (0,)), ((), ())), preferred_element_type=jnp.float32
    )


def matmul_right_t(left, right):
    return lax.dot_general(
        left, right, (((1,), (1,)), ((), ())), preferred_element_type=jnp.float32
    )


def column_sum(matrix):
    return jnp.sum(matrix.astype(jnp.float32), axis=0)


def add_pairs(former, latter):
    return tuple((first_one + second_one for first_one, second_one in zip(former, latter)))


def norm_apply(stream, gain_row, bias_row, epsilon):
    centred = stream - jnp.mean(stream, axis=-1, keepdims=True)
    spread = jnp.mean(centred * centred, axis=-1, keepdims=True)
    return centred * lax.rsqrt(spread + epsilon) * gain_row + bias_row


def norm_forward(stream, gain_row, bias_row, epsilon):
    return jax.vjp(
        partial(norm_apply, epsilon=epsilon),
        stream,
        gain_row.astype(jnp.float32),
        bias_row.astype(jnp.float32),
    )


def gelu_exact(values):
    return jax.nn.gelu(values, approximate=False)


def head_split(matrix, head_count):
    return matrix.reshape(matrix.shape[0], head_count, matrix.shape[1] // head_count)


def attend_forward(queries, key_rows, value_rows, allowed, head_count):
    total_rows, features = queries.shape
    score_scale = (features // head_count) ** (-0.5)
    key_heads = head_split(key_rows, head_count)
    value_heads = head_split(value_rows, head_count)
    step_rows = min(total_rows, 512)
    mixed_parts = []
    total_parts = []
    for first_row in range(0, total_rows, step_rows):
        query_heads = head_split(queries[first_row : first_row + step_rows], head_count)
        scores = (
            jnp.einsum("qhd,khd->hqk", query_heads, key_heads, preferred_element_type=jnp.float32)
            * score_scale
        )
        scores = jnp.where(allowed[None, first_row : first_row + step_rows], scores, NEG_FILL)
        row_peak = jnp.max(scores, axis=-1, keepdims=True)
        raised = jnp.exp(scores - row_peak)
        row_total = jnp.sum(raised, axis=-1, keepdims=True)
        chances = (raised / row_total).astype(jnp.bfloat16)
        mixed_rows = jnp.einsum(
            "hqk,khd->qhd", chances, value_heads, preferred_element_type=jnp.float32
        )
        mixed_parts.append(mixed_rows.reshape(step_rows, features))
        total_parts.append(row_peak + jnp.log(row_total))
    return (jnp.concatenate(mixed_parts, axis=0), jnp.concatenate(total_parts, axis=1))


def attend_backward(queries, key_rows, value_rows, allowed, head_count, log_total, grad_mixed):
    total_rows, features = queries.shape
    score_scale = (features // head_count) ** (-0.5)
    key_heads = head_split(key_rows, head_count)
    value_heads = head_split(value_rows, head_count)
    step_rows = min(total_rows, 512)
    grad_keys = jnp.zeros(key_heads.shape, jnp.float32)
    grad_values = jnp.zeros(value_heads.shape, jnp.float32)
    query_parts = []
    for first_row in range(0, total_rows, step_rows):
        query_heads = head_split(queries[first_row : first_row + step_rows], head_count)
        grad_heads = head_split(grad_mixed[first_row : first_row + step_rows], head_count)
        scores = (
            jnp.einsum("qhd,khd->hqk", query_heads, key_heads, preferred_element_type=jnp.float32)
            * score_scale
        )
        scores = jnp.where(allowed[None, first_row : first_row + step_rows], scores, NEG_FILL)
        chances = jnp.exp(scores - log_total[:, first_row : first_row + step_rows])
        grad_values = grad_values + jnp.einsum(
            "hqk,qhd->khd",
            chances.astype(jnp.bfloat16),
            grad_heads,
            preferred_element_type=jnp.float32,
        )
        grad_chances = jnp.einsum(
            "qhd,khd->hqk", grad_heads, value_heads, preferred_element_type=jnp.float32
        )
        grad_scores = (
            chances * (grad_chances - jnp.sum(chances * grad_chances, axis=-1, keepdims=True))
        ).astype(jnp.bfloat16)
        grad_query_part = (
            jnp.einsum("hqk,khd->qhd", grad_scores, key_heads, preferred_element_type=jnp.float32)
            * score_scale
        )
        query_parts.append(grad_query_part.reshape(step_rows, features))
        grad_keys = (
            grad_keys
            + jnp.einsum(
                "hqk,qhd->khd", grad_scores, query_heads, preferred_element_type=jnp.float32
            )
            * score_scale
        )
    return (
        jnp.concatenate(query_parts, axis=0),
        grad_keys.reshape(key_rows.shape),
        grad_values.reshape(value_rows.shape),
    )


def attn_forward(query_bf, source_bf, coefficient_nest, allowed, head_count):
    query_weight, pair_weight, query_bias, value_bias, proj_weight, proj_bias = coefficient_nest
    features = query_weight.shape[1]
    queries = (matmul_plain(query_bf, query_weight) + query_bias.astype(jnp.float32)).astype(
        jnp.bfloat16
    )
    paired = matmul_plain(source_bf, pair_weight)
    key_rows = paired[:, :features].astype(jnp.bfloat16)
    value_rows = (paired[:, features:] + value_bias.astype(jnp.float32)).astype(jnp.bfloat16)
    attended, log_total = attend_forward(queries, key_rows, value_rows, allowed, head_count)
    attended = attended.astype(jnp.bfloat16)
    branch = matmul_plain(attended, proj_weight) + proj_bias.astype(jnp.float32)
    return (branch, (queries, key_rows, value_rows, attended, log_total))


def attn_backward(
    query_bf, source_bf, coefficient_nest, kept_state, allowed, head_count, grad_branch
):
    query_weight, pair_weight, query_bias, value_bias, proj_weight, proj_bias = coefficient_nest
    queries, key_rows, value_rows, attended, log_total = kept_state
    features = query_weight.shape[1]
    grad_bf = grad_branch.astype(jnp.bfloat16)
    grad_attended = matmul_right_t(grad_bf, proj_weight).astype(jnp.bfloat16)
    grad_queries, grad_keys, grad_values = attend_backward(
        queries, key_rows, value_rows, allowed, head_count, log_total, grad_attended
    )
    grad_queries = grad_queries.astype(jnp.bfloat16)
    grad_pair = jnp.concatenate([grad_keys, grad_values], axis=1).astype(jnp.bfloat16)
    grads = (
        matmul_left_t(query_bf, grad_queries),
        matmul_left_t(source_bf, grad_pair),
        column_sum(grad_queries),
        column_sum(grad_pair[:, features:]),
        matmul_left_t(attended, grad_bf),
        column_sum(grad_bf),
    )
    return (
        grads,
        matmul_right_t(grad_queries, query_weight),
        matmul_right_t(grad_pair, pair_weight),
    )


def feed_forward(stream_bf, coefficient_nest):
    up_weight, up_bias, down_weight, down_bias = coefficient_nest
    hidden = matmul_plain(stream_bf, up_weight) + up_bias.astype(jnp.float32)
    active, gelu_back = jax.vjp(gelu_exact, hidden)
    active_bf = active.astype(jnp.bfloat16)
    branch = matmul_plain(active_bf, down_weight) + down_bias.astype(jnp.float32)
    return (branch, (active_bf, gelu_back))


def feed_backward(stream_bf, coefficient_nest, kept_state, grad_branch):
    up_weight, up_bias, down_weight, down_bias = coefficient_nest
    active_bf, gelu_back = kept_state
    grad_bf = grad_branch.astype(jnp.bfloat16)
    grad_active = matmul_right_t(grad_bf, down_weight)
    grad_hidden = gelu_back(grad_active)[0].astype(jnp.bfloat16)
    grads = (
        matmul_left_t(stream_bf, grad_hidden),
        column_sum(grad_hidden),
        matmul_left_t(active_bf, grad_bf),
        column_sum(grad_bf),
    )
    return (grads, matmul_right_t(grad_hidden, up_weight))


def split_layer(coefficient_nest):
    (
        joined_proj,
        joined_bias,
        proj_weight,
        proj_bias,
        feed_up,
        feed_up_bias,
        feed_down,
        feed_down_bias,
        gain_rows,
        bias_rows,
    ) = coefficient_nest
    features = joined_proj.shape[0]
    attn_set = (
        joined_proj[:, :features],
        joined_proj[:, features:],
        joined_bias[:features],
        joined_bias[features:],
        proj_weight,
        proj_bias,
    )
    return (attn_set, (feed_up, feed_up_bias, feed_down, feed_down_bias), gain_rows, bias_rows)


def join_layer(attn_grads, feed_grads, gain_pair, bias_pair):
    grad_query, grad_pair, grad_query_bias, grad_value_bias, grad_proj, grad_proj_bias = attn_grads
    return (
        (
            jnp.concatenate([grad_query, grad_pair], axis=1),
            jnp.concatenate([grad_query_bias, grad_value_bias]),
            grad_proj,
            grad_proj_bias,
        )
        + tuple(feed_grads)
        + (jnp.stack(gain_pair), jnp.stack(bias_pair))
    )


def encoder_pass(stream_bf, layer_set, allowed, grad_result):
    attn_set, feed_set, gain_rows, bias_rows = split_layer(layer_set)
    stream = stream_bf.astype(jnp.float32)
    attn_branch, attn_kept = attn_forward(stream_bf, stream_bf, attn_set, allowed, HEADS)
    middle, norm_one = norm_forward(stream + attn_branch, gain_rows[0], bias_rows[0], EPS_MODEL)
    middle_bf = middle.astype(jnp.bfloat16)
    feed_branch, feed_kept = feed_forward(middle_bf, feed_set)
    result, norm_two = norm_forward(middle + feed_branch, gain_rows[1], bias_rows[1], EPS_MODEL)
    if grad_result is None:
        return result
    grad_two, gain_two, bias_two = norm_two(grad_result)
    feed_grads, grad_feed_in = feed_backward(middle_bf, feed_set, feed_kept, grad_two)
    grad_one, gain_one, bias_one = norm_one(grad_two + grad_feed_in)
    attn_grads, grad_query_in, grad_source_in = attn_backward(
        stream_bf, stream_bf, attn_set, attn_kept, allowed, HEADS, grad_one
    )
    grad_stream = grad_one + grad_query_in + grad_source_in
    return (
        result,
        grad_stream,
        join_layer(attn_grads, feed_grads, (gain_one, gain_two), (bias_one, bias_two)),
    )


def decoder_pass(
    target_bf, memory_bf, layer_set, cross_set, self_allowed, cross_allowed, grad_result
):
    attn_set, feed_set, gain_rows, bias_rows = split_layer(layer_set)
    cross_attn = (
        cross_set[0],
        cross_set[2],
        cross_set[1],
        cross_set[3],
        cross_set[4],
        cross_set[5],
    )
    stream = target_bf.astype(jnp.float32)
    self_branch, self_kept = attn_forward(target_bf, target_bf, attn_set, self_allowed, HEADS)
    first_out, norm_one = norm_forward(stream + self_branch, gain_rows[0], bias_rows[0], EPS_MODEL)
    first_bf = first_out.astype(jnp.bfloat16)
    cross_branch, cross_kept = attn_forward(first_bf, memory_bf, cross_attn, cross_allowed, HEADS)
    second, norm_cross = norm_forward(
        first_out + cross_branch, cross_set[6], cross_set[7], EPS_MODEL
    )
    second_bf = second.astype(jnp.bfloat16)
    feed_branch, feed_kept = feed_forward(second_bf, feed_set)
    result, norm_two = norm_forward(second + feed_branch, gain_rows[1], bias_rows[1], EPS_MODEL)
    grad_two, gain_two, bias_two = norm_two(grad_result)
    feed_grads, grad_feed_in = feed_backward(second_bf, feed_set, feed_kept, grad_two)
    grad_cross_sum, gain_cross, bias_cross = norm_cross(grad_two + grad_feed_in)
    cross_grads, grad_first_in, grad_memory = attn_backward(
        first_bf, memory_bf, cross_attn, cross_kept, cross_allowed, HEADS, grad_cross_sum
    )
    grad_one, gain_one, bias_one = norm_one(grad_cross_sum + grad_first_in)
    self_grads, grad_query_in, grad_source_in = attn_backward(
        target_bf, target_bf, attn_set, self_kept, self_allowed, HEADS, grad_one
    )
    grad_stream = grad_one + grad_query_in + grad_source_in
    layer_grads = join_layer(self_grads, feed_grads, (gain_one, gain_two), (bias_one, bias_two))
    side_grads = (
        cross_grads[0],
        cross_grads[2],
        cross_grads[1],
        cross_grads[3],
        cross_grads[4],
        cross_grads[5],
        gain_cross,
        bias_cross,
    )
    return (result, grad_stream, grad_memory, layer_grads, side_grads)


def query_pass(question_bf, lengths, passage_rows, slot_rows, heat_row, layer_set, grad_scores):
    attn_set, feed_set, gain_rows, bias_rows = split_layer(layer_set)
    run_ends = jnp.cumsum(lengths)
    firsts = run_ends - lengths
    positions = jnp.arange(question_bf.shape[0], dtype=jnp.int32)
    allowed = (positions[None, :] >= firsts[:, None]) & (positions[None, :] < run_ends[:, None])
    head_bf = question_bf[firsts]
    attn_branch, attn_kept = attn_forward(head_bf, question_bf, attn_set, allowed, QHEADS)
    middle, norm_one = norm_forward(
        head_bf.astype(jnp.float32) + attn_branch, gain_rows[0], bias_rows[0], EPS_QUERY
    )
    middle_bf = middle.astype(jnp.bfloat16)
    feed_branch, feed_kept = feed_forward(middle_bf, feed_set)
    vectors, norm_two = norm_forward(middle + feed_branch, gain_rows[1], bias_rows[1], EPS_QUERY)
    chosen = passage_rows[slot_rows]
    raw_scores = jnp.sum(vectors[:, None, :] * chosen, axis=-1)
    scores = raw_scores / heat_row[0]
    heat_grad = (-jnp.sum(grad_scores * raw_scores) / (heat_row[0] * heat_row[0])).reshape(1)
    grad_vectors = jnp.sum((grad_scores / heat_row[0])[:, :, None] * chosen, axis=1)
    grad_two, gain_two, bias_two = norm_two(grad_vectors)
    feed_grads, grad_feed_in = feed_backward(middle_bf, feed_set, feed_kept, grad_two)
    grad_one, gain_one, bias_one = norm_one(grad_two + grad_feed_in)
    attn_grads, grad_head_in, grad_source_in = attn_backward(
        head_bf, question_bf, attn_set, attn_kept, allowed, QHEADS, grad_one
    )
    grad_stream = grad_source_in.at[firsts].add(grad_one + grad_head_in)
    return (
        scores,
        grad_stream,
        join_layer(attn_grads, feed_grads, (gain_one, gain_two), (bias_one, bias_two)),
        heat_grad,
    )


def add_block(running, position, rows_new):
    current = lax.dynamic_index_in_dim(running, position, 0, keepdims=False)
    return lax.dynamic_update_index_in_dim(running, current + rows_new, position, 0)


def reduce_layer_end(values):
    (
        joined_proj,
        joined_bias,
        proj_weight,
        proj_bias,
        feed_up,
        feed_up_bias,
        feed_down,
        feed_down_bias,
        gain_rows,
        bias_rows,
    ) = values
    return (
        lax.psum_scatter(joined_proj[None], "dp", scatter_dimension=1, tiled=True),
        lax.psum_scatter(joined_bias[None], "dp", scatter_dimension=1, tiled=True),
        lax.psum_scatter(proj_weight[None], "dp", scatter_dimension=1, tiled=True),
        lax.psum_scatter(proj_bias[None], "dp", scatter_dimension=1, tiled=True),
        lax.psum_scatter(feed_up[None], "dp", scatter_dimension=1, tiled=True),
        lax.psum_scatter(feed_up_bias[None], "dp", scatter_dimension=1, tiled=True),
        lax.psum_scatter(feed_down[None], "dp", scatter_dimension=1, tiled=True),
        lax.psum_scatter(feed_down_bias[None], "dp", scatter_dimension=1, tiled=True),
        lax.psum_scatter(gain_rows[None], "dp", scatter_dimension=2, tiled=True),
        lax.psum_scatter(bias_rows[None], "dp", scatter_dimension=2, tiled=True),
    )


def reduce_side_end(values):
    (
        cross_query,
        cross_query_bias,
        cross_pair,
        cross_value_bias,
        cross_proj,
        cross_proj_bias,
        cross_gain,
        cross_bias,
        query_joined,
        query_joined_bias,
        query_proj,
        query_proj_bias,
        query_up,
        query_up_bias,
        query_down,
        query_down_bias,
        query_gain,
        query_bias,
    ) = values
    return (
        lax.psum_scatter(cross_query, ("phase", "dp"), scatter_dimension=0, tiled=True),
        lax.psum_scatter(cross_query_bias, ("phase", "dp"), scatter_dimension=0, tiled=True),
        lax.psum_scatter(cross_pair, ("phase", "dp"), scatter_dimension=0, tiled=True),
        lax.psum_scatter(cross_value_bias, ("phase", "dp"), scatter_dimension=0, tiled=True),
        lax.psum_scatter(cross_proj, ("phase", "dp"), scatter_dimension=0, tiled=True),
        lax.psum_scatter(cross_proj_bias, ("phase", "dp"), scatter_dimension=0, tiled=True),
        lax.psum_scatter(cross_gain, ("phase", "dp"), scatter_dimension=0, tiled=True),
        lax.psum_scatter(cross_bias, ("phase", "dp"), scatter_dimension=0, tiled=True),
        lax.psum_scatter(query_joined, ("phase", "dp"), scatter_dimension=0, tiled=True),
        lax.psum_scatter(query_joined_bias, ("phase", "dp"), scatter_dimension=0, tiled=True),
        lax.psum_scatter(query_proj, ("phase", "dp"), scatter_dimension=0, tiled=True),
        lax.psum_scatter(query_proj_bias, ("phase", "dp"), scatter_dimension=0, tiled=True),
        lax.psum_scatter(query_up, ("phase", "dp"), scatter_dimension=0, tiled=True),
        lax.psum_scatter(query_up_bias, ("phase", "dp"), scatter_dimension=0, tiled=True),
        lax.psum_scatter(query_down, ("phase", "dp"), scatter_dimension=0, tiled=True),
        lax.psum_scatter(query_down_bias, ("phase", "dp"), scatter_dimension=0, tiled=True),
        lax.psum_scatter(query_gain, ("phase", "dp"), scatter_dimension=1, tiled=True),
        lax.psum_scatter(query_bias, ("phase", "dp"), scatter_dimension=1, tiled=True),
    )


def local(
    token_vectors,
    generation_result_adjoint,
    sequence_labels,
    inquiry_vectors,
    inquiry_token_spans,
    document_vectors,
    document_slots,
    relevance_adjoint,
    softness_scalar,
    intrinsic_triple_map,
    intrinsic_probe_content_offset,
    intrinsic_mixing_result_map,
    intrinsic_mixing_result_offset,
    perceptron_widen_map,
    perceptron_widen_offset,
    perceptron_narrow_map,
    perceptron_narrow_offset,
    standardize_scales,
    standardize_shifts,
    encoded_mixing_probe_map,
    encoded_mixing_probe_offset,
    encoded_lookup_content_map,
    encoded_mixing_content_offset,
    encoded_mixing_result_map,
    encoded_mixing_result_offset,
    encoded_mixing_scale_factor,
    encoded_mixing_scale_shift,
    retriever_triple_map,
    retriever_probe_content_offset,
    retriever_mixing_result_map,
    retriever_mixing_result_offset,
    retriever_widen_map,
    retriever_widen_offset,
    retriever_narrow_map,
    retriever_narrow_offset,
    retriever_standardize_scales,
    retriever_standardize_shifts,
):
    micro_count = token_vectors.shape[1]
    block_rows = token_vectors.shape[2]
    features = token_vectors.shape[3]
    phase_first = lax.axis_index("phase") == 0
    stacked = (
        lax.all_gather(intrinsic_triple_map, "dp", axis=1, tiled=True),
        lax.all_gather(intrinsic_probe_content_offset, "dp", axis=1, tiled=True),
        lax.all_gather(intrinsic_mixing_result_map, "dp", axis=1, tiled=True),
        lax.all_gather(intrinsic_mixing_result_offset, "dp", axis=1, tiled=True),
        lax.all_gather(perceptron_widen_map, "dp", axis=1, tiled=True),
        lax.all_gather(perceptron_widen_offset, "dp", axis=1, tiled=True),
        lax.all_gather(perceptron_narrow_map, "dp", axis=1, tiled=True),
        lax.all_gather(perceptron_narrow_offset, "dp", axis=1, tiled=True),
        lax.all_gather(standardize_scales, "dp", axis=2, tiled=True),
        lax.all_gather(standardize_shifts, "dp", axis=2, tiled=True),
    )
    layer_set = tuple((component_item[0] for component_item in stacked))
    side_set = (
        lax.all_gather(encoded_mixing_probe_map, ("phase", "dp"), axis=0, tiled=True),
        lax.all_gather(encoded_mixing_probe_offset, ("phase", "dp"), axis=0, tiled=True),
        lax.all_gather(encoded_lookup_content_map, ("phase", "dp"), axis=0, tiled=True),
        lax.all_gather(encoded_mixing_content_offset, ("phase", "dp"), axis=0, tiled=True),
        lax.all_gather(encoded_mixing_result_map, ("phase", "dp"), axis=0, tiled=True),
        lax.all_gather(encoded_mixing_result_offset, ("phase", "dp"), axis=0, tiled=True),
        lax.all_gather(encoded_mixing_scale_factor, ("phase", "dp"), axis=0, tiled=True),
        lax.all_gather(encoded_mixing_scale_shift, ("phase", "dp"), axis=0, tiled=True),
        lax.all_gather(retriever_triple_map, ("phase", "dp"), axis=0, tiled=True),
        lax.all_gather(retriever_probe_content_offset, ("phase", "dp"), axis=0, tiled=True),
        lax.all_gather(retriever_mixing_result_map, ("phase", "dp"), axis=0, tiled=True),
        lax.all_gather(retriever_mixing_result_offset, ("phase", "dp"), axis=0, tiled=True),
        lax.all_gather(retriever_widen_map, ("phase", "dp"), axis=0, tiled=True),
        lax.all_gather(retriever_widen_offset, ("phase", "dp"), axis=0, tiled=True),
        lax.all_gather(retriever_narrow_map, ("phase", "dp"), axis=0, tiled=True),
        lax.all_gather(retriever_narrow_offset, ("phase", "dp"), axis=0, tiled=True),
        lax.all_gather(retriever_standardize_scales, ("phase", "dp"), axis=1, tiled=True),
        lax.all_gather(retriever_standardize_shifts, ("phase", "dp"), axis=1, tiled=True),
    )
    layer_local = (
        intrinsic_triple_map,
        intrinsic_probe_content_offset,
        intrinsic_mixing_result_map,
        intrinsic_mixing_result_offset,
        perceptron_widen_map,
        perceptron_widen_offset,
        perceptron_narrow_map,
        perceptron_narrow_offset,
        standardize_scales,
        standardize_shifts,
    )
    side_local = (
        encoded_mixing_probe_map,
        encoded_mixing_probe_offset,
        encoded_lookup_content_map,
        encoded_mixing_content_offset,
        encoded_mixing_result_map,
        encoded_mixing_result_offset,
        encoded_mixing_scale_factor,
        encoded_mixing_scale_shift,
        retriever_triple_map,
        retriever_probe_content_offset,
        retriever_mixing_result_map,
        retriever_mixing_result_offset,
        retriever_widen_map,
        retriever_widen_offset,
        retriever_narrow_map,
        retriever_narrow_offset,
        retriever_standardize_scales,
        retriever_standardize_shifts,
    )
    layer_zero = tuple(
        (jnp.zeros(component_item.shape, jnp.float32) for component_item in layer_set)
    )
    side_zero = tuple((jnp.zeros(component_item.shape, jnp.float32) for component_item in side_set))
    positions = jnp.arange(block_rows, dtype=jnp.int32)

    def masks_for(micro_index):
        segments = sequence_labels[micro_index, 0]
        same_segment = segments[:, None] == segments[None, :]
        return (same_segment, same_segment & (positions[:, None] >= positions[None, :]))

    plan = []
    for micro_index in range(micro_count):
        plan = plan + [
            (micro_index, None, None),
            (None, None, micro_index),
            (None, micro_index, None),
        ]
    forward_inbox = {}
    back_inbox = {}
    score_parts = {}
    question_parts = {}

    def blank_outcome(layer_acc, side_acc):
        blank_send = jnp.zeros((block_rows, features), jnp.bfloat16)
        blank_rows = jnp.zeros((block_rows, features), jnp.float32)
        return [
            blank_send,
            blank_send,
            jnp.zeros(relevance_adjoint.shape[1:], jnp.float32),
            jnp.zeros(inquiry_vectors.shape[1:], jnp.float32),
            blank_rows,
            blank_rows,
            layer_acc,
            side_acc,
            jnp.zeros((1,), jnp.float32),
        ]

    def encoder_work(forward_index, back_index, layer_acc, side_acc):

        def run_zero():
            outcome = blank_outcome(layer_acc, side_acc)
            if forward_index is not None:
                same_segment, causal = masks_for(forward_index)
                memory = encoder_pass(
                    token_vectors[0, forward_index], layer_set, same_segment, None
                )
                outcome[0] = memory.astype(jnp.bfloat16)
                outcome[4] = memory
                score_rows, question_rows, query_grads, heat_grad = query_pass(
                    inquiry_vectors[forward_index],
                    inquiry_token_spans[forward_index, 0],
                    document_vectors[forward_index],
                    document_slots[forward_index],
                    softness_scalar,
                    side_set[8:],
                    relevance_adjoint[forward_index],
                )
                outcome[2] = score_rows
                outcome[3] = question_rows
                outcome[7] = side_acc[:8] + add_pairs(side_acc[8:], query_grads)
                outcome[8] = heat_grad
            if back_index is not None:
                same_segment, causal = masks_for(back_index)
                recomputed, grad_rows, layer_grads = encoder_pass(
                    token_vectors[0, back_index],
                    layer_set,
                    same_segment,
                    back_inbox[back_index].astype(jnp.float32),
                )
                outcome[5] = grad_rows
                outcome[6] = add_pairs(layer_acc, layer_grads)
            return tuple(outcome)

        return run_zero

    def decoder_work(dec_index, layer_acc, side_acc):

        def run_one():
            outcome = blank_outcome(layer_acc, side_acc)
            if dec_index is not None:
                same_segment, causal = masks_for(dec_index)
                result, grad_rows, grad_memory, layer_grads, cross_grads = decoder_pass(
                    token_vectors[0, dec_index],
                    forward_inbox[dec_index],
                    layer_set,
                    side_set[:8],
                    causal,
                    same_segment,
                    generation_result_adjoint[dec_index].astype(jnp.float32),
                )
                outcome[1] = grad_memory.astype(jnp.bfloat16)
                outcome[4] = result
                outcome[5] = grad_rows
                outcome[6] = add_pairs(layer_acc, layer_grads)
                outcome[7] = add_pairs(side_acc[:8], cross_grads) + side_acc[8:]
            return tuple(outcome)

        return run_one

    layer_acc = layer_zero
    side_acc = side_zero
    layer_shards = tuple(
        (jnp.zeros(component_item.shape, jnp.float32) for component_item in layer_local)
    )
    side_shards = tuple(
        (jnp.zeros(component_item.shape, jnp.float32) for component_item in side_local)
    )
    heat_acc = jnp.zeros((1,), jnp.float32)
    out_total = jnp.zeros((micro_count, block_rows, features), jnp.float32)
    grad_total = jnp.zeros((micro_count, block_rows, features), jnp.float32)
    for forward_index, back_index, dec_index in plan:
        start_layer, start_side = (layer_acc, side_acc)
        outcome = lax.cond(
            phase_first,
            encoder_work(forward_index, back_index, start_layer, start_side),
            decoder_work(dec_index, start_layer, start_side),
        )
        (
            memory_send,
            back_send,
            score_rows,
            question_rows,
            out_rows,
            grad_rows,
            layer_new,
            side_new,
            heat_grad,
        ) = outcome
        heat_acc = heat_acc + heat_grad
        if forward_index is not None:
            forward_inbox[forward_index] = jax.tree.map(
                lambda part, own: part.astype(own.dtype),
                from_behind(as_sent(memory_send), "phase", 1),
                memory_send,
            )
            copied = (
                from_behind(as_sent(score_rows), "phase", 1).astype(score_rows.dtype),
                from_behind(as_sent(question_rows), "phase", 1).astype(question_rows.dtype),
            )
            score_parts[forward_index] = score_rows + copied[0]
            question_parts[forward_index] = question_rows + copied[1]
        if dec_index is not None:
            back_inbox[dec_index] = jax.tree.map(
                lambda part, own: part.astype(own.dtype),
                from_behind(as_sent(back_send), "phase", -1),
                back_send,
            )
        dec_slot = dec_index if dec_index is not None else 0
        out_at = jnp.where(phase_first, forward_index if forward_index is not None else 0, dec_slot)
        grad_at = jnp.where(phase_first, back_index if back_index is not None else 0, dec_slot)
        out_total = add_block(out_total, out_at, out_rows)
        grad_total = add_block(grad_total, grad_at, grad_rows)
        layer_acc, side_acc = (layer_new, side_new)
    layer_shards = reduce_layer_end(layer_acc)
    side_shards = reduce_side_end(side_acc)
    heat_total = lax.psum(heat_acc, ("phase", "dp"))
    layer_out = out_total.astype(jnp.bfloat16)[None]
    input_grad = grad_total[None]
    scores_own = jnp.where(phase_first, score_parts[0], score_parts[1])[None]
    question_own = jnp.where(phase_first, question_parts[0], question_parts[1])[None]
    return (
        (layer_out, input_grad, scores_own, question_own, heat_total)
        + tuple(layer_shards)
        + tuple(side_shards)
    )


def solution(mesh):
    in_specs = (
        P("phase", None, "dp", None),
        P(None, "dp", None),
        P(None, "dp", None),
        P(None, "dp", None),
        P(None, "dp", None),
        P(None, "dp", None),
        P(None, "dp", None),
        P(None, "dp", None),
        P(),
        P("phase", "dp", None),
        P("phase", "dp"),
        P("phase", "dp", None),
        P("phase", "dp"),
        P("phase", "dp", None),
        P("phase", "dp"),
        P("phase", "dp", None),
        P("phase", "dp"),
        P("phase", None, "dp"),
        P("phase", None, "dp"),
        P(("phase", "dp"), None),
        P(("phase", "dp")),
        P(("phase", "dp"), None),
        P(("phase", "dp")),
        P(("phase", "dp"), None),
        P(("phase", "dp")),
        P(("phase", "dp")),
        P(("phase", "dp")),
        P(("phase", "dp"), None),
        P(("phase", "dp")),
        P(("phase", "dp"), None),
        P(("phase", "dp")),
        P(("phase", "dp"), None),
        P(("phase", "dp")),
        P(("phase", "dp"), None),
        P(("phase", "dp")),
        P(None, ("phase", "dp")),
        P(None, ("phase", "dp")),
    )
    out_specs = (
        P("phase", None, "dp", None),
        P("phase", None, "dp", None),
        P("phase", "dp", None),
        P("phase", "dp", None),
        P(),
        P("phase", "dp", None),
        P("phase", "dp"),
        P("phase", "dp", None),
        P("phase", "dp"),
        P("phase", "dp", None),
        P("phase", "dp"),
        P("phase", "dp", None),
        P("phase", "dp"),
        P("phase", None, "dp"),
        P("phase", None, "dp"),
        P(("phase", "dp"), None),
        P(("phase", "dp")),
        P(("phase", "dp"), None),
        P(("phase", "dp")),
        P(("phase", "dp"), None),
        P(("phase", "dp")),
        P(("phase", "dp")),
        P(("phase", "dp")),
        P(("phase", "dp"), None),
        P(("phase", "dp")),
        P(("phase", "dp"), None),
        P(("phase", "dp")),
        P(("phase", "dp"), None),
        P(("phase", "dp")),
        P(("phase", "dp"), None),
        P(("phase", "dp")),
        P(None, ("phase", "dp")),
        P(None, ("phase", "dp")),
    )
    return jax.shard_map(local, mesh=mesh, in_specs=in_specs, out_specs=out_specs, check_vma=False)
```

profile of v0, /device:TPU:1, one launch (start us, length us, event | category | flops | bytes accessed | tf_op | source)
XLA Modules:
  0.0 3811.3 jit_solution(8098920413585143406)
XLA Ops:
  16.2 34.5 all_gather.85
  50.7 28.9 all_gather.91
  79.7 79.5 %all-gather = bf16[32,24,2]{1,2,0:T(2,128)(2,1)S(1)} all-gather(bf16[1,24,2]{1,2,0:T(2,128)(2,1)} %bitcast.921), channel_id=1, replica_groups=mesh['phase'=2,'dp'=16] {'phase','dp'}, dimensions={0}, use_global_device_ids=true | all-gather | bytes 3168 | tf_op jit(solution)/shard_map/all_gather | solution.py:514
  159.3 63.2 %all-gather.1 = bf16[32,24,2]{1,2,0:T(2,128)(2,1)S(1)} all-gather(bf16[1,24,2]{1,2,0:T(2,128)(2,1)} %bitcast.922), channel_id=1, replica_groups=mesh['phase'=2,'dp'=16] {'phase','dp'}, dimensions={0}, use_global_device_ids=true | all-gather | bytes 3168 | tf_op jit(solution)/shard_map/all_gather | solution.py:515
  224.2 36.2 all_gather.89
  260.7 33.3 all_gather.88
  297.6 52.1 %all-reduce.25 = (bf16[1536]{0:T(1024)(128)(2,1)S(1)}, bf16[768]{0:T(1024)(128)(2,1)S(1)}, bf16[3072]{0:T(1024)(128)(2,1)S(1)}, bf16[768]{0:T(1024)(128)(2,1)S(1...) all-reduce(bf16[1536]{0:T(1024)(128)(2,1)S(1)} %dynamic-update-slic, ...), channel_id=1, replica_groups=mesh['phase'=2,'dp'=16] {'phase','dp'}, use_global_device_ids=true, to_apply=%add.4 | all-reduce | flops 11264 | bytes 45056
  349.8 33.4 all-reduce.26
  383.3 38.9 %all-gather.14.cloned.1.call-done = bf16[1,1024,3072]{2,1,0:T(8,128)(2,1)} async-done(((bf16[1,64,3072]{2,1,0:T(8,128)(2,1)}), bf16[1,1024,3072]{2,1,0:T(8,128)(2,1)}) %all-gather.14.cloned.1.call-update) | async-done | bytes 6291472 | tf_op jit(solution)/shard_map/all_gather | solution.py:485
  422.2 114.4 %all-gather.18.cloned.1.call-done = bf16[1,1024,4096]{2,1,0:T(8,128)(2,1)} async-done(((bf16[1,64,4096]{2,1,0:T(8,128)(2,1)}), bf16[1,1024,4096]{2,1,0:T(8,128)(2,1)}) %all-gather.18.cloned.1.call-update) | async-done | bytes 8388624 | tf_op jit(solution)/shard_map/all_gather | solution.py:489
  536.6 113.8 %all-gather.20.cloned.1.call-done = bf16[1,4096,1024]{2,1,0:T(8,128)(2,1)} async-done(((bf16[1,256,1024]{2,1,0:T(8,128)(2,1)}), bf16[1,4096,1024]{2,1,0:T(8,128)(2,1)}) %all-gather.20.cloned.1.call-update) | async-done | bytes 8388624 | tf_op jit(solution)/shard_map/all_gather | solution.py:491
  650.5 30.2 conditional.6
  662.6 4.3 broadcast_in_dim.379
  666.8 4.8 broadcast_in_dim.377
  682.1 27.1 all-gather.30.cloned.1.call-done
  709.2 58.1 %all-gather.34.cloned.1.call-done = bf16[1024,1024]{1,0:T(8,128)(2,1)} async-done(((bf16[32,1024]{1,0:T(8,128)(2,1)}), bf16[1024,1024]{1,0:T(8,128)(2,1)}) %all-gather.34.cloned.1.call-update) | async-done | bytes 2097168 | tf_op jit(solution)/shard_map/all_gather | solution.py:502
  767.3 64.2 %all-gather.32.cloned.1.call-done = bf16[1024,2048]{1,0:T(8,128)(2,1)} async-done(((bf16[32,2048]{1,0:T(8,128)(2,1)}), bf16[1024,2048]{1,0:T(8,128)(2,1)}) %all-gather.32.cloned.1.call-update) | async-done | bytes 4194320 | tf_op jit(solution)/shard_map/all_gather | solution.py:500
  831.4 182.2 %conditional.7 = (bf16[256,1024]{1,0:T(8,128)(2,1)}, f32[256,1024]{1,0:T(8,128)}, f32[256,1024]{1,0:T(8,128)S(1)}, f32[1024,3072]{0,1:T(8,128)}, f32[2048]{0:T(1...) conditional(s32[]{:T(128)} %convert_element_type.993, ...), branch_computations={%region_33.66_spmd, %region_66.67_spmd} | conditional | flops 27552575488 | bytes 648526848 | solution.py:662
  877.6 13.6 multiply_convert_fusion.2
  897.4 12.0 convert_reduce_fusion
  909.5 7.5 multiply_reduce_fusion.2
  949.6 4.5 fusion.82
  973.6 4.6 convolution_bitcast_fusion
  978.2 4.6 convolution_bitcast_fusion.1
  982.9 11.9 pad_maximum_fusion
  994.7 10.4 fusion.79
  1005.1 8.2 fusion.657
  1015.7 11.0 conditional.8
  1028.1 14.6 conditional.9
  1042.9 175.9 %conditional.10 = (bf16[256,1024]{1,0:T(8,128)(2,1)}, f32[256,1024]{1,0:T(8,128)}, f32[256,1024]{1,0:T(8,128)S(1)}, f32[1024,3072]{0,1:T(8,128)}, f32[2048]{0:T(...) conditional(s32[]{:T(128)} %convert_element_type.993, ...), branch_computations={%region_122.155_spmd, %region_155.156_spmd} | conditional | flops 27569364992 | bytes 648722880 | solution.py:662
  1050.8 3.8 fusion.659
  1079.2 16.5 multiply_convert_fusion.7
  1100.7 11.9 convert_reduce_fusion.15
  1112.6 14.1 convolution_add_fusion.14
  1126.7 6.1 multiply_reduce_fusion.16
  1132.9 14.3 convolution_add_fusion.15
  1149.4 4.9 convolution_add_fusion.17
  1166.7 8.3 bitcast_add_fusion
  1178.7 5.1 convolution_add_fusion.18
  1187.0 5.0 convolution_add_fusion.19
  1200.1 3.7 fusion.153
  1208.5 10.1 maximum_add_fusion.4
  1222.1 10.7 conditional.11
  1244.0 8.0 copy.417
  1255.5 9.2 copy.416
  1264.8 12.6 copy.415
  1284.3 107.2 %collective-permute-done.4 = bf16[4,5]{1,0:T(4,128)(2,1)S(1)} collective-permute-done((bf16[4,5]{1,0:T(4,128)(2,1)S(1)}, bf16[4,5]{1,0:T(4,128)(2,1)S(1)}, u32[]{:S(2)}, u32[]{:S(2)}) %collective-permute-start.4) | collective-permute-done | bytes 72 | tf_op jit(solution)/shard_map/ppermute | solution.py:28
  1408.6 40.0 %all-reduce.24 = (f32[1]{0:T(128)}, f32[1024]{0:T(1024)S(1)}, f32[1024]{0:T(1024)S(1)}, f32[1024]{0:T(1024)S(1)}, f32[1024]{0:T(1024)S(1)}, /*index=5*/f32[1024]...) all-reduce(f32[1]{0:T(128)S(6)} %add.1357, ...), channel_id=1, replica_groups=mesh['phase'=2,'dp'=16] {'phase','dp'}, use_global_device_ids=true, to_apply=%region_178.179 | all-reduce | flops 14337 | bytes 114696 | tf_op jit(solution)/shard_map/psum | solution.py:705
  1469.0 14.4 reduce-scatter.60.cloned.1.call-done
  1484.7 73.6 %reduce-scatter.62.cloned.1.call-done = f32[64,2]{1,0:T(8,128)} async-done(((f32[1024,2]{1,0:T(8,128)}), f32[64,2]{1,0:T(8,128)}) %reduce-scatter.62.cloned.1.call-update) | async-done | bytes 528
  1559.8 74.3 %reduce-scatter.64.cloned.1.call-done = f32[64,2]{1,0:T(8,128)} async-done(((f32[1024,2]{1,0:T(8,128)}), f32[64,2]{1,0:T(8,128)}) %reduce-scatter.64.cloned.1.call-update) | async-done | bytes 528
  1635.5 74.7 %reduce-scatter.54.cloned.1.call-done = f32[128,1]{1,0:T(8,128)} async-done(((f32[2048,1]{1,0:T(8,128)}), f32[128,1]{1,0:T(8,128)}) %reduce-scatter.54.cloned.1.call-update) | async-done | bytes 528
  1711.6 78.1 %reduce-scatter.58.cloned.1.call-done = f32[256,1]{1,0:T(8,128)} async-done(((f32[4096,1]{1,0:T(8,128)}), f32[256,1]{1,0:T(8,128)}) %reduce-scatter.58.cloned.1.call-update) | async-done | bytes 1040
  1791.2 110.6 %reduce-scatter.48.cloned.1.call-done = f32[24,768]{1,0:T(8,128)} async-done(((f32[768,768]{1,0:T(8,128)}), f32[24,768]{1,0:T(8,128)}) %reduce-scatter.48.cloned.1.call-update) | async-done | bytes 73744 | tf_op jit(solution)/shard_map/reduce_scatter | solution.py:430
  1901.8 124.4 %reduce-scatter.46.cloned.1.call-done = f32[24,2304]{1,0:T(8,128)} async-done(((f32[768,2304]{1,0:T(8,128)}), f32[24,2304]{1,0:T(8,128)}) %reduce-scatter.46.cloned.1.call-update) | async-done | bytes 221200 | tf_op jit(solution)/shard_map/reduce_scatter | solution.py:428
  2026.2 150.5 %reduce-scatter.40.cloned.1.call-done = f32[32,1024]{1,0:T(8,128)} async-done(((f32[1024,1024]{1,0:T(8,128)}), f32[32,1024]{1,0:T(8,128)}) %reduce-scatter.40.cloned.1.call-update) | async-done | bytes 131088 | tf_op jit(solution)/shard_map/reduce_scatter | solution.py:420
  2176.6 146.4 %reduce-scatter.44.cloned.1.call-done = f32[32,1024]{1,0:T(8,128)} async-done(((f32[1024,1024]{1,0:T(8,128)}), f32[32,1024]{1,0:T(8,128)}) %reduce-scatter.44.cloned.1.call-update) | async-done | bytes 131088 | tf_op jit(solution)/shard_map/reduce_scatter | solution.py:424
  2323.0 95.2 %reduce-scatter.34.cloned.1.call-done = f32[1,64,1024]{2,1,0:T(8,128)} async-done(((f32[1,1024,1024]{2,1,0:T(8,128)}), f32[1,64,1024]{2,1,0:T(8,128)}) %reduce-scatter.34.cloned.1.call-update) | async-done | bytes 262160 | tf_op jit(solution)/shard_map/reduce_scatter | solution.py:387
  2418.2 141.6 %reduce-scatter.50.cloned.1.call-done = f32[24,3072]{1,0:T(8,128)} async-done(((f32[768,3072]{1,0:T(8,128)}), f32[24,3072]{1,0:T(8,128)}) %reduce-scatter.50.cloned.1.call-update) | async-done | bytes 294928 | tf_op jit(solution)/shard_map/reduce_scatter | solution.py:432
  2559.9 141.0 %reduce-scatter.52.cloned.1.call-done = f32[96,768]{1,0:T(8,128)} async-done(((f32[3072,768]{1,0:T(8,128)}), f32[96,768]{1,0:T(8,128)}) %reduce-scatter.52.cloned.1.call-update) | async-done | bytes 294928 | tf_op jit(solution)/shard_map/reduce_scatter | solution.py:434
  2700.9 189.0 %reduce-scatter.42.cloned.1.call-done = f32[32,2048]{1,0:T(8,128)} async-done(((f32[1024,2048]{1,0:T(8,128)}), f32[32,2048]{1,0:T(8,128)}) %reduce-scatter.42.cloned.1.call-update) | async-done | bytes 262160 | tf_op jit(solution)/shard_map/reduce_scatter | solution.py:422
  2889.8 210.6 %reduce-scatter.32.cloned.1.call-done = f32[1,64,3072]{2,1,0:T(8,128)} async-done(((f32[1,1024,3072]{2,1,0:T(8,128)}), f32[1,64,3072]{2,1,0:T(8,128)}) %reduce-scatter.32.cloned.1.call-update) | async-done | bytes 786448 | tf_op jit(solution)/shard_map/reduce_scatter | solution.py:385
  3100.4 348.9 %reduce-scatter.36.cloned.1.call-done = f32[1,64,4096]{2,1,0:T(8,128)} async-done(((f32[1,1024,4096]{2,1,0:T(8,128)}), f32[1,64,4096]{2,1,0:T(8,128)}) %reduce-scatter.36.cloned.1.call-update) | async-done | bytes 1048592 | tf_op jit(solution)/shard_map/reduce_scatter | solution.py:389
  3449.3 354.9 %reduce-scatter.38.cloned.1.call-done = f32[1,256,1024]{2,1,0:T(8,128)} async-done(((f32[1,4096,1024]{2,1,0:T(8,128)}), f32[1,256,1024]{2,1,0:T(8,128)}) %reduce-scatter.38.cloned.1.call-update) | async-done | bytes 1048592 | tf_op jit(solution)/shard_map/reduce_scatter | solution.py:391
  (752 shorter events, 280.0 us)
Async XLA Ops:
  7.2 287.8 %copy-start.314 = (bf16[32]{0:T(256)(128)(2,1)S(1)}, bf16[32]{0:T(256)(128)(2,1)}, u32[]{:S(2)}) copy-start(bf16[32]{0:T(256)(128)(2,1)} %param.74) | copy-start | bytes 196
  7.2 288.0 %copy-start.315 = (bf16[32]{0:T(256)(128)(2,1)S(1)}, bf16[32]{0:T(256)(128)(2,1)}, u32[]{:S(2)}) copy-start(bf16[32]{0:T(256)(128)(2,1)} %param.73) | copy-start | bytes 196
  7.2 288.2 %copy-start.316 = (bf16[32]{0:T(256)(128)(2,1)S(1)}, bf16[32]{0:T(256)(128)(2,1)}, u32[]{:S(2)}) copy-start(bf16[32]{0:T(256)(128)(2,1)} %param.71) | copy-start | bytes 196
  7.2 288.5 %copy-start.317 = (bf16[32]{0:T(256)(128)(2,1)S(1)}, bf16[32]{0:T(256)(128)(2,1)}, u32[]{:S(2)}) copy-start(bf16[32]{0:T(256)(128)(2,1)} %param.69) | copy-start | bytes 196
  7.3 288.7 %copy-start.318 = (bf16[1,64]{1,0:T(2,128)(2,1)S(1)}, bf16[1,64]{1,0:T(2,128)(2,1)}, u32[]{:S(2)}) copy-start(bf16[1,64]{1,0:T(2,128)(2,1)} %param.65) | copy-start | bytes 388
  7.3 288.9 %copy-start.319 = (bf16[1,64]{1,0:T(2,128)(2,1)S(1)}, bf16[1,64]{1,0:T(2,128)(2,1)}, u32[]{:S(2)}) copy-start(bf16[1,64]{1,0:T(2,128)(2,1)} %param.61) | copy-start | bytes 388
  7.3 289.1 %copy-start.320 = (bf16[24]{0:T(256)(128)(2,1)S(1)}, bf16[24]{0:T(256)(128)(2,1)}, u32[]{:S(2)}) copy-start(bf16[24]{0:T(256)(128)(2,1)} %param.79) | copy-start | bytes 148
  7.3 289.4 %copy-start.321 = (bf16[24]{0:T(256)(128)(2,1)S(1)}, bf16[24]{0:T(256)(128)(2,1)}, u32[]{:S(2)}) copy-start(bf16[24]{0:T(256)(128)(2,1)} %param.83) | copy-start | bytes 148
  7.3 289.6 %copy-start.322 = (bf16[32]{0:T(256)(128)(2,1)S(1)}, bf16[32]{0:T(256)(128)(2,1)}, u32[]{:S(2)}) copy-start(bf16[32]{0:T(256)(128)(2,1)} %param.75) | copy-start | bytes 196
  7.3 289.8 %copy-start.323 = (bf16[48]{0:T(256)(128)(2,1)S(1)}, bf16[48]{0:T(256)(128)(2,1)}, u32[]{:S(2)}) copy-start(bf16[48]{0:T(256)(128)(2,1)} %param.77) | copy-start | bytes 292
  7.3 290.1 %copy-start.324 = (bf16[96]{0:T(256)(128)(2,1)S(1)}, bf16[96]{0:T(256)(128)(2,1)}, u32[]{:S(2)}) copy-start(bf16[96]{0:T(256)(128)(2,1)} %param.81) | copy-start | bytes 580
  7.3 643.1 %copy-start.258 = (s32[2,1,256]{2,1,0:T(1,128)S(1)}, s32[2,1,256]{2,1,0:T(1,128)}, u32[]{:S(2)}) copy-start(s32[2,1,256]{2,1,0:T(1,128)} %param.51) | copy-start | bytes 6148
  7.3 643.1 %copy-start.18 = (bf16[1,2,256,1024]{3,2,1,0:T(8,128)(2,1)S(1)}, bf16[1,2,256,1024]{3,2,1,0:T(8,128)(2,1)}, u32[]{:S(2)}) copy-start(bf16[1,2,256,1024]{3,2,1,0:T(8,128)(2,1)} %param.49) | copy-start | bytes 3145732
  7.4 643.0 %copy-start.302 = (s32[2,4,5]{2,1,0:T(4,128)S(1)}, s32[2,4,5]{2,1,0:T(4,128)}, u32[]{:S(2)}) copy-start(s32[2,4,5]{2,1,0:T(4,128)} %param.55) | copy-start | bytes 484
  7.4 643.0 %copy-start.197 = (f32[2,16,768]{2,1,0:T(8,128)S(1)}, f32[2,16,768]{2,1,0:T(8,128)}, u32[]{:S(2)}) copy-start(f32[2,16,768]{2,1,0:T(8,128)} %param.54) | copy-start | bytes 294916
  7.4 643.0 %copy-start.313 = (s32[2,1,4]{2,1,0:T(1,128)S(1)}, s32[2,1,4]{2,1,0:T(1,128)}, u32[]{:S(2)}) copy-start(s32[2,1,4]{2,1,0:T(1,128)} %param.53) | copy-start | bytes 100
  7.4 643.0 %copy-start.124 = (bf16[2,128,768]{2,1,0:T(8,128)(2,1)S(1)}, bf16[2,128,768]{2,1,0:T(8,128)(2,1)}, u32[]{:S(2)}) copy-start(bf16[2,128,768]{2,1,0:T(8,128)(2,1)} %param.52) | copy-start | bytes 1179652
  7.4 375.8 %all-gather.24.cloned.1.call-start = ((), (), s32[]{:S(2)}) async-start(), calls=%async_computation.22 | async-start | bytes 1216512 | tf_op jit(solution)/shard_map/all_gather | solution.py:508
  8.1 375.1 %all-gather.16.cloned.1.call-start = ((), (), s32[]{:S(2)}) async-start(), calls=%async_computation.18 | async-start | bytes 2228224 | tf_op jit(solution)/shard_map/all_gather | solution.py:487
  8.9 374.3 %all-gather.22.cloned.1.call-start = ((), (), s32[]{:S(2)}) async-start(), calls=%async_computation.21 | async-start | bytes 3649536 | tf_op jit(solution)/shard_map/all_gather | solution.py:506
  9.6 373.6 %all-gather.26.cloned.1.call-start = ((), (), s32[]{:S(2)}) async-start(), calls=%async_computation.23 | async-start | bytes 4866048 | tf_op jit(solution)/shard_map/all_gather | solution.py:510
  10.2 373.1 %all-gather.28.cloned.1.call-start = ((), (), s32[]{:S(2)}) async-start(), calls=%async_computation.24 | async-start | bytes 4866048 | tf_op jit(solution)/shard_map/all_gather | solution.py:512
  10.8 411.4 %all-gather.14.cloned.1.call-start = ((), (), s32[]{:S(2)}) async-start(), calls=%async_computation.17 | async-start | bytes 6684672 | tf_op jit(solution)/shard_map/all_gather | solution.py:485
  11.4 525.2 %all-gather.18.cloned.1.call-start = ((), (), s32[]{:S(2)}) async-start(), calls=%async_computation.19 | async-start | bytes 8912896 | tf_op jit(solution)/shard_map/all_gather | solution.py:489
  12.1 638.3 %all-gather.20.cloned.1.call-start = ((), (), s32[]{:S(2)}) async-start(), calls=%async_computation.20 | async-start | bytes 8912896 | tf_op jit(solution)/shard_map/all_gather | solution.py:491
  12.9 696.3 %all-gather.30.cloned.1.call-start = ((), (), s32[]{:S(2)}) async-start(), calls=%async_computation.25 | async-start | bytes 2162688 | tf_op jit(solution)/shard_map/all_gather | solution.py:498
  13.6 753.7 %all-gather.34.cloned.1.call-start = ((), (), s32[]{:S(2)}) async-start(), calls=%async_computation.27 | async-start | bytes 2162688 | tf_op jit(solution)/shard_map/all_gather | solution.py:502
  14.2 817.3 %all-gather.32.cloned.1.call-start = ((), (), s32[]{:S(2)}) async-start(), calls=%async_computation.26 | async-start | bytes 4325376 | tf_op jit(solution)/shard_map/all_gather | solution.py:500
  14.9 1452.7 %reduce-scatter.56.cloned.1.call-start = ((), (), s32[]{:S(2)}) async-start(), calls=%async_computation.40 | async-start | bytes 557056
  50.7 599.7 %copy-start.176 = (bf16[2048]{0:T(1024)(128)(2,1)}, bf16[2048]{0:T(1024)(128)(2,1)S(1)}, u32[]{:S(2)}) copy-start(bf16[2048]{0:T(1024)(128)(2,1)S(1)} %reduce.26) | copy-start | bytes 12292
  79.7 570.8 %copy-start.143 = (bf16[4096]{0:T(1024)(128)(2,1)}, bf16[4096]{0:T(1024)(128)(2,1)S(1)}, u32[]{:S(2)}) copy-start(bf16[4096]{0:T(1024)(128)(2,1)S(1)} %reduce.27) | copy-start | bytes 24580
  159.3 491.1 %copy-start.201 = (bf16[768,2]{0,1:T(2,128)(2,1)}, bf16[768,2]{0,1:T(2,128)(2,1)S(1)}, u32[]{:S(2)}) copy-start(bf16[768,2]{0,1:T(2,128)(2,1)S(1)} %reshape.1690) | copy-start | bytes 9220
  222.7 427.8 %copy-start.202 = (bf16[768,2]{0,1:T(2,128)(2,1)}, bf16[768,2]{0,1:T(2,128)(2,1)S(1)}, u32[]{:S(2)}) copy-start(bf16[768,2]{0,1:T(2,128)(2,1)S(1)} %reshape.1692) | copy-start | bytes 9220
  260.7 389.8 %copy-start.142 = (bf16[1,2,1024]{2,1,0:T(2,128)(2,1)}, bf16[1,2,1024]{2,1,0:T(2,128)(2,1)S(1)}, u32[]{:S(2)}) copy-start(bf16[1,2,1024]{2,1,0:T(2,128)(2,1)S(1)} %copy.412) | copy-start | bytes 12292
  349.7 300.7 %copy-start.251 = (bf16[3072]{0:T(1024)(128)(2,1)}, bf16[3072]{0:T(1024)(128)(2,1)S(1)}, u32[]{:S(2)}) copy-start(bf16[3072]{0:T(1024)(128)(2,1)S(1)} %get-tuple-element.1340) | copy-start | bytes 18436
  349.7 300.7 %copy-start.272 = (bf16[1536]{0:T(1024)(128)(2,1)}, bf16[1536]{0:T(1024)(128)(2,1)S(1)}, u32[]{:S(2)}) copy-start(bf16[1536]{0:T(1024)(128)(2,1)S(1)} %get-tuple-element.1338) | copy-start | bytes 9220
  349.8 300.7 %copy-start.297 = (bf16[768]{0:T(1024)(128)(2,1)}, bf16[768]{0:T(1024)(128)(2,1)S(1)}, u32[]{:S(2)}) copy-start(bf16[768]{0:T(1024)(128)(2,1)S(1)} %get-tuple-element.1339) | copy-start | bytes 4612
  349.8 300.8 %copy-start.298 = (bf16[768]{0:T(1024)(128)(2,1)}, bf16[768]{0:T(1024)(128)(2,1)S(1)}, u32[]{:S(2)}) copy-start(bf16[768]{0:T(1024)(128)(2,1)S(1)} %get-tuple-element.1341) | copy-start | bytes 4612
  383.1 267.4 %copy-start.203 = (bf16[1024]{0:T(1024)(128)(2,1)}, bf16[1024]{0:T(1024)(128)(2,1)S(1)}, u32[]{:S(2)}) copy-start(bf16[1024]{0:T(1024)(128)(2,1)S(1)} %get-tuple-element.1347) | copy-start | bytes 6148
  383.1 267.4 %copy-start.204 = (bf16[1024]{0:T(1024)(128)(2,1)}, bf16[1024]{0:T(1024)(128)(2,1)S(1)}, u32[]{:S(2)}) copy-start(bf16[1024]{0:T(1024)(128)(2,1)S(1)} %get-tuple-element.1348) | copy-start | bytes 6148
  680.8 150.7 %collective-permute-start = (bf16[256,1024]{1,0:T(8,128)(2,1)}, bf16[256,1024]{1,0:T(8,128)(2,1)S(1)}, u32[]{:S(2)}, u32[]{:S(2)}) collective-permute-start(bf16[256,1024]{1,0:T(8,128)(2,1)} %get-tuple-element.1000), channel_id=1, source_target_pairs={{0,16},{1,17},{2,18},{3,19},{4,20},{5,21},{6,22},{7,23},{8,24},{9,... | collective-permute-start | bytes 1572872 | tf_op jit(solution)/shard_map/ppermute | solution.py:28
  1013.6 14.4 collective-permute-start.2
  1026.7 16.1 collective-permute-start.1
  1218.9 3.2 collective-permute-start.3
  1234.5 248.9 %reduce-scatter.60.cloned.1.call-start = ((), (), s32[]{:S(2)}) async-start(), calls=%async_computation.42 | async-start | bytes 557056
  1236.3 322.1 %reduce-scatter.62.cloned.1.call-start = ((), (), s32[]{:S(2)}) async-start(), calls=%async_computation.43 | async-start | bytes 557056
  1238.1 396.0 %reduce-scatter.64.cloned.1.call-start = ((), (), s32[]{:S(2)}) async-start(), calls=%async_computation.44 | async-start | bytes 557056
  1239.8 470.3 %reduce-scatter.54.cloned.1.call-start = ((), (), s32[]{:S(2)}) async-start(), calls=%async_computation.39 | async-start | bytes 1114112
  1241.3 548.3 %reduce-scatter.58.cloned.1.call-start = ((), (), s32[]{:S(2)}) async-start(), calls=%async_computation.41 | async-start | bytes 2228224
  1243.4 658.4 %reduce-scatter.48.cloned.1.call-start = ((), (), s32[]{:S(2)}) async-start(), calls=%async_computation.36 | async-start | bytes 2433024 | tf_op jit(solution)/shard_map/reduce_scatter | solution.py:430
  1244.0 782.2 %reduce-scatter.46.cloned.1.call-start = ((), (), s32[]{:S(2)}) async-start(), calls=%async_computation.35 | async-start | bytes 7299072 | tf_op jit(solution)/shard_map/reduce_scatter | solution.py:428
  1252.1 924.5 %reduce-scatter.40.cloned.1.call-start = ((), (), s32[]{:S(2)}) async-start(), calls=%async_computation.32 | async-start | bytes 4325376 | tf_op jit(solution)/shard_map/reduce_scatter | solution.py:420
  1252.7 1070.3 %reduce-scatter.44.cloned.1.call-start = ((), (), s32[]{:S(2)}) async-start(), calls=%async_computation.34 | async-start | bytes 4325376 | tf_op jit(solution)/shard_map/reduce_scatter | solution.py:424
  1253.4 1164.8 %reduce-scatter.34.cloned.1.call-start = ((), (), s32[]{:S(2)}) async-start(), calls=%async_computation.29 | async-start | bytes 4456448 | tf_op jit(solution)/shard_map/reduce_scatter | solution.py:387
  1254.2 1305.7 %reduce-scatter.50.cloned.1.call-start = ((), (), s32[]{:S(2)}) async-start(), calls=%async_computation.37 | async-start | bytes 9732096 | tf_op jit(solution)/shard_map/reduce_scatter | solution.py:432
  1254.9 1445.9 %reduce-scatter.52.cloned.1.call-start = ((), (), s32[]{:S(2)}) async-start(), calls=%async_computation.38 | async-start | bytes 9732096 | tf_op jit(solution)/shard_map/reduce_scatter | solution.py:434
  1255.5 1634.3 %reduce-scatter.42.cloned.1.call-start = ((), (), s32[]{:S(2)}) async-start(), calls=%async_computation.33 | async-start | bytes 8650752 | tf_op jit(solution)/shard_map/reduce_scatter | solution.py:422
  1264.8 1835.7 %reduce-scatter.32.cloned.1.call-start = ((), (), s32[]{:S(2)}) async-start(), calls=%async_computation.28 | async-start | bytes 13369344 | tf_op jit(solution)/shard_map/reduce_scatter | solution.py:385
  1277.5 2171.9 %reduce-scatter.36.cloned.1.call-start = ((), (), s32[]{:S(2)}) async-start(), calls=%async_computation.30 | async-start | bytes 17825792 | tf_op jit(solution)/shard_map/reduce_scatter | solution.py:389
  1278.1 2526.2 %reduce-scatter.38.cloned.1.call-start = ((), (), s32[]{:S(2)}) async-start(), calls=%async_computation.31 | async-start | bytes 17825792 | tf_op jit(solution)/shard_map/reduce_scatter | solution.py:391
  1278.9 112.6 %collective-permute-start.4 = (bf16[4,5]{1,0:T(4,128)(2,1)S(1)}, bf16[4,5]{1,0:T(4,128)(2,1)S(1)}, u32[]{:S(2)}, u32[]{:S(2)}) collective-permute-start(bf16[4,5]{1,0:T(4,128)(2,1)S(1)} %convert_element_type.995), channel_id=1, source_target_pairs={{0,16},{1,17},{2,18},{3,19},{4,20},{5,21},{6,22},{7,23},{8,24},{9,... | collective-permute-start | bytes 128 | tf_op jit(solution)/shard_map/ppermute | solution.py:28
  1280.3 112.5 %collective-permute-start.5 = (bf16[4,5]{1,0:T(4,128)(2,1)S(1)}, bf16[4,5]{1,0:T(4,128)(2,1)S(1)}, u32[]{:S(2)}, u32[]{:S(2)}) collective-permute-start(bf16[4,5]{1,0:T(4,128)(2,1)S(1)} %convert_element_type.997), channel_id=1, source_target_pairs={{0,16},{1,17},{2,18},{3,19},{4,20},{5,21},{6,22},{7,23},{8,24},{9,... | collective-permute-start | bytes 128 | tf_op jit(solution)/shard_map/ppermute | solution.py:28
  1281.7 112.8 %collective-permute-start.6 = (bf16[128,768]{1,0:T(8,128)(2,1)S(1)}, bf16[128,768]{1,0:T(8,128)(2,1)S(1)}, u32[]{:S(2)}, u32[]{:S(2)}) collective-permute-start(bf16[128,768]{1,0:T(8,128)(2,1)S(1)} %convert_element_type.999), channel_id=1, source_target_pairs={{0,16},{1,17},{2,18},{3,19},{4,20},{5,21},{6,22},{7,23},{8,24},{9,... | collective-permute-start | bytes 589832 | tf_op jit(solution)/shard_map/ppermute | solution.py:28
  1283.0 112.8 %collective-permute-start.7 = (bf16[128,768]{1,0:T(8,128)(2,1)S(1)}, bf16[128,768]{1,0:T(8,128)(2,1)S(1)}, u32[]{:S(2)}, u32[]{:S(2)}) collective-permute-start(bf16[128,768]{1,0:T(8,128)(2,1)S(1)} %convert_element_type.1001), channel_id=1, source_target_pairs={{0,16},{1,17},{2,18},{3,19},{4,20},{5,21},{6,22},{7,23},{8,24},{9,... | collective-permute-start | bytes 589832 | tf_op jit(solution)/shard_map/ppermute | solution.py:28
  (168 other events, 1504.8 us)
Sparse Core Ops, SparseCore 0:
  11.1 56.5 all-gather.23
  70.5 58.7 all-gather.15
  132.2 59.7 all-gather.21
  194.7 67.0 all-gather.25
  264.5 62.7 all-gather.27
  330.0 92.1 all-gather.13
  424.9 111.5 all-gather.17
  539.3 111.0 all-gather.19
  653.3 55.8 all-gather.29
  711.9 55.2 all-gather.33
  770.2 61.1 all-gather.31
  1234.6 173.3 reduce-scatter.55
  1410.4 72.9 reduce-scatter.59
  1485.5 72.8 reduce-scatter.61
  1560.6 73.4 reduce-scatter.63
  1636.2 73.9 reduce-scatter.53
  1712.4 77.2 reduce-scatter.57
  1796.2 105.5 reduce-scatter.47
  1908.1 118.0 reduce-scatter.45
  2029.0 147.6 reduce-scatter.39
  2179.6 143.3 reduce-scatter.43
  2326.0 92.2 reduce-scatter.33
  2425.7 134.1 reduce-scatter.49
  2566.2 134.6 reduce-scatter.51
  2703.8 185.9 reduce-scatter.41
  2896.9 203.4 reduce-scatter.31
  3103.1 346.1 reduce-scatter.35
  3452.2 352.0 reduce-scatter.37
where the time goes:
time: 3830 us; the launch traced here: 3810 us
  waiting for transfers between devices  2870 us (75%)
  blocking collectives  401 us (10%)
  matrix products  258 us (7%)
  local copies, waits for them, and re-layouts  129 us (3%)
  other arithmetic  82.6 us (2%)
  loops' own time  41.7 us (1%)
    reduce_scatter x1, waiting for transfers between devices, reduce_layer_end(): lax.psum_scatter(feed_down[None], 'dp', scatter_dimension=1, tiled=True)  355 us
    reduce_scatter x1, waiting for transfers between devices, reduce_layer_end(): lax.psum_scatter(feed_up[None], 'dp', scatter_dimension=1, tiled=True)  349 us
    unnamed x34, waiting for transfers between devices  327 us
    reduce_scatter x1, waiting for transfers between devices, reduce_layer_end(): lax.psum_scatter(joined_proj[None], 'dp', scatter_dimension=1, tiled=True)  211 us
    reduce_scatter x1, waiting for transfers between devices, reduce_side_end(): lax.psum_scatter(cross_pair, ('phase', 'dp'), scatter_dimension=0, tiled=...  189 us
    reduce_scatter x1, waiting for transfers between devices, reduce_side_end(): lax.psum_scatter(cross_query, ('phase', 'dp'), scatter_dimension=0, tiled...  150 us
    reduce_scatter x1, waiting for transfers between devices, reduce_side_end(): lax.psum_scatter(cross_proj, ('phase', 'dp'), scatter_dimension=0, tiled=...  146 us
    reduce_scatter x1, waiting for transfers between devices, reduce_side_end(): lax.psum_scatter(query_up, ('phase', 'dp'), scatter_dimension=0, tiled=True)  142 us
  transfers between devices with their start and end apart: 36, of which 27 were waited for; matrix products, arithmetic and copies ran while one was open for 3% of the time, Pallas kernels for 0%

commit v1 on v0

v1 whole, which is shorter than its diff:
```python
from functools import partial

import jax
import jax.numpy as jnp
from jax import lax
from jax.experimental import pallas as pl
from jax.experimental.pallas import tpu as pltpu
from jax.sharding import PartitionSpec as P

HEADS = 16
QHEADS = 12
NEG_FILL = -1e30
EPS_MODEL = 1e-05
EPS_QUERY = 1e-12
BF = jnp.bfloat16
F32 = jnp.float32


def mm(left, right):
    return jnp.dot(left, right, preferred_element_type=F32)


def mm_lt(left, right):
    return lax.dot_general(left, right, (((0,), (0,)), ((), ())), preferred_element_type=F32)


def mm_rt(left, right):
    return lax.dot_general(left, right, (((1,), (1,)), ((), ())), preferred_element_type=F32)


def colsum(matrix):
    return jnp.sum(matrix.astype(F32), axis=0)


def norm_fwd(stream, gain, bias, eps):
    centred = stream - jnp.mean(stream, axis=-1, keepdims=True)
    rstd = lax.rsqrt(jnp.mean(centred * centred, axis=-1, keepdims=True) + eps)
    hat = centred * rstd
    return hat * gain + bias, (hat, rstd)


def norm_bwd(grad, kept, gain):
    hat, rstd = kept
    scaled = grad * gain
    centre = jnp.mean(scaled, axis=-1, keepdims=True)
    along = jnp.mean(scaled * hat, axis=-1, keepdims=True)
    return rstd * (scaled - centre - hat * along), jnp.sum(grad * hat, axis=0), jnp.sum(grad, axis=0)


def gelu_pair(hidden):
    cdf = 0.5 * (1.0 + lax.erf(hidden * 0.7071067811865476))
    pdf = jnp.exp(-0.5 * hidden * hidden) * 0.3989422804014327
    return (hidden * cdf).astype(BF), (cdf + hidden * pdf).astype(BF)


def allowed_bias(key_ref, query_ref, causal_ref):
    same = key_ref[0] == query_ref[0]
    keys = lax.broadcasted_iota(jnp.int32, same.shape, 0)
    queries = lax.broadcasted_iota(jnp.int32, same.shape, 1)
    seen = jnp.logical_and(same, jnp.logical_or(queries >= keys, causal_ref[0] == 0))
    return jnp.where(seen, 0.0, NEG_FILL).astype(F32)


def attn_fwd_body(
    head_size, q_off, k_off, v_off, causal_ref, key_ref, query_ref, q_ref, k_ref, v_ref, o_ref
):
    bias = allowed_bias(key_ref, query_ref, causal_ref)
    scale = head_size ** (-0.5)
    pairs = o_ref.shape[1] // 128

    def one(pair, carry):
        at = pl.multiple_of(pair * 128, 128)
        q2 = q_ref[:, pl.ds(q_off + at, 128)]
        q2 = (q2.astype(F32) * scale).astype(BF)
        k2 = k_ref[:, pl.ds(k_off + at, 128)]
        v_t = v_ref[:, pl.ds(v_off + at, 128)].T
        lane = lax.broadcasted_iota(jnp.int32, q2.shape, 1) < head_size
        mixed = []
        for mine in (lane, jnp.logical_not(lane)):
            scores = mm_rt(k2, jnp.where(mine, q2, jnp.zeros_like(q2))) + bias
            raised = jnp.exp(scores - jnp.max(scores, axis=0, keepdims=True))
            total = jnp.sum(raised, axis=0, keepdims=True)
            mixed.append(mm(v_t, raised.astype(BF)) * (1.0 / total))
        row = lax.broadcasted_iota(jnp.int32, mixed[0].shape, 0) < head_size
        o_ref[:, pl.ds(at, 128)] = jnp.where(row, mixed[0], mixed[1]).T.astype(BF)
        return carry

    lax.fori_loop(0, pairs, one, 0)


def attn_bwd_body(
    head_size, q_off, k_off, v_off, joint, causal_ref, key_ref, query_ref, q_ref, k_ref, v_ref, g_ref, *outs
):
    bias = allowed_bias(key_ref, query_ref, causal_ref)
    scale = head_size ** (-0.5)
    pairs = g_ref.shape[1] // 128
    dq_ref, dk_ref, dv_ref = (outs[0],) * 3 if joint else (outs[0], outs[1], outs[1])

    def one(pair, carry):
        at = pl.multiple_of(pair * 128, 128)
        q2 = q_ref[:, pl.ds(q_off + at, 128)]
        q2 = (q2.astype(F32) * scale).astype(BF)
        k2 = k_ref[:, pl.ds(k_off + at, 128)]
        v2 = v_ref[:, pl.ds(v_off + at, 128)]
        g2 = g_ref[:, pl.ds(at, 128)]
        k_t = k2.T
        lane = lax.broadcasted_iota(jnp.int32, q2.shape, 1) < head_size
        parts = []
        for mine in (lane, jnp.logical_not(lane)):
            scores = mm_rt(k2, jnp.where(mine, q2, jnp.zeros_like(q2))) + bias
            raised = jnp.exp(scores - jnp.max(scores, axis=0, keepdims=True))
            chances = raised * (1.0 / jnp.sum(raised, axis=0, keepdims=True))
            grad_p = mm_rt(v2, jnp.where(mine, g2, jnp.zeros_like(g2)))
            inner = jnp.sum(chances * grad_p, axis=0, keepdims=True)
            grad_s = (chances * (grad_p - inner)).astype(BF)
            grad_v = mm(chances.astype(BF), g2)
            grad_k = mm(grad_s, q2)
            grad_q_t = mm(k_t, grad_s)
            parts.append((grad_q_t, grad_k, grad_v))
        row = lax.broadcasted_iota(jnp.int32, parts[0][0].shape, 0) < head_size
        grad_q = jnp.where(row, parts[0][0], parts[1][0]).T * scale
        dq_ref[:, pl.ds(q_off + at, 128)] = grad_q.astype(BF)
        dk_ref[:, pl.ds(k_off + at, 128)] = jnp.where(lane, parts[0][1], parts[1][1]).astype(BF)
        dv_ref[:, pl.ds(v_off + at, 128)] = jnp.where(lane, parts[0][2], parts[1][2]).astype(BF)
        return carry

    lax.fori_loop(0, pairs, one, 0)


def attn_specs(rows, arrays):
    specs = [
        pl.BlockSpec(memory_space=pltpu.SMEM),
        pl.BlockSpec((1, rows, 1), lambda m: (m, 0, 0)),
        pl.BlockSpec((1, 1, rows), lambda m: (m, 0, 0)),
    ]
    return specs + [pl.BlockSpec((rows, a.shape[1]), lambda m: (m, 0)) for a in arrays]


def attn_params():
    return pltpu.CompilerParams(dimension_semantics=("arbitrary",), vmem_limit_bytes=48 << 20)


def attn_cost(total, rows, width, products):
    return pl.CostEstimate(
        flops=2 * products * total * rows * width,
        transcendentals=total * rows * HEADS,
        bytes_accessed=total * width * 2 * (4 if products == 2 else 7),
    )


def attend(q, k, v, offsets, width, labels, causal):
    rows = labels.shape[1]
    total = q.shape[0]
    return pl.pallas_call(
        partial(attn_fwd_body, width // HEADS, *offsets),
        grid=(total // rows,),
        in_specs=attn_specs(rows, (q, k, v)),
        out_specs=pl.BlockSpec((rows, width), lambda m: (m, 0)),
        out_shape=jax.ShapeDtypeStruct((total, width), BF),
        compiler_params=attn_params(),
        cost_estimate=attn_cost(total, rows, width, 2),
        name="attend_fwd",
    )(causal, labels[:, :, None], labels[:, None, :], q, k, v)


def attend_back(q, k, v, offsets, width, labels, causal, grad, joint):
    rows = labels.shape[1]
    total = q.shape[0]
    widths = (3 * width,) if joint else (width, 2 * width)
    out = pl.pallas_call(
        partial(attn_bwd_body, width // HEADS, *offsets, joint),
        grid=(total // rows,),
        in_specs=attn_specs(rows, (q, k, v, grad)),
        out_specs=[pl.BlockSpec((rows, w), lambda m: (m, 0)) for w in widths],
        out_shape=[jax.ShapeDtypeStruct((total, w), BF) for w in widths],
        compiler_params=attn_params(),
        cost_estimate=attn_cost(total, rows, width, 5),
        name="attend_bwd",
    )(causal, labels[:, :, None], labels[:, None, :], q, k, v, grad)
    return out[0] if joint else tuple(out)


def heads_of(matrix, count):
    return matrix.reshape(matrix.shape[0], count, matrix.shape[1] // count)


def query_work(
    rows_bf, firsts, ends, chosen, adjoint, heat, sheet, hidden_size, shards, vectors
):
    b_joint, b_out, b_up, b_down, gains, shifts = vectors
    width = rows_bf.shape[1]
    folds = hidden_size // width
    w_joint = sheet[:, : 3 * width]
    w_out = sheet[:, 3 * width : 4 * width]
    w_up = sheet[:, 4 * width : 4 * width + hidden_size]
    downs = [
        sheet[:, 4 * width + hidden_size + i * width : 5 * width + hidden_size + i * width]
        for i in range(folds)
    ]

    def fold(matrix):
        split = matrix.reshape(matrix.shape[0], shards, folds, -1)
        return [split[:, :, i].reshape(matrix.shape[0], width) for i in range(folds)]

    def unfold(parts):
        split = [p.reshape(p.shape[0], shards, 1, -1) for p in parts]
        return jnp.concatenate(split, axis=2).reshape(parts[0].shape[0], -1)

    scale = (width // QHEADS) ** (-0.5)
    positions = jnp.arange(rows_bf.shape[0], dtype=jnp.int32)
    allowed = (positions[None, :] >= firsts[:, None]) & (positions[None, :] < ends[:, None])
    pick = (positions[None, :] == firsts[:, None]).astype(BF)
    head_bf = mm(pick, rows_bf).astype(BF)
    queries = (mm(head_bf, w_joint[:, :width]) + b_joint[:width]).astype(BF)
    paired = mm(rows_bf, w_joint[:, width:])
    keys = paired[:, :width].astype(BF)
    values = (paired[:, width:] + b_joint[width:]).astype(BF)
    qh, kh, vh = heads_of(queries, QHEADS), heads_of(keys, QHEADS), heads_of(values, QHEADS)
    scores = jnp.einsum("qhd,khd->hqk", qh, kh, preferred_element_type=F32) * scale
    scores = jnp.where(allowed[None], scores, NEG_FILL)
    chances = jax.nn.softmax(scores, axis=-1)
    chances_bf = chances.astype(BF)
    mixed = jnp.einsum("hqk,khd->qhd", chances_bf, vh, preferred_element_type=F32)
    mixed = mixed.reshape(queries.shape).astype(BF)
    branch = mm(mixed, w_out) + b_out
    middle, kept_one = norm_fwd(head_bf.astype(F32) + branch, gains[0], shifts[0], EPS_QUERY)
    middle_bf = middle.astype(BF)
    active, slope = gelu_pair(mm(middle_bf, w_up) + b_up)
    folded = fold(active)
    fed = sum(mm(part, down) for part, down in zip(folded, downs))
    found, kept_two = norm_fwd(middle + fed + b_down, gains[1], shifts[1], EPS_QUERY)
    raw = jnp.sum(found[:, None, :] * chosen, axis=-1)
    scored = raw / heat
    grad_heat = -jnp.sum(adjoint * raw) / (heat * heat)
    grad_found = jnp.sum((adjoint / heat)[:, :, None] * chosen, axis=1)
    grad_two, gain_two, shift_two = norm_bwd(grad_found, kept_two, gains[1])
    grad_two_bf = grad_two.astype(BF)
    grad_active = unfold([mm_rt(grad_two_bf, down) for down in downs])
    grad_hidden = (grad_active * slope.astype(F32)).astype(BF)
    grad_middle = grad_two + mm_rt(grad_hidden, w_up)
    grad_one, gain_one, shift_one = norm_bwd(grad_middle, kept_one, gains[0])
    grad_one_bf = grad_one.astype(BF)
    grad_mixed = heads_of(mm_rt(grad_one_bf, w_out).astype(BF), QHEADS)
    grad_values = jnp.einsum("hqk,qhd->khd", chances_bf, grad_mixed, preferred_element_type=F32)
    grad_chances = jnp.einsum("qhd,khd->hqk", grad_mixed, vh, preferred_element_type=F32)
    inner = jnp.sum(chances * grad_chances, axis=-1, keepdims=True)
    grad_scores = (chances * (grad_chances - inner)).astype(BF)
    grad_q = jnp.einsum("hqk,khd->qhd", grad_scores, kh, preferred_element_type=F32) * scale
    grad_k = jnp.einsum("hqk,qhd->khd", grad_scores, qh, preferred_element_type=F32) * scale
    grad_q = grad_q.reshape(queries.shape).astype(BF)
    grad_kv = jnp.concatenate(
        [grad_k.reshape(keys.shape), grad_values.reshape(keys.shape)], axis=1
    ).astype(BF)
    grad_heads = grad_one + mm_rt(grad_q, w_joint[:, :width])
    spread = lax.dot_general(
        pick.astype(F32), grad_heads, (((0,), (0,)), ((), ())),
        precision=lax.Precision.HIGHEST, preferred_element_type=F32,
    )
    grad_rows = mm_rt(grad_kv, w_joint[:, width:]) + spread
    factors = [
        head_bf, grad_q, mixed, grad_one_bf, middle_bf, grad_hidden, active, grad_two_bf,
        queries, grad_mixed.reshape(queries.shape),
    ]
    seen = [
        jnp.einsum("hqk,kd->qhd", p, rows_bf, preferred_element_type=F32)
        for p in (grad_scores, chances_bf)
    ]
    seen = jnp.concatenate(seen, axis=2).astype(BF).reshape(-1, 2 * width)
    flat = jnp.concatenate(factors, axis=1).reshape(seen.shape[0], -1)
    mats = jnp.concatenate([seen, flat], axis=1)
    smalls = (
        jnp.concatenate([colsum(grad_q), colsum(grad_kv[:, width:])]),
        colsum(grad_one_bf),
        colsum(grad_hidden),
        colsum(grad_two_bf),
        jnp.stack([gain_one, gain_two]),
        jnp.stack([shift_one, shift_two]),
    )
    return scored, grad_rows, grad_heat, mats, smalls


class Links:
    def __init__(self):
        self.n = lax.axis_size("dp")
        self.half = self.n // 2
        self.bits = self.half.bit_length() - 1
        self.core = lax.axis_index("phase")
        self.dp = lax.axis_index("dp")
        self.is_enc = self.dp < self.half

    def all_pairs(self, value, pairs):
        return lax.ppermute(value, ("phase", "dp"), pairs)

    def swap(self, value):
        n, h = self.n, self.half
        pairs = []
        for i in range(h):
            pairs += [(i, i), (n + i, i + h), (i + h, n + i), (n + i + h, n + i + h)]
        return self.all_pairs(value, pairs)

    def pull_enc(self, value):
        n, h = self.n, self.half
        pairs = []
        for i in range(h):
            pairs += [(i, i), (i + h, n + i)]
        return self.all_pairs(value, pairs)

    def home_enc(self, value):
        n, h = self.n, self.half
        pairs = []
        for i in range(h):
            pairs += [(i, i), (n + i, i + h)]
        return self.all_pairs(value, pairs)

    def push_dec(self, value):
        n, h = self.n, self.half
        pairs = []
        for i in range(h):
            pairs += [(n + i + h, n + i + h), (n + i, i + h)]
        return self.all_pairs(value, pairs)

    def to_dec(self, value):
        return lax.ppermute(value, "dp", [(i, i + self.half) for i in range(self.half)])

    def to_enc(self, value):
        return lax.ppermute(value, "dp", [(i + self.half, i) for i in range(self.half)])

    def across(self, value):
        h = self.half
        pairs = [(i, i + h) for i in range(h)] + [(i + h, i) for i in range(h)]
        return lax.ppermute(value, "dp", pairs)

    def flip(self, value, who="both"):
        first = self.half if who == "dec" else 0
        last = self.half if who == "enc" else self.n
        pairs = []
        for i in range(first, last):
            pairs += [(i, self.n + i), (self.n + i, i)]
        return self.all_pairs(value, pairs)

    def hop(self, value, bit, who):
        first = self.half if who == "dec" else 0
        last = self.half if who == "enc" else self.n
        return lax.ppermute(value, "dp", [(i, i ^ (1 << bit)) for i in range(first, last)])

    def order(self, turn):
        return [(turn + k) % self.bits for k in range(self.bits)]

    def gather_hop(self, held, turn, step, who="both"):
        return self.hop(held, self.order(turn)[step], who)

    def places(self, turn, lead=1):
        order = self.order(turn)
        mine = self.dp % self.half
        masks = [
            sum(((p >> j) & 1) << order[j] for j in range(self.bits)) for p in range(self.half)
        ]
        own = jnp.stack(
            [jnp.bitwise_xor(mine, m) + r * self.half for m in masks for r in range(lead)]
        ).astype(jnp.int32)
        wide = lead * self.half
        return jnp.concatenate([own + self.core * wide, own + (1 - self.core) * wide])

    def half_of(self, left, core):
        wide = left.shape[1] // 2
        return lax.dynamic_slice_in_dim(left, core * wide, wide, 1)

    def reduce_open(self, left, right):
        return self.flip(mm_lt(self.half_of(left, 1 - self.core), right).astype(BF))

    def reduce_own(self, left, right, got):
        own = mm_lt(self.half_of(left, self.core), right) + got.astype(F32)
        shard = left.shape[1] // self.n
        return own.astype(BF).reshape((2,) * self.bits + (shard, right.shape[1]))

    def reduce_step(self, value, turn, step, who="both", lead=0):
        bit = self.order(turn)[step]
        mine = (self.dp >> bit) & 1
        axis = lead + self.bits - 1 - bit
        send = lax.dynamic_slice_in_dim(value, 1 - mine, 1, axis)
        keep = lax.dynamic_slice_in_dim(value, mine, 1, axis)
        got = self.hop(send, bit, who)
        return (keep.astype(F32) + got.astype(F32)).astype(value.dtype)


def weave_body(quarter, streams, place_ref, *refs):
    count = len(streams)
    at = pl.program_id(0)
    for index in range(4):

        @pl.when(jnp.logical_and(at >= index * quarter, at < (index + 1) * quarter))
        def _(index=index):
            out = 4 * count
            for stream, widths in enumerate(streams):
                low = 0
                for width in widths:
                    refs[out][...] = refs[4 * stream + index][0, :, low : low + width]
                    low += width
                    out += 1


def weave(streams, places, widths):
    quarter = streams[0][0].shape[0]
    total = 4 * quarter

    def source(part, index):
        return pl.BlockSpec(
            (1,) + part.shape[1:],
            lambda g, place: (jnp.clip(g - index * quarter, 0, quarter - 1), 0, 0),
        )

    def target(rows, width, stream):
        return pl.BlockSpec((rows, width), lambda g, place: (place[stream, g], 0))

    shapes = [
        (parts[0].shape[1], w, i)
        for i, (parts, ws) in enumerate(zip(streams, widths))
        for w in ws
    ]
    moved = sum(4 * p.size for parts in streams for p in parts)
    return pl.pallas_call(
        partial(weave_body, quarter, widths),
        grid_spec=pltpu.PrefetchScalarGridSpec(
            num_scalar_prefetch=1,
            grid=(total,),
            in_specs=[source(p, i) for parts in streams for i, p in enumerate(parts)],
            out_specs=[target(*shape) for shape in shapes],
        ),
        out_shape=[jax.ShapeDtypeStruct((total * r, w), BF) for r, w, _ in shapes],
        compiler_params=pltpu.CompilerParams(
            dimension_semantics=("arbitrary",), vmem_limit_bytes=48 << 20
        ),
        cost_estimate=pl.CostEstimate(flops=0, transcendentals=0, bytes_accessed=moved),
        name="weave",
    )(places, *[p for parts in streams for p in parts])


def stage(*values):
    return lax.optimization_barrier(values)


def block_of(values, rows):
    flat = jnp.concatenate([v.reshape(1, -1).astype(BF) for v in values], axis=1)
    return jnp.pad(flat, ((0, 0), (0, rows * 128 - flat.size))).reshape(rows, 128)


def local(
    token_vectors,
    generation_result_adjoint,
    sequence_labels,
    inquiry_vectors,
    inquiry_token_spans,
    document_vectors,
    document_slots,
    relevance_adjoint,
    softness_scalar,
    intrinsic_triple_map,
    intrinsic_probe_content_offset,
    intrinsic_mixing_result_map,
    intrinsic_mixing_result_offset,
    perceptron_widen_map,
    perceptron_widen_offset,
    perceptron_narrow_map,
    perceptron_narrow_offset,
    standardize_scales,
    standardize_shifts,
    encoded_mixing_probe_map,
    encoded_mixing_probe_offset,
    encoded_lookup_content_map,
    encoded_mixing_content_offset,
    encoded_mixing_result_map,
    encoded_mixing_result_offset,
    encoded_mixing_scale_factor,
    encoded_mixing_scale_shift,
    retriever_triple_map,
    retriever_probe_content_offset,
    retriever_mixing_result_map,
    retriever_mixing_result_offset,
    retriever_widen_map,
    retriever_widen_offset,
    retriever_narrow_map,
    retriever_narrow_offset,
    retriever_standardize_scales,
    retriever_standardize_shifts,
):
    links = Links()
    n, half, is_enc, core = links.n, links.half, links.is_enc, links.core
    micro, rows, width = token_vectors.shape[1:]
    total = micro * rows
    joint_w = intrinsic_triple_map.shape[2]
    ff = perceptron_widen_map.shape[2]
    heat = softness_scalar[0]

    role_vecs = (
        intrinsic_probe_content_offset,
        intrinsic_mixing_result_offset,
        perceptron_widen_offset,
        perceptron_narrow_offset,
        standardize_scales,
        standardize_shifts,
    )
    cross_vecs = (
        encoded_mixing_probe_offset,
        encoded_mixing_content_offset,
        encoded_mixing_result_offset,
        encoded_mixing_scale_factor,
        encoded_mixing_scale_shift,
    )
    query_vecs = (
        retriever_probe_content_offset,
        retriever_mixing_result_offset,
        retriever_widen_offset,
        retriever_narrow_offset,
        retriever_standardize_scales,
        retriever_standardize_shifts,
    )
    n_role = sum(v.size for v in role_vecs)
    n_cross = sum(v.size for v in cross_vecs)
    n_query = sum(v.size for v in query_vecs)
    everyone = ("phase", "dp")
    shard_rows = intrinsic_triple_map.shape[1]
    q_width = inquiry_vectors.shape[2]
    q_ff = retriever_widen_map.shape[1]
    q_rows = retriever_triple_map.shape[0]
    q_folds = q_ff // q_width
    cross_rows = encoded_mixing_probe_map.shape[0]

    def vectors_of(table, like):
        at, out = 0, []
        for vec in like:
            lead = vec.shape[-2] if vec.ndim > 1 and vec.shape[-2] > 1 else 1
            piece = table[:, at : at + vec.size].reshape(table.shape[0], lead, -1)
            piece = piece.transpose(1, 0, 2).reshape(lead, -1)
            out.append(piece if lead > 1 else piece[0])
            at += vec.size
        return out

    attn_in = jnp.concatenate(
        [
            intrinsic_triple_map[0],
            intrinsic_mixing_result_map[0],
            block_of(role_vecs + (sequence_labels,), shard_rows),
        ],
        axis=1,
    )
    held = list(
        stage(
            links.swap(attn_in),
            links.swap(perceptron_widen_map[0]),
            links.swap(perceptron_narrow_map[0]),
        )
    )
    labels = held[0][:, joint_w + width :].reshape(1, -1)[:, n_role : n_role + total]
    labels = labels.astype(jnp.int32).reshape(micro, rows)
    held = [v[None] for v in held]
    tokens_in, held = stage(token_vectors[0].reshape(total, width), held)
    stream_bf = links.swap(tokens_in)
    adjoint_own = generation_result_adjoint.reshape(total, width)
    query_in = jnp.concatenate(
        [retriever_triple_map, retriever_mixing_result_map, retriever_widen_map]
        + [retriever_narrow_map[i * q_rows : (i + 1) * q_rows] for i in range(q_folds)]
        + [block_of(query_vecs, q_rows)],
        axis=1,
    )
    cross_in = jnp.concatenate(
        [
            encoded_mixing_probe_map,
            encoded_lookup_content_map,
            encoded_mixing_result_map,
            block_of(cross_vecs, cross_rows),
        ],
        axis=1,
    )
    asked = inquiry_token_spans.shape[2]
    chosen_count = document_slots.shape[2]
    ints = jnp.concatenate(
        [
            inquiry_token_spans.reshape(1, -1).astype(F32),
            document_slots.reshape(1, -1).astype(F32),
            relevance_adjoint.reshape(1, -1),
        ],
        axis=1,
    )
    doc_own = jnp.concatenate(
        [
            document_vectors.reshape(-1, q_width),
            jnp.pad(ints, ((0, 0), (0, q_width - ints.size))),
        ]
    )
    q_own = inquiry_vectors.reshape(-1, q_width)
    last = links.bits - 1
    for step in range(last):
        held = [
            jnp.concatenate([v, links.gather_hop(v, turn, step)], axis=0)
            for turn, v in enumerate(held)
        ]
        if step == 0:
            held, stream_bf, adjoint_own, cross_in, doc_own, q_own = stage(
                held, stream_bf, adjoint_own, cross_in, doc_own, q_own
            )
            cross_full = lax.all_gather(cross_in, everyone, axis=0, tiled=True)
        else:
            (held,) = stage(held)
    recv = [links.gather_hop(v, turn, last) for turn, v in enumerate(held)]
    theirs = [links.flip(v) for v in held]
    adjoint_bf = links.push_dec(adjoint_own)
    doc_packet = links.pull_enc(doc_own)
    q_block_rows = links.pull_enc(q_own)
    recv, theirs, adjoint_bf, query_in, doc_packet, q_block_rows = stage(
        recv, theirs, adjoint_bf, query_in, doc_packet, q_block_rows
    )
    query_full = lax.all_gather(query_in, everyone, axis=0, tiled=True)
    got = [links.flip(v) for v in recv]
    w_joint, w_out, w_small, w_up, w_down = weave(
        list(zip(held, recv, theirs, got)),
        jnp.stack([links.places(turn) for turn in range(3)]),
        ((joint_w, width, 128), (ff,), (width,)),
    )
    mine_small = w_small.reshape(n, -1)[:, :n_role].astype(F32)
    b_joint, b_out, b_up, b_down, gains, shifts = vectors_of(mine_small, role_vecs)

    causal = jnp.where(is_enc, 0, 1).astype(jnp.int32).reshape(1)
    plain = jnp.zeros((1,), jnp.int32)
    stream = stream_bf.astype(F32)
    bias_joint = jnp.concatenate([b_joint[:width], jnp.zeros((width,), F32), b_joint[width:]])
    joint = (mm(stream_bf, w_joint) + bias_joint).astype(BF)
    self_off = (0, width, 2 * width)
    mixed = attend(joint, joint, joint, self_off, width, labels, causal)
    first, kept_one = norm_fwd(stream + mm(mixed, w_out) + b_out, gains[0], shifts[0], EPS_MODEL)
    first_bf = first.astype(BF)

    def feed(stream_one, stream_one_bf):
        active, slope = gelu_pair(mm(stream_one_bf, w_up) + b_up)
        result, kept = norm_fwd(
            stream_one + mm(active, w_down) + b_down, gains[1], shifts[1], EPS_MODEL
        )
        return result.astype(BF), active, slope, kept

    def feed_back(grad_result, slope, kept):
        grad_two, gain_two, shift_two = norm_bwd(grad_result, kept, gains[1])
        grad_f = grad_two.astype(BF)
        grad_h = (mm_rt(grad_f, w_down) * slope.astype(F32)).astype(BF)
        return grad_f, grad_h, grad_two + mm_rt(grad_h, w_up), gain_two, shift_two

    def blank(shapes):
        return jax.tree.map(lambda s: jnp.zeros(s.shape, s.dtype), shapes)

    def when(flag, work):
        return lax.cond(flag, work, lambda: blank(jax.eval_shape(work)))

    enc_out, enc_active, enc_slope, enc_kept = when(is_enc, lambda: feed(first, first_bf))
    (enc_out,) = stage(enc_out)
    memory_low = links.to_dec(enc_out)
    (memory_low,) = stage(memory_low)

    cross_off = (0, 0, width)

    def decoder_branch():
        w_cq = cross_full[:, :width]
        w_ckv = cross_full[:, width : 3 * width]
        w_co = cross_full[:, 3 * width : 4 * width]
        cross_small = cross_full[:, 4 * width :]
        cross_small = cross_small.reshape(2 * n, -1).astype(F32)
        cb_q, cb_v, cb_o, c_gain, c_shift = vectors_of(cross_small, cross_vecs)
        cq = (mm(first_bf, w_cq) + cb_q).astype(BF)
        bias_kv = jnp.concatenate([jnp.zeros((width,), F32), cb_v])
        ckv = (mm(memory_low, w_ckv) + bias_kv).astype(BF)
        cmixed = attend(cq, ckv, ckv, cross_off, width, labels, plain)
        second, kept_cross = norm_fwd(
            first + mm(cmixed, w_co) + cb_o, c_gain, c_shift, EPS_MODEL
        )
        second_bf = second.astype(BF)
        decoded, active, slope, kept = feed(second, second_bf)
        grad_f, grad_h, grad_second, gain_two, shift_two = feed_back(
            adjoint_bf.astype(F32), slope, kept
        )
        grad_cross, cgain, cshift = norm_bwd(grad_second, kept_cross, c_gain)
        grad_cross_bf = grad_cross.astype(BF)
        grad_cmixed = mm_rt(grad_cross_bf, w_co).astype(BF)
        grad_cq, grad_ckv = attend_back(
            cq, ckv, ckv, cross_off, width, labels, plain, grad_cmixed, False
        )
        grad_memory = mm_rt(grad_ckv, w_ckv).astype(BF)
        cross_small_grads = (
            colsum(grad_cq),
            colsum(grad_ckv[:, width:]),
            colsum(grad_cross_bf),
            cgain,
            cshift,
        )
        return (
            decoded,
            grad_memory,
            second_bf,
            active,
            grad_f,
            grad_h,
            (gain_two, shift_two),
            cross_small_grads,
            (grad_cross, grad_cross_bf, cmixed, grad_cq, grad_ckv),
        )

    shapes = jax.eval_shape(decoder_branch)
    dec = lax.cond(
        is_enc,
        lambda: (enc_out, jnp.zeros((total, width), BF), first_bf, enc_active) + blank(shapes[4:]),
        decoder_branch,
    )
    (
        layer_rows, grad_memory, feed_in, active, dec_f, dec_h, dec_norm, cross_small_grads, cross_kept
    ) = dec
    grad_memory, cross_kept, query_full = stage(grad_memory, cross_kept, query_full)

    passages = document_vectors.shape[1]
    n_span, n_pick = micro * asked, micro * asked * chosen_count

    def query_branch():
        tail = doc_packet[micro * passages]
        spans = tail[:n_span].astype(jnp.int32).reshape(micro, asked)
        slots = tail[n_span : n_span + n_pick].astype(jnp.int32).reshape(micro, asked, chosen_count)
        adjoint = tail[n_span + n_pick : n_span + 2 * n_pick].reshape(n_span, chosen_count)
        base = jnp.arange(micro, dtype=jnp.int32)[:, None]
        per_block = inquiry_vectors.shape[1]
        ends = jnp.cumsum(spans, axis=1)
        firsts = (ends - spans + base * per_block).reshape(-1)
        ends = (ends + base * per_block).reshape(-1)
        where_doc = (slots + base[:, :, None] * passages).reshape(n_span, chosen_count)
        query_small = query_full[:, 4 * q_width + 2 * q_ff :].reshape(2 * n, -1).astype(F32)
        return query_work(
            q_block_rows,
            firsts,
            ends,
            doc_packet[where_doc],
            adjoint,
            heat,
            query_full,
            q_ff,
            2 * n,
            vectors_of(query_small, query_vecs),
        )

    queried = when(is_enc, query_branch)
    memory_grad = links.to_enc(grad_memory)

    def cross_late():
        grad_cross, grad_cross_bf, cmixed, grad_cq, grad_ckv = cross_kept
        grads = jnp.concatenate(
            [
                mm_lt(first_bf, grad_cq).astype(BF),
                mm_lt(memory_low, grad_ckv).astype(BF),
                mm_lt(cmixed, grad_cross_bf).astype(BF),
            ],
            axis=1,
        )
        return grads, grad_cross + mm_rt(grad_cq, cross_full[:, :width])

    cross_grads, dec_first = lax.cond(
        is_enc,
        lambda: (jnp.zeros((width, 4 * width), BF), jnp.zeros((total, width), F32)),
        cross_late,
    )
    scored, q_grad_rows, grad_heat, query_grads, query_small_grads = queried
    half_rows = query_grads.shape[0] // 2
    factors_got = links.to_dec(query_grads[half_rows:])
    memory_grad, cross_grads, dec_first, query_grads, factors_got = stage(
        memory_grad, cross_grads, dec_first, query_grads, factors_got
    )
    factors = lax.all_gather(
        jnp.where(is_enc, query_grads[:half_rows], factors_got), everyone, axis=0, tiled=True
    )

    def enc_back():
        grad_f, grad_h, grad_first, gain_two, shift_two = feed_back(
            memory_grad.astype(F32), enc_slope, enc_kept
        )
        return grad_f, grad_h, grad_first, (gain_two, shift_two)

    grad_f, grad_h, grad_first, norm_two = lax.cond(
        is_enc, enc_back, lambda: (dec_f, dec_h, dec_first, dec_norm)
    )

    grad_h, grad_f, grad_first, layer_rows = stage(grad_h, grad_f, grad_first, layer_rows)
    layer_home = links.swap(layer_rows)
    up_got = links.reduce_open(feed_in, grad_h)
    down_got = links.reduce_open(active, grad_f)
    cross_pair = cross_grads.reshape(2, width // 2, 4 * width)
    cross_got = links.flip(
        lax.dynamic_index_in_dim(cross_pair, 1 - core, 0, keepdims=False), "dec"
    )
    grad_one, gain_one, shift_one = norm_bwd(grad_first, kept_one, gains[0])
    grad_one_bf = grad_one.astype(BF)
    grad_mixed = mm_rt(grad_one_bf, w_out).astype(BF)
    up_got, down_got, cross_got, grad_mixed, layer_home = stage(
        up_got, down_got, cross_got, grad_mixed, layer_home
    )
    cross_sum = lax.dynamic_index_in_dim(cross_pair, core, 0, keepdims=False)
    cross_sum = (cross_sum.astype(F32) + cross_got.astype(F32)).astype(BF)
    cross_sum = cross_sum.reshape((2,) + (2,) * links.bits + (cross_rows, 4 * width))
    cross_sum = links.reduce_step(cross_sum, 0, 0, "dec", 1)
    up_sum = links.reduce_step(links.reduce_own(feed_in, grad_h, up_got), 1, 0)
    down_sum = links.reduce_step(links.reduce_own(active, grad_f, down_got), 2, 0)
    grad_joint = attend_back(
        joint, joint, joint, self_off, width, labels, causal, grad_mixed, True
    )
    up_sum, down_sum, cross_sum, grad_joint, factors = stage(
        up_sum, down_sum, cross_sum, grad_joint, factors
    )
    device = core * n + links.dp

    def own_columns(matrix, count):
        wide = matrix.shape[1]
        lines = lax.broadcasted_iota(jnp.int32, (wide, count), 0)
        places = lax.broadcasted_iota(jnp.int32, (wide, count), 1) + device * count
        return mm(matrix, (lines == places).astype(BF)).astype(BF)

    all_asked = 2 * n * asked
    seen_keys = own_columns(factors[:, :q_width], q_rows).reshape(all_asked, QHEADS, q_rows)
    seen_values = own_columns(factors[:, q_width : 2 * q_width], q_rows)
    seen_values = seen_values.reshape(all_asked, QHEADS, q_rows)
    factors = factors[:, 2 * q_width :].reshape(all_asked, -1)
    sizes, at, cols = [q_width] * 5 + [q_ff, q_ff] + [q_width] * 3, 0, []
    for size in sizes:
        cols.append(factors[:, at : at + size])
        at += size
    f_head, f_q, f_mixed, f_one, f_middle, f_hidden, f_active, f_two, f_asks, f_gmix = cols

    def by_head(seen, other, scale):
        per_head = jnp.einsum(
            "qhd,qhe->hde", seen, heads_of(other, QHEADS), preferred_element_type=F32
        )
        return per_head.transpose(1, 0, 2).reshape(q_rows, q_width) * scale

    query_k_own = by_head(seen_keys, f_asks, (q_width // QHEADS) ** (-0.5))
    query_v_own = by_head(seen_values, f_gmix, 1.0)
    query_q_own = mm_lt(own_columns(f_head, q_rows), f_q)
    query_out_own = mm_lt(own_columns(f_mixed, q_rows), f_one)
    query_up_own = mm_lt(own_columns(f_middle, q_rows), f_hidden)
    query_down_own = mm_lt(own_columns(f_active, q_rows * q_folds), f_two)
    cross_sum = links.reduce_step(cross_sum, 0, 1, "dec", 1)
    split_joint = [(0, joint_w // 2), (joint_w // 2, joint_w)]
    attn_jobs = [(stream_bf, grad_joint[:, a:b]) for a, b in split_joint]
    attn_jobs += [(mixed, grad_one_bf)]
    attn_got = [links.reduce_open(left, right) for left, right in attn_jobs]
    grad_rows = (grad_one + mm_rt(grad_joint, w_joint)).astype(BF)
    query_own_mats = [
        jnp.concatenate([query_q_own, query_k_own, query_v_own], axis=1),
        query_out_own,
        query_up_own,
        query_down_own,
    ]
    up_sum = links.reduce_step(up_sum, 1, 1)
    down_sum = links.reduce_step(down_sum, 2, 1)

    def role_rows(vec):
        return vec.reshape(n, -1)

    def role_pair_rows(one, two):
        return jnp.stack([role_rows(one), role_rows(two)], axis=1).reshape(n, -1)

    def side_rows(vec):
        lead = vec.reshape(-1, vec.shape[-1]).shape[0]
        return vec.reshape(lead, 2 * n, -1).transpose(1, 0, 2).reshape(2 * n, -1)

    joint_cols = colsum(grad_joint)
    role_grads = jnp.concatenate(
        [
            role_rows(jnp.concatenate([joint_cols[:width], joint_cols[2 * width :]])),
            role_rows(colsum(grad_one_bf)),
            role_rows(colsum(grad_h)),
            role_rows(colsum(grad_f)),
            role_pair_rows(gain_one, norm_two[0]),
            role_pair_rows(shift_one, norm_two[1]),
        ],
        axis=-1,
    )
    def lead_rows(table):
        table = table.reshape(2, 2, half, -1).transpose(0, 2, 1, 3)
        return table.reshape(2, half, -1)

    cross_table = jnp.concatenate([side_rows(v) for v in cross_small_grads], axis=1)
    query_table = jnp.concatenate([side_rows(v) for v in query_small_grads], axis=1)
    small_grads = jnp.concatenate(
        [
            role_grads.reshape(2, half, n_role),
            lead_rows(cross_table),
            lead_rows(query_table),
            jnp.broadcast_to(grad_heat, (2, half, 1)),
        ],
        axis=2,
    )
    small_sum = lax.dynamic_index_in_dim(small_grads, core, 0, keepdims=False)
    small_got = links.flip(lax.dynamic_index_in_dim(small_grads, 1 - core, 0, keepdims=False))
    small_sum = (small_sum + small_got).reshape((2,) * links.bits + (1, -1))
    up_sum, down_sum, cross_sum, attn_got, grad_rows, small_sum = stage(
        up_sum, down_sum, cross_sum, attn_got, grad_rows, small_sum
    )
    rows_home = links.swap(grad_rows)
    for step in range(2, links.bits):
        up_sum = links.reduce_step(up_sum, 1, step)
        down_sum = links.reduce_step(down_sum, 2, step)
        cross_sum = links.reduce_step(cross_sum, 0, step, "dec", 1)
    attn_sum = [
        links.reduce_step(links.reduce_own(left, right, got), turn, 0)
        for turn, ((left, right), got) in enumerate(zip(attn_jobs, attn_got))
    ]
    small_sum = links.reduce_step(small_sum, 0, 0)
    attn_sum, up_sum, down_sum, rows_home, small_sum, cross_sum, query_own_mats = stage(
        attn_sum, up_sum, down_sum, rows_home, small_sum, cross_sum, query_own_mats
    )
    up_own = links.swap(up_sum.reshape(-1, ff)).astype(F32)
    down_own = links.swap(down_sum.reshape(-1, width)).astype(F32)
    for step in range(1, links.bits):
        attn_sum = [links.reduce_step(v, turn, step) for turn, v in enumerate(attn_sum)]
        small_sum = links.reduce_step(small_sum, 0, step)
        if step + 1 < links.bits:
            attn_sum, small_sum = stage(attn_sum, small_sum)
    attn_home = jnp.concatenate([v.reshape(-1, v.shape[-1]) for v in attn_sum], axis=1)
    attn_home = links.swap(attn_home).astype(F32)
    joint_own, out_own = attn_home[:, :joint_w], attn_home[:, joint_w:]
    cross_sum = cross_sum.reshape(2, cross_rows, 4 * width)
    cross_sum = jnp.where(is_enc, links.to_enc(cross_sum[0]), cross_sum[1]).astype(F32)
    cross_own_mats = [
        cross_sum[:, :width],
        cross_sum[:, width : 3 * width],
        cross_sum[:, 3 * width :],
    ]
    small_sum = small_sum.reshape(-1)
    role_own = links.swap(small_sum[:n_role])
    cross_pair = small_sum[n_role : n_role + 2 * n_cross].reshape(2, n_cross)
    query_pair = small_sum[n_role + 2 * n_cross : n_role + 2 * n_cross + 2 * n_query]
    pairs = jnp.concatenate([cross_pair, query_pair.reshape(2, n_query)], axis=1)
    keep_side = jnp.concatenate([jnp.where(is_enc, pairs[0], pairs[1]), small_sum[-1:]])
    send_side = jnp.concatenate([jnp.where(is_enc, pairs[1], pairs[0]), small_sum[-1:]])
    side_own = keep_side + links.across(send_side)
    cross_own = side_own[:n_cross]
    query_own = side_own[n_cross : n_cross + n_query]
    heat_total = side_own[-1:]

    layer_out = layer_home.reshape(1, micro, rows, width)
    input_grad = rows_home.astype(F32).reshape(1, micro, rows, width)

    per_block = inquiry_vectors.shape[1]
    score_row = jnp.pad(scored.reshape(1, -1), ((0, 0), (0, q_width - scored.size))).astype(BF)
    q_packet = jnp.concatenate([q_grad_rows.astype(BF), score_row])
    up_mark, q_packet = stage(up_own, q_packet)
    q_home = links.home_enc(q_packet)
    q_mats = q_home[: micro * per_block].reshape(micro, per_block, q_width)
    s_mats = q_home[micro * per_block :, : scored.size].reshape(micro, 1, -1)
    second = jnp.concatenate(
        [q_mats[1], jnp.pad(s_mats[1], ((0, 0), (0, q_width - s_mats.shape[2])))]
    )
    got_second = lax.ppermute(second, "phase", [(0, 1)])
    question_grad = jnp.where(core == 0, q_mats[0], got_second[:per_block]).astype(F32)[None]
    own_scores = jnp.where(core == 0, s_mats[0], got_second[per_block:, : s_mats.shape[2]])
    scores = own_scores.astype(F32).reshape(1, asked, chosen_count)

    sizes = [
        intrinsic_probe_content_offset.shape[1],
        intrinsic_mixing_result_offset.shape[1],
        perceptron_widen_offset.shape[1],
        perceptron_narrow_offset.shape[1],
        2 * standardize_scales.shape[2],
        2 * standardize_shifts.shape[2],
    ]
    cut, role_out = 0, []
    for size in sizes:
        role_out.append(role_own[cut : cut + size])
        cut += size
    role_tuple = (
        joint_own[None],
        role_out[0][None],
        out_own[None],
        role_out[1][None],
        up_own[None],
        role_out[2][None],
        down_own[None],
        role_out[3][None],
        role_out[4].reshape(1, 2, -1),
        role_out[5].reshape(1, 2, -1),
    )
    c = cross_own.reshape(5, -1)
    cross_tuple = (
        cross_own_mats[0],
        c[0],
        cross_own_mats[1],
        c[1],
        cross_own_mats[2],
        c[2],
        c[3],
        c[4],
    )
    cut, q_out = 0, []
    for part in (
        retriever_probe_content_offset,
        retriever_mixing_result_offset,
        retriever_widen_offset,
        retriever_narrow_offset,
        retriever_standardize_scales,
        retriever_standardize_shifts,
    ):
        q_out.append(query_own[cut : cut + part.size].reshape(part.shape))
        cut += part.size
    query_tuple = (
        query_own_mats[0],
        q_out[0],
        query_own_mats[1],
        q_out[1],
        query_own_mats[2],
        q_out[2],
        query_own_mats[3],
        q_out[3],
        q_out[4],
        q_out[5],
    )
    return (
        (layer_out, input_grad, scores, question_grad, heat_total)
        + role_tuple
        + cross_tuple
        + query_tuple
    )


def solution(mesh):
    row = P(None, "dp", None)
    mat, vec = P("phase", "dp", None), P("phase", "dp")
    pair = P("phase", None, "dp")
    side_mat, side_vec = P(("phase", "dp"), None), P(("phase", "dp"))
    side_pair = P(None, ("phase", "dp"))
    role = (mat, vec, mat, vec, mat, vec, mat, vec, pair, pair)
    cross = (side_mat, side_vec, side_mat, side_vec, side_mat, side_vec, side_vec, side_vec)
    query = (side_mat, side_vec) * 4 + (side_pair, side_pair)
    stream = P("phase", None, "dp", None)
    in_specs = (stream,) + (row,) * 7 + (P(),) + role + cross + query
    out_specs = (stream, stream, mat, mat, P()) + role + cross + query
    return jax.shard_map(local, mesh=mesh, in_specs=in_specs, out_specs=out_specs, check_vma=False)
```

time: 3830 us -> 927 us (0.24)
  waiting for transfers between devices: 2870 us -> 311 us
  blocking collectives: 401 us -> 0 us
  starting transfers between devices: 13.2 us -> 167 us
  matrix products: 258 us -> 151 us
  Pallas kernels: 0 us -> 57.4 us
    reduce_scatter x11 -> x0, waiting for transfers between devices: 2010 us -> none  [the longest x1 355 us: reduce_layer_end(): lax.psum_scatter(feed_down[None], 'dp', scatter_dimension=1, tiled=True)]
    all_gather x11 -> x3, waiting for transfers between devices: 417 us -> 0.02 us  [the longest x1 0.02 us: local(): query_full = lax.all_gather(query_in, everyone, axis=0, tiled=True)]
    unnamed x34 -> x3, waiting for transfers between devices: 327 us -> 0.05 us
    all_gather x6 -> x0, blocking collectives: 276 us -> none  [the longest x1 79.5 us: local(): lax.all_gather(retriever_standardize_scales, ('phase', 'dp'), axis=1, til...]
    ppermute x8 -> x63, waiting for transfers between devices: 112 us -> 311 us  [the longest x27 145 us: all_pairs(): return lax.ppermute(value, ('phase', 'dp'), pairs)]
    ppermute x8 -> x63, starting transfers between devices: 12.1 us -> 167 us  [the longest x27 85.4 us: all_pairs(): return lax.ppermute(value, ('phase', 'dp'), pairs)]
    dot_general x72 -> x52, matrix products: 258 us -> 151 us  [the longest x15 53.4 us: mm(): return jnp.dot(left, right, preferred_element_type=F32)]
    pallas_call x0 -> x3, Pallas kernels: none -> 57.4 us  [the longest x1 22.8 us: weave(): pl.pallas_call(partial(weave_body, quarter, widths), grid_spec=pltpu.Pref...]
  transfers between devices with their start and end apart: 36 -> 66, of which waited for: 27 -> 23; matrix products, arithmetic and copies ran while one was open for 3% -> 37% of each run, Pallas kernels for 0% -> 6%
where the time goes in v1:
time: 927 us; the launch traced here: 914 us
  waiting for transfers between devices  311 us (34%)
  starting transfers between devices  167 us (18%)
  matrix products  151 us (16%)
  local copies, waits for them, and re-layouts  119 us (13%)
  other arithmetic  85.9 us (9%)
  Pallas kernels  57.4 us (6%)
  between operations  16.1 us (2%)
    ppermute x27, waiting for transfers between devices, all_pairs(): return lax.ppermute(value, ('phase', 'dp'), pairs)  145 us
    ppermute x30, waiting for transfers between devices, hop(): lax.ppermute(value, 'dp', [(i, i ^ 1 << bit) for i in range(first, last)])  106 us
    ppermute x27, starting transfers between devices, all_pairs(): return lax.ppermute(value, ('phase', 'dp'), pairs)  85.4 us
    dot_general x15, matrix products, mm(): return jnp.dot(left, right, preferred_element_type=F32)  53.4 us
    dot_general x12, matrix products, mm_rt(): lax.dot_general(left, right, (((1,), (1,)), ((), ())), preferred_element_...  47.2 us
    ppermute x2, starting transfers between devices, to_dec(): lax.ppermute(value, 'dp', [(i, i + self.half) for i in range(self.half)])  46.1 us
    dot_general x14, matrix products, mm_lt(): lax.dot_general(left, right, (((0,), (0,)), ((), ())), preferred_element_...  45.4 us
    ppermute x30, starting transfers between devices, hop(): lax.ppermute(value, 'dp', [(i, i ^ 1 << bit) for i in range(first, last)])  32 us
  transfers between devices with their start and end apart: 66, of which 23 were waited for; matrix products, arithmetic and copies ran while one was open for 37% of the time, Pallas kernels for 6%

profile of v1, /device:TPU:1, one launch (start us, length us, event | category | flops | bytes accessed | tf_op | source)
XLA Modules:
  0.0 913.9 jit_solution(11868485860674787242)
XLA Ops:
  11.4 5.6 collective-permute-start
  18.9 4.5 collective-permute-start.2
  28.3 18.5 %collective-permute-done.1 = bf16[64,4096]{1,0:T(8,128)(2,1)S(1)} collective-permute-done((bf16[64,4096]{1,0:T(8,128)(2,1)}, bf16[64,4096]{1,0:T(8,128)(2,1)S(1)}, u32[]{:S(2)}, u32[]{:S(2)}) %collective-permute-start.1) | collective-permute-done | bytes 524320 | tf_op jit(solution)/shard_map/ppermute | solution.py:292
  46.8 5.6 collective-permute-done.2
  57.0 6.1 collective-permute-start.6
  63.1 3.4 collective-permute-done.5
  69.3 17.4 %collective-permute-done.6 = bf16[512,1024]{1,0:T(8,128)(2,1)} collective-permute-done((bf16[512,1024]{1,0:T(8,128)(2,1)}, bf16[512,1024]{1,0:T(8,128)(2,1)}, u32[]{:S(2)}, u32[]{:S(2)}) %collective-permute-start.6) | collective-permute-done | bytes 1048608 | tf_op jit(solution)/shard_map/ppermute | solution.py:292
  87.8 24.2 %collective-permute-done.9 = bf16[2,256,1024]{2,1,0:T(8,128)(2,1)S(1)} collective-permute-done((bf16[2,256,1024]{2,1,0:T(8,128)(2,1)S(1)}, bf16[2,256,1024]{2,1,0:T(8,128)(2,1)S(1)}, u32[]{:S(2)}, u32[]{:S(2)}) %collective-permute-start.9) | collective-permute-done | bytes 1048608 | tf_op jit(solution)/shard_map/ppermute | solution.py:344
  113.5 8.2 collective-permute-done.8
  126.1 5.9 collective-permute-start.16
  134.7 3.2 collective-permute-start.10
  137.9 23.5 %collective-permute-done.17 = f32[33,768]{1,0:T(8,128)S(1)} collective-permute-done((f32[33,768]{1,0:T(8,128)S(1)}, f32[33,768]{1,0:T(8,128)S(1)}, u32[]{:S(2)}, u32[]{:S(2)}) %collective-permute-start.17) | collective-permute-done | bytes 101408 | tf_op jit(solution)/shard_map/ppermute | solution.py:292
  162.0 3.6 collective-permute-done.11.refs_5_
  171.3 38.2 %collective-permute-done.12.refs_9_ = bf16[4,256,1024]{2,1,0:T(8,128)(2,1)} collective-permute-done((bf16[4,256,1024]{2,1,0:T(8,128)(2,1)}, bf16[4,256,1024]{2,1,0:T(8,128)(2,1)}, u32[]{:S(2)}, u32[]{:S(2)}) %collective-permute-start.12) | collective-permute-done | bytes 2097184 | tf_op jit(solution)/shard_map/ppermute | solution.py:344
  212.5 5.2 collective-permute-done.20.refs_7_
  220.7 22.8 %weave.1 = (bf16[1024,3072]{1,0:T(8,128)(2,1)}, bf16[1024,1024]{1,0:T(8,128)(2,1)S(1)}, bf16[1024,128]{1,0:T(8,128)(2,1)S(1)}, bf16[1024,4096]{1,0:T(8,128)(2,1)}, bf16[4096,1024]{1,0:T(8,128)(2,1)}) custom-call(s32[3,16]{1,0:T(4,128)S(1)} %pad_add_fusion.place_ref, bf16[4,64,4224]{2,1,0:T(8,128)(2,1)} %pad_maximum_fusion.6.refs_0_, ...), custom_call_target="tpu_custom_call" | custom-call | bytes 50855936 | tf_op jit(solution)/shard_map/weave/pallas_call | solution.py:421
  245.7 6.6 add_convert_fusion.6.q_ref.k_ref.v_ref
  252.3 13.2 %attend_fwd.3 = bf16[512,1024]{1,0:T(8,128)(2,1)S(1)} custom-call(s32[1]{0:T(128)} %bitcast.45.causal_ref, s32[2,256,1]{2,1,0:T(8,128)S(1)} %broadcast_in_dim_reshape.19.key_ref, s32[2,1,256]{2,1,0:T(1,128)S(1)} %bitcast.297, bf16[512,3072]{1,0:T(8,128)(2,1)S(1)} %add_convert_fusion.6.q_ref.k_ref.v_ref, ...), custom_call_target="tpu_custom_call" | custom-call | flops 536870912 | bytes 4194304 | tf_op jit(solution)/shard_map/attend_fwd/pallas_call | solution.py:154
  271.7 22.8 %conditional.5 = (bf16[512,1024]{1,0:T(8,128)(2,1)S(1)}, bf16[512,4096]{1,0:T(8,128)(2,1)}, bf16[512,4096]{1,0:T(8,128)(2,1)}, f32[512,1024]{1,0:T(8,128)S(1)}, f32[512,1]{0,1:T(1,128)}) conditional(s32[]{:T(128)} %convert_element_type.564, () %tuple.100, (bf16[512,1024]{1,0:T(8,128)(2,1)S(1)}, bf16[1024,4096]{1,0:T(8,128)(2,1)}, ...), branch_computations={%region_2.3_spmd, %region_3.6_spmd} | conditional | flops 8620868608 | bytes 50436164 | solution.py:649
  271.9 12.0 %fusion.4 = (bf16[512,4096]{1,0:T(8,128)(2,1)}, bf16[512,4096]{1,0:T(8,128)(2,1)}) fusion(f32[4096]{0:T(1024)S(1)} %bitcast.314, bf16[512,1024]{1,0:T(8,128)(2,1)S(1)} %get-tuple-element.130, bf16[1024,4096]{1,0:T(8,128)(2,1)} %get-tuple-element.131), kind=kOutput, calls=%fused_computation.6 | convolution fusion | flops 4320133120 | bytes 17842176 | tf_op jit(solution)/shard_map/cond/branch_1_fun/dot_general | solution.py:20
  283.9 8.4 fusion.215
  296.7 31.0 %collective-permute-done.22 = bf16[512,1024]{1,0:T(8,128)(2,1)} collective-permute-done((bf16[512,1024]{1,0:T(8,128)(2,1)S(1)}, bf16[512,1024]{1,0:T(8,128)(2,1)}, u32[]{:S(2)}, u32[]{:S(2)}) %collective-permute-start.22) | collective-permute-done | bytes 1048608 | tf_op jit(solution)/shard_map/ppermute | solution.py:323
  327.7 17.2 %conditional.6 = (bf16[512,1024]{1,0:T(8,128)(2,1)}, bf16[512,1024]{1,0:T(8,128)(2,1)S(1)}, bf16[512,1024]{1,0:T(8,128)(2,1)}, bf16[512,4096]{1,0:T(8,128)(2,1)}...) conditional(s32[]{:T(128)} %convert_element_type.564, ...), branch_computations={%region_6.22_spmd, %region_22.23_spmd} | conditional | flops 26658598912 | bytes 213386096 | solution.py:704
  347.2 71.8 %conditional.8 = (f32[]{:T(128)}, bf16[96,2560]{1,0:T(8,128)(2,1)S(1)}, f32[2,768]{1,0:T(2,128)S(1)}, f32[2,768]{1,0:T(2,128)}, bf16[256,768]{1,0:T(8,128)(2,1)}...) conditional(s32[]{:T(128)} %convert_element_type.564, ...), branch_computations={%region_25.26_spmd, %region_26.51_spmd} | conditional | flops 1519886464 | bytes 60356568 | solution.py:649
  363.4 3.7 multiply_convert_fusion.6
  391.2 4.4 multiply_reduce_fusion.11
  420.4 43.8 %collective-permute-start.24 = (bf16[48,2560]{1,0:T(8,128)(2,1)}, bf16[48,2560]{1,0:T(8,128)(2,1)S(1)}, u32[]{:S(2)}, u32[]{:S(2)}) collective-permute-start(bf16[48,2560]{1,0:T(8,128)(2,1)} %slice.484), channel_id=1, source_target_pairs={{0,8},{1,9},{2,10},{3,11},{4,12},{5,13},{6,14},{7,15},{16,24},{17,... | collective-permute-start | bytes 737288 | tf_op jit(solution)/shard_map/ppermute | solution.py:323
  464.2 6.0 conditional.7
  464.3 4.4 broadcast.417
  470.2 24.7 %collective-permute-done.23 = bf16[512,1024]{1,0:T(8,128)(2,1)S(1)} collective-permute-done((bf16[512,1024]{1,0:T(8,128)(2,1)}, bf16[512,1024]{1,0:T(8,128)(2,1)S(1)}, u32[]{:S(2)}, u32[]{:S(2)}) %collective-permute-start.23) | collective-permute-done | bytes 1048608 | tf_op jit(solution)/shard_map/ppermute | solution.py:326
  496.7 23.8 %conditional.9 = ((bf16[512,1024]{1,0:T(8,128)(2,1)}, bf16[512,4096]{1,0:T(8,128)(2,1)}, f32[512,1024]{1,0:T(8,128)}, f32[1024]{0:T(1024)}, f32[1024]{0:T(1024)})) conditional(s32[]{:T(128)} %convert_element_type.564, (bf16[512,1024]{1,0:T(8,128)(2,1)}, bf16[512,4096]{1,0:T(8,128)(2,1)}, f32[512,1024]{1,0:T(8,128)}, f32[1024]{0:T(1024)}, ...), branch_computations={%region_51.52_spmd, %region_52.57_spmd} | conditional | flops 8607758336 | bytes 72405152 | solution.py:778
  500.0 9.2 %multiply_convert_fusion.1 = bf16[512,4096]{1,0:T(8,128)(2,1)S(1)} fusion(bf16[512,4096]{1,0:T(8,128)(2,1)} %get-tuple-element.171, bf16[512,1024]{1,0:T(8,128)(2,1)S(1)} %fusion.17, bf16[4096,1024]{1,0:T(8,128)(2,1)} %get-tuple-element.170), kind=kOutput, calls=%fused_computation.22 | convolution fusion | flops 4301258752 | bytes 17825792 | tf_op jit(solution)/shard_map/cond/branch_1_fun/dot_general | solution.py:28
  509.2 10.8 %convolution_add_fusion = f32[512,1024]{1,0:T(8,128)} fusion(bf16[512,4096]{1,0:T(8,128)(2,1)S(1)} %multiply_convert_fusion.1, bf16[1024,4096]{1,0:T(8,128)(2,1)} %get-tuple-element.172, f32[512,1024]{1,0:T(8,128)S(1)} %get-tuple-element.169, f32[512]{0:T(512)S(1)} %get-tuple-element.525, f32[512]{0:T(512)S(1)} %get-tuple-element.526, ...), kind=kOutput, calls=%fused_computation.33 | convolution fusion | flops 4298637312 | bytes 17836032 | tf_op jit(solution)/shard_map/cond/branch_1_fun/dot_general | solution.py:28
  520.5 6.4 convolution_convert_fusion.10
  528.0 4.5 convolution_convert_fusion.9
  532.6 4.8 dynamic-slice_bitcast_fusion
  542.6 7.8 collective-permute-done.48
  556.7 5.6 collective-permute-start.28
  565.2 3.2 convert_reduce_fusion.12
  569.2 3.8 convert_reduce_fusion.15
  575.3 29.5 %collective-permute-done.28 = bf16[512,1024]{1,0:T(8,128)(2,1)} collective-permute-done((bf16[512,1024]{1,0:T(8,128)(2,1)}, bf16[512,1024]{1,0:T(8,128)(2,1)}, u32[]{:S(2)}, u32[]{:S(2)}) %collective-permute-start.28) | collective-permute-done | bytes 1048608 | tf_op jit(solution)/shard_map/ppermute | solution.py:292
  604.8 5.2 add_convert_fusion.4
  612.7 5.1 fusion.126
  623.1 4.7 add_convert_fusion.5
  638.0 21.4 %attend_bwd.3 = bf16[512,3072]{1,0:T(8,128)(2,1)S(1)} custom-call(s32[1]{0:T(128)} %bitcast.45.causal_ref, s32[2,256,1]{2,1,0:T(8,128)S(1)} %copy-done.4, s32[2,1,256]{2,1,0:T(1,128)S(1)} %bitcast.298, bf16[512,3072]{1,0:T(8,128)(2,1)} %copy-done, bf16[512,3072]{1,0:T(8,128)(2,1)} %copy-done, bf16[512,3072]{1,0:T(8,128)(2,1)} %copy-done, ...), custom_call_target="tpu_custom_call" | custom-call | flops 1342177280 | bytes 7340032 | tf_op jit(solution)/shard_map/attend_bwd/pallas_call | solution.py:170
  659.4 4.1 add_convert_fusion.8
  663.5 3.9 add_convert_fusion.7
  667.4 3.7 add_convert_fusion.9
  671.2 3.9 slice.492
  675.0 3.0 fusion.133
  681.1 7.2 reshape.873
  693.3 3.2 convolution_convert_fusion.12
  696.5 3.2 convolution_convert_fusion.11
  705.3 3.5 reshape.874
  713.1 3.6 reshape.876
  719.2 7.9 add_convert_fusion.11
  742.7 19.6 %collective-permute-done.33 = bf16[1,2,1,256,1024]{4,3,2,1,0:T(8,128)(2,1)} collective-permute-done((bf16[1,2,1,256,1024]{4,3,2,1,0:T(8,128)(2,1)}, bf16[1,2,1,256,1024]{4,3,2,1,0:T(8,128)(2,1)}, u32[]{:S(2)}, u32[]{:S(2)}) %collective-permute-start.33) | collective-permute-done | bytes 1048608 | tf_op jit(solution)/shard_map/ppermute | solution.py:344
  779.5 25.0 %collective-permute-start.44 = (bf16[512,1024]{1,0:T(8,128)(2,1)S(1)}, bf16[512,1024]{1,0:T(8,128)(2,1)S(1)}, u32[]{:S(2)}, u32[]{:S(2)}) collective-permute-start(bf16[512,1024]{1,0:T(8,128)(2,1)S(1)} %copy-done.157), channel_id=1, source_target_pairs={{0,0},{16,8},{8,16},{24,24},{1,1},{17,9},{9,17},{25,25},{2,2},{18,... | collective-permute-start | bytes 3145736 | tf_op jit(solution)/shard_map/ppermute | solution.py:292
  805.5 22.7 %collective-permute-done.44 = bf16[512,1024]{1,0:T(8,128)(2,1)S(1)} collective-permute-done((bf16[512,1024]{1,0:T(8,128)(2,1)S(1)}, bf16[512,1024]{1,0:T(8,128)(2,1)S(1)}, u32[]{:S(2)}, u32[]{:S(2)}) %collective-permute-start.44) | collective-permute-done | bytes 1048608 | tf_op jit(solution)/shard_map/ppermute | solution.py:292
  835.2 6.1 collective-permute-start.61
  849.8 7.6 collective-permute-done.54
  861.7 3.4 collective-permute-done.55
  865.1 9.2 %collective-permute-start.60 = (f32[768]{0:T(1024)S(1)}, f32[768]{0:T(1024)S(1)}, u32[]{:S(2)}, u32[]{:S(2)}) collective-permute-start(f32[768]{0:T(1024)S(1)} %slice_reduce_fusion.4), channel_id=1, source_target_pairs={{0,0},{16,8},{8,16},{24,24},{1,1},{17,9},{9,17},{25,25},{2,2},{18,... | collective-permute-start | bytes 9224 | tf_op jit(solution)/shard_map/ppermute | solution.py:292
  891.6 11.4 %collective-permute-done.59 = bf16[64,4096]{1,0:T(8,128)(2,1)S(1)} collective-permute-done((bf16[64,4096]{1,0:T(8,128)(2,1)S(1)}, bf16[64,4096]{1,0:T(8,128)(2,1)S(1)}, u32[]{:S(2)}, u32[]{:S(2)}) %collective-permute-start.59) | collective-permute-done | bytes 524320 | tf_op jit(solution)/shard_map/ppermute | solution.py:292
  (758 shorter events, 268.4 us)
Async XLA Ops:
  7.2 320.5 %all-gather.4.cloned.1.call-start = ((), (), s32[]{:S(2)}) async-start(), calls=%async_computation | async-start | bytes 8921088 | tf_op jit(solution)/shard_map/all_gather | solution.py:601
  11.4 41.0 %collective-permute-start = (bf16[64,4224]{1,0:T(8,128)(2,1)S(1)}, bf16[64,4224]{1,0:T(8,128)(2,1)S(1)}, u32[]{:S(2)}, u32[]{:S(2)}) collective-permute-start(bf16[64,4224]{1,0:T(8,128)(2,1)S(1)} %pad_maximum_fusion.12), channel_id=1, source_target_pairs={{0,0},{16,8},{8,16},{24,24},{1,1},{17,9},{9,17},{25,25},{2,2},{18,... | collective-permute-start | bytes 1622024 | tf_op jit(solution)/shard_map/ppermute | solution.py:292
  17.0 29.8 %collective-permute-start.1 = (bf16[64,4096]{1,0:T(8,128)(2,1)}, bf16[64,4096]{1,0:T(8,128)(2,1)S(1)}, u32[]{:S(2)}, u32[]{:S(2)}) collective-permute-start(bf16[64,4096]{1,0:T(8,128)(2,1)} %bitcast.332), channel_id=1, source_target_pairs={{0,0},{16,8},{8,16},{24,24},{1,1},{17,9},{9,17},{25,25},{2,2},{18,... | collective-permute-start | bytes 1572872 | tf_op jit(solution)/shard_map/ppermute | solution.py:292
  18.9 33.5 %collective-permute-start.2 = (bf16[256,1024]{1,0:T(8,128)(2,1)}, bf16[256,1024]{1,0:T(8,128)(2,1)S(1)}, u32[]{:S(2)}, u32[]{:S(2)}) collective-permute-start(bf16[256,1024]{1,0:T(8,128)(2,1)} %bitcast.333), channel_id=1, source_target_pairs={{0,0},{16,8},{8,16},{24,24},{1,1},{17,9},{9,17},{25,25},{2,2},{18,... | collective-permute-start | bytes 1572872 | tf_op jit(solution)/shard_map/ppermute | solution.py:292
  52.4 14.1 %collective-permute-start.5 = (bf16[1,256,1024]{2,1,0:T(8,128)(2,1)S(1)}, bf16[1,256,1024]{2,1,0:T(8,128)(2,1)S(1)}, u32[]{:S(2)}, u32[]{:S(2)}) collective-permute-start(bf16[1,256,1024]{2,1,0:T(8,128)(2,1)S(1)} %bitcast.278), channel_id=1, source_target_pairs={{0,4},{1,5},{2,6},{3,7},{4,0},{5,1},{6,2},{7,3},{8,12},{9,13},{10,... | collective-permute-start | bytes 1572872 | tf_op jit(solution)/shard_map/ppermute | solution.py:344
  52.9 13.7 %collective-permute-start.4 = (bf16[1,64,4096]{2,1,0:T(8,128)(2,1)S(1)}, bf16[1,64,4096]{2,1,0:T(8,128)(2,1)}, u32[]{:S(2)}, u32[]{:S(2)}) collective-permute-start(bf16[1,64,4096]{2,1,0:T(8,128)(2,1)S(1)} %bitcast.276), channel_id=1, source_target_pairs={{0,2},{1,3},{2,0},{3,1},{4,6},{5,7},{6,4},{7,5},{8,10},{9,11},{10,... | collective-permute-start | bytes 1572872 | tf_op jit(solution)/shard_map/ppermute | solution.py:344
  55.8 12.0 %collective-permute-start.3 = (bf16[1,64,4224]{2,1,0:T(8,128)(2,1)S(1)}, bf16[1,64,4224]{2,1,0:T(8,128)(2,1)S(1)}, u32[]{:S(2)}, u32[]{:S(2)}) collective-permute-start(bf16[1,64,4224]{2,1,0:T(8,128)(2,1)S(1)} %bitcast.272), channel_id=1, source_target_pairs={{0,1},{1,0},{2,3},{3,2},{4,5},{5,4},{6,7},{7,6},{8,9},{9,8},{10,11... | collective-permute-start | bytes 1622024 | tf_op jit(solution)/shard_map/ppermute | solution.py:344
  57.0 29.7 %collective-permute-start.6 = (bf16[512,1024]{1,0:T(8,128)(2,1)}, bf16[512,1024]{1,0:T(8,128)(2,1)}, u32[]{:S(2)}, u32[]{:S(2)}) collective-permute-start(bf16[512,1024]{1,0:T(8,128)(2,1)} %bitcast.330), channel_id=1, source_target_pairs={{0,0},{16,8},{8,16},{24,24},{1,1},{17,9},{9,17},{25,25},{2,2},{18,... | collective-permute-start | bytes 3145736 | tf_op jit(solution)/shard_map/ppermute | solution.py:292
  86.7 258.2 %all-gather.6.cloned.1.call-start = ((), (), s32[]{:S(2)}) async-start(), calls=%async_computation.1 | async-start | bytes 14800896 | tf_op jit(solution)/shard_map/all_gather | solution.py:612
  86.8 25.2 %collective-permute-start.9 = (bf16[2,256,1024]{2,1,0:T(8,128)(2,1)S(1)}, bf16[2,256,1024]{2,1,0:T(8,128)(2,1)S(1)}, u32[]{:S(2)}, u32[]{:S(2)}) collective-permute-start(bf16[2,256,1024]{2,1,0:T(8,128)(2,1)S(1)} %pad_maximum_fusion.11), channel_id=1, source_target_pairs={{0,1},{1,0},{2,3},{3,2},{4,5},{5,4},{6,7},{7,6},{8,9},{9,8},{10,11... | collective-permute-start | bytes 3145736 | tf_op jit(solution)/shard_map/ppermute | solution.py:344
  87.1 34.6 %collective-permute-start.8 = (bf16[2,64,4096]{2,1,0:T(8,128)(2,1)S(1)}, bf16[2,64,4096]{2,1,0:T(8,128)(2,1)S(1)}, u32[]{:S(2)}, u32[]{:S(2)}) collective-permute-start(bf16[2,64,4096]{2,1,0:T(8,128)(2,1)S(1)} %pad_maximum_fusion.10), channel_id=1, source_target_pairs={{0,4},{1,5},{2,6},{3,7},{4,0},{5,1},{6,2},{7,3},{8,12},{9,13},{10,... | collective-permute-start | bytes 3145736 | tf_op jit(solution)/shard_map/ppermute | solution.py:344
  87.1 36.2 %collective-permute-start.7 = (bf16[2,64,4224]{2,1,0:T(8,128)(2,1)S(1)}, bf16[2,64,4224]{2,1,0:T(8,128)(2,1)S(1)}, u32[]{:S(2)}, u32[]{:S(2)}) collective-permute-start(bf16[2,64,4224]{2,1,0:T(8,128)(2,1)S(1)} %pad_maximum_fusion.9), channel_id=1, source_target_pairs={{0,2},{1,3},{2,0},{3,1},{4,6},{5,7},{6,4},{7,5},{8,10},{9,11},{10,... | collective-permute-start | bytes 3244040 | tf_op jit(solution)/shard_map/ppermute | solution.py:344
  124.9 40.7 %collective-permute-start.11 = (bf16[4,64,4096]{2,1,0:T(8,128)(2,1)S(1)}, bf16[4,64,4096]{2,1,0:T(8,128)(2,1)S(1)}, u32[]{:S(2)}, u32[]{:S(2)}) collective-permute-start(bf16[4,64,4096]{2,1,0:T(8,128)(2,1)S(1)} %pad_maximum_fusion.7.refs_4_), channel_id=1, source_target_pairs={{0,1},{1,0},{2,3},{3,2},{4,5},{5,4},{6,7},{7,6},{8,9},{9,8},{10,11... | collective-permute-start | bytes 6291464 | tf_op jit(solution)/shard_map/ppermute | solution.py:344
  126.1 35.8 %collective-permute-start.16 = (bf16[512,1024]{1,0:T(8,128)(2,1)S(1)}, bf16[512,1024]{1,0:T(8,128)(2,1)S(1)}, u32[]{:S(2)}, u32[]{:S(2)}) collective-permute-start(bf16[512,1024]{1,0:T(8,128)(2,1)S(1)} %bitcast.331), channel_id=1, source_target_pairs={{24,24},{16,8},{25,25},{17,9},{26,26},{18,10},{27,27},{19,11},{28,... | collective-permute-start | bytes 3145736 | tf_op jit(solution)/shard_map/ppermute | solution.py:292
  132.1 29.4 %collective-permute-start.18 = (bf16[256,768]{1,0:T(8,128)(2,1)S(1)}, bf16[256,768]{1,0:T(8,128)(2,1)S(1)}, u32[]{:S(2)}, u32[]{:S(2)}) collective-permute-start(bf16[256,768]{1,0:T(8,128)(2,1)S(1)} %bitcast.334), channel_id=1, source_target_pairs={{0,0},{8,16},{1,1},{9,17},{2,2},{10,18},{3,3},{11,19},{4,4},{12,20... | collective-permute-start | bytes 1179656 | tf_op jit(solution)/shard_map/ppermute | solution.py:292
  133.4 28.1 %collective-permute-start.17 = (f32[33,768]{1,0:T(8,128)S(1)}, f32[33,768]{1,0:T(8,128)S(1)}, u32[]{:S(2)}, u32[]{:S(2)}) collective-permute-start(f32[33,768]{1,0:T(8,128)S(1)} %copy-done.73), channel_id=1, source_target_pairs={{0,0},{8,16},{1,1},{9,17},{2,2},{10,18},{3,3},{11,19},{4,4},{12,20... | collective-permute-start | bytes 304136 | tf_op jit(solution)/shard_map/ppermute | solution.py:292
  134.7 74.8 %collective-permute-start.10 = (bf16[4,64,4224]{2,1,0:T(8,128)(2,1)}, bf16[4,64,4224]{2,1,0:T(8,128)(2,1)}, u32[]{:S(2)}, u32[]{:S(2)}) collective-permute-start(bf16[4,64,4224]{2,1,0:T(8,128)(2,1)} %pad_maximum_fusion.6.refs_0_), channel_id=1, source_target_pairs={{0,4},{1,5},{2,6},{3,7},{4,0},{5,1},{6,2},{7,3},{8,12},{9,13},{10,... | collective-permute-start | bytes 6488072 | tf_op jit(solution)/shard_map/ppermute | solution.py:344
  161.4 48.0 %collective-permute-start.13 = (bf16[4,64,4224]{2,1,0:T(8,128)(2,1)}, bf16[4,64,4224]{2,1,0:T(8,128)(2,1)}, u32[]{:S(2)}, u32[]{:S(2)}) collective-permute-start(bf16[4,64,4224]{2,1,0:T(8,128)(2,1)} %pad_maximum_fusion.6.refs_0_), channel_id=1, source_target_pairs={{0,16},{16,0},{1,17},{17,1},{2,18},{18,2},{3,19},{19,3},{4,20},{20... | collective-permute-start | bytes 6488072 | tf_op jit(solution)/shard_map/ppermute | solution.py:292
  161.5 48.0 %collective-permute-start.14 = (bf16[4,64,4096]{2,1,0:T(8,128)(2,1)S(1)}, bf16[4,64,4096]{2,1,0:T(8,128)(2,1)}, u32[]{:S(2)}, u32[]{:S(2)}) collective-permute-start(bf16[4,64,4096]{2,1,0:T(8,128)(2,1)S(1)} %pad_maximum_fusion.7.refs_4_), channel_id=1, source_target_pairs={{0,16},{16,0},{1,17},{17,1},{2,18},{18,2},{3,19},{19,3},{4,20},{20... | collective-permute-start | bytes 6291464 | tf_op jit(solution)/shard_map/ppermute | solution.py:292
  162.0 47.5 %collective-permute-start.12 = (bf16[4,256,1024]{2,1,0:T(8,128)(2,1)}, bf16[4,256,1024]{2,1,0:T(8,128)(2,1)}, u32[]{:S(2)}, u32[]{:S(2)}) collective-permute-start(bf16[4,256,1024]{2,1,0:T(8,128)(2,1)} %pad_maximum_fusion.8.refs_8_), channel_id=1, source_target_pairs={{0,2},{1,3},{2,0},{3,1},{4,6},{5,7},{6,4},{7,5},{8,10},{9,11},{10,... | collective-permute-start | bytes 6291464 | tf_op jit(solution)/shard_map/ppermute | solution.py:344
  166.9 42.5 %collective-permute-start.15 = (bf16[4,256,1024]{2,1,0:T(8,128)(2,1)}, bf16[4,256,1024]{2,1,0:T(8,128)(2,1)}, u32[]{:S(2)}, u32[]{:S(2)}) collective-permute-start(bf16[4,256,1024]{2,1,0:T(8,128)(2,1)} %pad_maximum_fusion.8.refs_8_), channel_id=1, source_target_pairs={{0,16},{16,0},{1,17},{17,1},{2,18},{18,2},{3,19},{19,3},{4,20},{20... | collective-permute-start | bytes 6291464 | tf_op jit(solution)/shard_map/ppermute | solution.py:292
  209.5 461.6 %all-gather.8.cloned.1.call-start = ((), (), s32[]{:S(2)}) async-start(), calls=%async_computation.2 | async-start | bytes 8110080 | tf_op jit(solution)/shard_map/all_gather | solution.py:768
  209.6 11.2 %collective-permute-start.19 = (bf16[4,64,4224]{2,1,0:T(8,128)(2,1)}, bf16[4,64,4224]{2,1,0:T(8,128)(2,1)}, u32[]{:S(2)}, u32[]{:S(2)}) collective-permute-start(bf16[4,64,4224]{2,1,0:T(8,128)(2,1)} %collective-permute-done.10.refs_1_), channel_id=1, source_target_pairs={{0,16},{16,0},{1,17},{17,1},{2,18},{18,2},{3,19},{19,3},{4,20},{20... | collective-permute-start | bytes 6488072 | tf_op jit(solution)/shard_map/ppermute | solution.py:292
  210.5 7.2 collective-permute-start.20
  210.6 10.1 %collective-permute-start.21 = (bf16[4,256,1024]{2,1,0:T(8,128)(2,1)}, bf16[4,256,1024]{2,1,0:T(8,128)(2,1)}, u32[]{:S(2)}, u32[]{:S(2)}) collective-permute-start(bf16[4,256,1024]{2,1,0:T(8,128)(2,1)} %collective-permute-done.12.refs_9_), channel_id=1, source_target_pairs={{0,16},{16,0},{1,17},{17,1},{2,18},{18,2},{3,19},{19,3},{4,20},{20... | collective-permute-start | bytes 6291464 | tf_op jit(solution)/shard_map/ppermute | solution.py:292
  294.4 33.3 %collective-permute-start.22 = (bf16[512,1024]{1,0:T(8,128)(2,1)S(1)}, bf16[512,1024]{1,0:T(8,128)(2,1)}, u32[]{:S(2)}, u32[]{:S(2)}) collective-permute-start(bf16[512,1024]{1,0:T(8,128)(2,1)S(1)} %get-tuple-element.359), channel_id=1, source_target_pairs={{0,8},{1,9},{2,10},{3,11},{4,12},{5,13},{6,14},{7,15},{16,24},{17,... | collective-permute-start | bytes 3145736 | tf_op jit(solution)/shard_map/ppermute | solution.py:323
  345.9 149.1 %collective-permute-start.23 = (bf16[512,1024]{1,0:T(8,128)(2,1)}, bf16[512,1024]{1,0:T(8,128)(2,1)S(1)}, u32[]{:S(2)}, u32[]{:S(2)}) collective-permute-start(bf16[512,1024]{1,0:T(8,128)(2,1)} %copy-done.158), channel_id=1, source_target_pairs={{8,0},{9,1},{10,2},{11,3},{12,4},{13,5},{14,6},{15,7},{24,16},{25,... | collective-permute-start | bytes 3145736 | tf_op jit(solution)/shard_map/ppermute | solution.py:326
  420.4 49.9 %collective-permute-start.24 = (bf16[48,2560]{1,0:T(8,128)(2,1)}, bf16[48,2560]{1,0:T(8,128)(2,1)S(1)}, u32[]{:S(2)}, u32[]{:S(2)}) collective-permute-start(bf16[48,2560]{1,0:T(8,128)(2,1)} %slice.484), channel_id=1, source_target_pairs={{0,8},{1,9},{2,10},{3,11},{4,12},{5,13},{6,14},{7,15},{16,24},{17,... | collective-permute-start | bytes 737288 | tf_op jit(solution)/shard_map/ppermute | solution.py:323
  526.9 77.9 %collective-permute-start.26 = (bf16[2048,1024]{1,0:T(8,128)(2,1)}, bf16[2048,1024]{1,0:T(8,128)(2,1)}, u32[]{:S(2)}, u32[]{:S(2)}) collective-permute-start(bf16[2048,1024]{1,0:T(8,128)(2,1)} %convolution_convert_fusion.10), channel_id=1, source_target_pairs={{0,16},{16,0},{1,17},{17,1},{2,18},{18,2},{3,19},{19,3},{4,20},{20... | collective-permute-start | bytes 12582920 | tf_op jit(solution)/shard_map/ppermute | solution.py:292
  532.5 72.3 %collective-permute-start.25 = (bf16[512,4096]{1,0:T(8,128)(2,1)}, bf16[512,4096]{1,0:T(8,128)(2,1)}, u32[]{:S(2)}, u32[]{:S(2)}) collective-permute-start(bf16[512,4096]{1,0:T(8,128)(2,1)} %convolution_convert_fusion.9), channel_id=1, source_target_pairs={{0,16},{16,0},{1,17},{17,1},{2,18},{18,2},{3,19},{19,3},{4,20},{20... | collective-permute-start | bytes 12582920 | tf_op jit(solution)/shard_map/ppermute | solution.py:292
  537.4 67.4 %collective-permute-start.27 = (bf16[512,4096]{1,0:T(8,128)(2,1)}, bf16[512,4096]{1,0:T(8,128)(2,1)}, u32[]{:S(2)}, u32[]{:S(2)}) collective-permute-start(bf16[512,4096]{1,0:T(8,128)(2,1)} %dynamic-slice_bitcast_fusion), channel_id=1, source_target_pairs={{8,24},{24,8},{9,25},{25,9},{10,26},{26,10},{11,27},{27,11},{12,28... | collective-permute-start | bytes 12582920 | tf_op jit(solution)/shard_map/ppermute | solution.py:292
  541.3 9.2 %collective-permute-start.48 = (bf16[257,768]{1,0:T(8,128)(2,1)S(1)}, bf16[257,768]{1,0:T(8,128)(2,1)S(1)}, u32[]{:S(2)}, u32[]{:S(2)}) collective-permute-start(bf16[257,768]{1,0:T(8,128)(2,1)S(1)} %pad_maximum_fusion.14), channel_id=1, source_target_pairs={{0,0},{16,8},{1,1},{17,9},{2,2},{18,10},{3,3},{19,11},{4,4},{20,12... | collective-permute-start | bytes 1184264 | tf_op jit(solution)/shard_map/ppermute | solution.py:292
  556.7 48.1 %collective-permute-start.28 = (bf16[512,1024]{1,0:T(8,128)(2,1)}, bf16[512,1024]{1,0:T(8,128)(2,1)}, u32[]{:S(2)}, u32[]{:S(2)}) collective-permute-start(bf16[512,1024]{1,0:T(8,128)(2,1)} %get-tuple-element.400), channel_id=1, source_target_pairs={{0,0},{16,8},{8,16},{24,24},{1,1},{17,9},{9,17},{25,25},{2,2},{18,... | collective-permute-start | bytes 3145736 | tf_op jit(solution)/shard_map/ppermute | solution.py:292
  612.7 46.7 %collective-permute-start.30 = (bf16[1,2,2,256,1024]{4,3,2,1,0:T(8,128)(2,1)}, bf16[1,2,2,256,1024]{4,3,2,1,0:T(8,128)(2,1)}, u32[]{:S(2)}, u32[]{:S(2)}) collective-permute-start(bf16[1,2,2,256,1024]{4,3,2,1,0:T(8,128)(2,1)} %constant_dynamic-slice_fusion.20), channel_id=1, source_target_pairs={{0,4},{1,5},{2,6},{3,7},{4,0},{5,1},{6,2},{7,3},{8,12},{9,13},{10,... | collective-permute-start | bytes 6291464 | tf_op jit(solution)/shard_map/ppermute | solution.py:344
  621.0 42.6 %collective-permute-start.31 = (bf16[2,2,2,1,32,4096]{5,4,3,2,1,0:T(8,128)(2,1)}, bf16[2,2,2,1,32,4096]{5,4,3,2,1,0:T(8,128)(2,1)}, u32[]{:S(2)}, u32[]{:S(2)}) collective-permute-start(bf16[2,2,2,1,32,4096]{5,4,3,2,1,0:T(8,128)(2,1)} %constant_dynamic-slice_fusion.19), channel_id=1, source_target_pairs={{8,9},{9,8},{10,11},{11,10},{12,13},{13,12},{14,15},{15,14},{24,25... | collective-permute-start | bytes 6291464 | tf_op jit(solution)/shard_map/ppermute | solution.py:344
  630.3 37.1 %collective-permute-start.29 = (bf16[2,1,2,64,4096]{4,3,2,1,0:T(8,128)(2,1)}, bf16[2,1,2,64,4096]{4,3,2,1,0:T(8,128)(2,1)}, u32[]{:S(2)}, u32[]{:S(2)}) collective-permute-start(bf16[2,1,2,64,4096]{4,3,2,1,0:T(8,128)(2,1)} %constant_dynamic-slice_fusion.21), channel_id=1, source_target_pairs={{0,2},{1,3},{2,0},{3,1},{4,6},{5,7},{6,4},{7,5},{8,10},{9,11},{10,... | collective-permute-start | bytes 6291464 | tf_op jit(solution)/shard_map/ppermute | solution.py:344
  635.9 128.4 %collective-permute-start.37 = (bf16[512,1024]{1,0:T(8,128)(2,1)}, bf16[512,1024]{1,0:T(8,128)(2,1)}, u32[]{:S(2)}, u32[]{:S(2)}) collective-permute-start(bf16[512,1024]{1,0:T(8,128)(2,1)} %convolution_convert_fusion.14), channel_id=1, source_target_pairs={{0,16},{16,0},{1,17},{17,1},{2,18},{18,2},{3,19},{19,3},{4,20},{20... | collective-permute-start | bytes 3145736 | tf_op jit(solution)/shard_map/ppermute | solution.py:292
  718.7 18.5 %collective-permute-start.38 = (f32[8,1665]{1,0:T(8,128)S(1)}, f32[8,1665]{1,0:T(8,128)}, u32[]{:S(2)}, u32[]{:S(2)}) collective-permute-start(f32[8,1665]{1,0:T(8,128)S(1)} %dynamic-slice_bitcast_fusion.1), channel_id=1, source_target_pairs={{0,16},{16,0},{1,17},{17,1},{2,18},{18,2},{3,19},{19,3},{4,20},{20... | collective-permute-start | bytes 159848 | tf_op jit(solution)/shard_map/ppermute | solution.py:292
  727.2 37.1 %collective-permute-start.35 = (bf16[512,1536]{1,0:T(8,128)(2,1)}, bf16[512,1536]{1,0:T(8,128)(2,1)}, u32[]{:S(2)}, u32[]{:S(2)}) collective-permute-start(bf16[512,1536]{1,0:T(8,128)(2,1)} %convolution_convert_fusion.12), channel_id=1, source_target_pairs={{0,16},{16,0},{1,17},{17,1},{2,18},{18,2},{3,19},{19,3},{4,20},{20... | collective-permute-start | bytes 4718600 | tf_op jit(solution)/shard_map/ppermute | solution.py:292
  727.3 37.0 %collective-permute-start.36 = (bf16[512,1536]{1,0:T(8,128)(2,1)}, bf16[512,1536]{1,0:T(8,128)(2,1)}, u32[]{:S(2)}, u32[]{:S(2)}) collective-permute-start(bf16[512,1536]{1,0:T(8,128)(2,1)} %convolution_convert_fusion.11), channel_id=1, source_target_pairs={{0,16},{16,0},{1,17},{17,1},{2,18},{18,2},{3,19},{19,3},{4,20},{20... | collective-permute-start | bytes 4718600 | tf_op jit(solution)/shard_map/ppermute | solution.py:292
  728.8 10.5 %collective-permute-start.34 = (bf16[2,2,1,1,32,4096]{5,4,3,2,1,0:T(8,128)(2,1)}, bf16[2,2,1,1,32,4096]{5,4,3,2,1,0:T(8,128)(2,1)}, u32[]{:S(2)}, u32[]{:S(2)}) collective-permute-start(bf16[2,2,1,1,32,4096]{5,4,3,2,1,0:T(8,128)(2,1)} %constant_dynamic-slice_fusion.16), channel_id=1, source_target_pairs={{8,10},{9,11},{10,8},{11,9},{12,14},{13,15},{14,12},{15,13},{24,26... | collective-permute-start | bytes 3145736 | tf_op jit(solution)/shard_map/ppermute | solution.py:344
  737.2 25.1 %collective-permute-start.33 = (bf16[1,2,1,256,1024]{4,3,2,1,0:T(8,128)(2,1)}, bf16[1,2,1,256,1024]{4,3,2,1,0:T(8,128)(2,1)}, u32[]{:S(2)}, u32[]{:S(2)}) collective-permute-start(bf16[1,2,1,256,1024]{4,3,2,1,0:T(8,128)(2,1)} %constant_dynamic-slice_fusion.17), channel_id=1, source_target_pairs={{0,1},{1,0},{2,3},{3,2},{4,5},{5,4},{6,7},{7,6},{8,9},{9,8},{10,11... | collective-permute-start | bytes 3145736 | tf_op jit(solution)/shard_map/ppermute | solution.py:344
  739.3 24.7 %collective-permute-start.32 = (bf16[1,1,2,64,4096]{4,3,2,1,0:T(8,128)(2,1)}, bf16[1,1,2,64,4096]{4,3,2,1,0:T(8,128)(2,1)S(1)}, u32[]{:S(2)}, u32[]{:S(2)}) collective-permute-start(bf16[1,1,2,64,4096]{4,3,2,1,0:T(8,128)(2,1)} %constant_dynamic-slice_fusion.18), channel_id=1, source_target_pairs={{0,4},{1,5},{2,6},{3,7},{4,0},{5,1},{6,2},{7,3},{8,12},{9,13},{10,... | collective-permute-start | bytes 3145736 | tf_op jit(solution)/shard_map/ppermute | solution.py:344
  764.4 12.7 %collective-permute-start.46 = (bf16[2,1,1,1,32,4096]{5,4,3,2,1,0:T(8,128)(2,1)S(1)}, bf16[2,1,1,1,32,4096]{5,4,3,2,1,0:T(8,128)(2,1)S(1)}, u32[]{:S(2)}, u32[]{:S(2)}) collective-permute-start(bf16[2,1,1,1,32,4096]{5,4,3,2,1,0:T(8,128)(2,1)S(1)} %constant_dynamic-slice_fusion.9), channel_id=1, source_target_pairs={{8,12},{9,13},{10,14},{11,15},{12,8},{13,9},{14,10},{15,11},{24,28... | collective-permute-start | bytes 1572872 | tf_op jit(solution)/shard_map/ppermute | solution.py:344
  765.3 10.5 %collective-permute-start.45 = (f32[2,2,1,1,1665]{4,2,1,0,3:T(1,128)S(1)}, f32[2,2,1,1,1665]{4,2,1,0,3:T(1,128)S(1)}, u32[]{:S(2)}, u32[]{:S(2)}) collective-permute-start(f32[2,2,1,1,1665]{4,2,1,0,3:T(1,128)S(1)} %constant_dynamic-slice_fusion.10), channel_id=1, source_target_pairs={{0,1},{1,0},{2,3},{3,2},{4,5},{5,4},{6,7},{7,6},{8,9},{9,8},{10,11... | collective-permute-start | bytes 79928 | tf_op jit(solution)/shard_map/ppermute | solution.py:344
  766.5 38.2 %collective-permute-start.43 = (bf16[1,1,1,256,1024]{4,3,2,1,0:T(8,128)(2,1)S(1)}, bf16[1,1,1,256,1024]{4,3,2,1,0:T(8,128)(2,1)S(1)}, u32[]{:S(2)}, u32[]{:S(2)}) collective-permute-start(bf16[1,1,1,256,1024]{4,3,2,1,0:T(8,128)(2,1)S(1)} %constant_dynamic-slice_fusion.11), channel_id=1, source_target_pairs={{0,2},{1,3},{2,0},{3,1},{4,6},{5,7},{6,4},{7,5},{8,10},{9,11},{10,... | collective-permute-start | bytes 1572872 | tf_op jit(solution)/shard_map/ppermute | solution.py:344
  766.8 12.7 %collective-permute-start.42 = (bf16[1,1,1,64,4096]{4,3,2,1,0:T(8,128)(2,1)S(1)}, bf16[1,1,1,64,4096]{4,3,2,1,0:T(8,128)(2,1)S(1)}, u32[]{:S(2)}, u32[]{:S(2)}) collective-permute-start(bf16[1,1,1,64,4096]{4,3,2,1,0:T(8,128)(2,1)S(1)} %constant_dynamic-slice_fusion.12), channel_id=1, source_target_pairs={{0,1},{1,0},{2,3},{3,2},{4,5},{5,4},{6,7},{7,6},{8,9},{9,8},{10,11... | collective-permute-start | bytes 1572872 | tf_op jit(solution)/shard_map/ppermute | solution.py:344
  768.9 36.0 %collective-permute-start.41 = (bf16[1,2,2,64,1024]{4,3,2,1,0:T(8,128)(2,1)S(1)}, bf16[1,2,2,64,1024]{4,3,2,1,0:T(8,128)(2,1)S(1)}, u32[]{:S(2)}, u32[]{:S(2)}) collective-permute-start(bf16[1,2,2,64,1024]{4,3,2,1,0:T(8,128)(2,1)S(1)} %constant_dynamic-slice_fusion.13), channel_id=1, source_target_pairs={{0,4},{1,5},{2,6},{3,7},{4,0},{5,1},{6,2},{7,3},{8,12},{9,13},{10,... | collective-permute-start | bytes 1572872 | tf_op jit(solution)/shard_map/ppermute | solution.py:344
  775.8 29.3 %collective-permute-start.40 = (bf16[2,1,2,64,1536]{4,3,2,1,0:T(8,128)(2,1)S(1)}, bf16[2,1,2,64,1536]{4,3,2,1,0:T(8,128)(2,1)S(1)}, u32[]{:S(2)}, u32[]{:S(2)}) collective-permute-start(bf16[2,1,2,64,1536]{4,3,2,1,0:T(8,128)(2,1)S(1)} %constant_dynamic-slice_fusion.14), channel_id=1, source_target_pairs={{0,2},{1,3},{2,0},{3,1},{4,6},{5,7},{6,4},{7,5},{8,10},{9,11},{10,... | collective-permute-start | bytes 2359304 | tf_op jit(solution)/shard_map/ppermute | solution.py:344
  777.1 28.2 %collective-permute-start.39 = (bf16[2,2,1,64,1536]{4,3,2,1,0:T(8,128)(2,1)S(1)}, bf16[2,2,1,64,1536]{4,3,2,1,0:T(8,128)(2,1)S(1)}, u32[]{:S(2)}, u32[]{:S(2)}) collective-permute-start(bf16[2,2,1,64,1536]{4,3,2,1,0:T(8,128)(2,1)S(1)} %constant_dynamic-slice_fusion.15), channel_id=1, source_target_pairs={{0,1},{1,0},{2,3},{3,2},{4,5},{5,4},{6,7},{7,6},{8,9},{9,8},{10,11... | collective-permute-start | bytes 2359304 | tf_op jit(solution)/shard_map/ppermute | solution.py:344
  779.5 48.8 %collective-permute-start.44 = (bf16[512,1024]{1,0:T(8,128)(2,1)S(1)}, bf16[512,1024]{1,0:T(8,128)(2,1)S(1)}, u32[]{:S(2)}, u32[]{:S(2)}) collective-permute-start(bf16[512,1024]{1,0:T(8,128)(2,1)S(1)} %copy-done.157), channel_id=1, source_target_pairs={{0,0},{16,8},{8,16},{24,24},{1,1},{17,9},{9,17},{25,25},{2,2},{18,... | collective-permute-start | bytes 3145736 | tf_op jit(solution)/shard_map/ppermute | solution.py:292
  828.3 13.7 %collective-permute-start.62 = (bf16[32,4096]{1,0:T(8,128)(2,1)S(1)}, bf16[32,4096]{1,0:T(8,128)(2,1)S(1)}, u32[]{:S(2)}, u32[]{:S(2)}) collective-permute-start(bf16[32,4096]{1,0:T(8,128)(2,1)S(1)} %slice_bitcast_fusion.2), channel_id=1, source_target_pairs={{8,0},{9,1},{10,2},{11,3},{12,4},{13,5},{14,6},{15,7},{24,16},{25,... | collective-permute-start | bytes 786440 | tf_op jit(solution)/shard_map/ppermute | solution.py:326
  829.6 5.6 collective-permute-start.53
  830.5 14.9 %collective-permute-start.52 = (bf16[1,2,1,64,1024]{4,3,2,1,0:T(8,128)(2,1)S(1)}, bf16[1,2,1,64,1024]{4,3,2,1,0:T(8,128)(2,1)S(1)}, u32[]{:S(2)}, u32[]{:S(2)}) collective-permute-start(bf16[1,2,1,64,1024]{4,3,2,1,0:T(8,128)(2,1)S(1)} %constant_dynamic-slice_fusion.6), channel_id=1, source_target_pairs={{0,1},{1,0},{2,3},{3,2},{4,5},{5,4},{6,7},{7,6},{8,9},{9,8},{10,11... | collective-permute-start | bytes 786440 | tf_op jit(solution)/shard_map/ppermute | solution.py:344
  832.6 12.9 %collective-permute-start.51 = (bf16[1,1,2,64,1536]{4,3,2,1,0:T(8,128)(2,1)S(1)}, bf16[1,1,2,64,1536]{4,3,2,1,0:T(8,128)(2,1)S(1)}, u32[]{:S(2)}, u32[]{:S(2)}) collective-permute-start(bf16[1,1,2,64,1536]{4,3,2,1,0:T(8,128)(2,1)S(1)} %constant_dynamic-slice_fusion.7), channel_id=1, source_target_pairs={{0,4},{1,5},{2,6},{3,7},{4,0},{5,1},{6,2},{7,3},{8,12},{9,13},{10,... | collective-permute-start | bytes 1179656 | tf_op jit(solution)/shard_map/ppermute | solution.py:344
  833.5 12.1 %collective-permute-start.50 = (bf16[2,1,1,64,1536]{4,3,2,1,0:T(8,128)(2,1)S(1)}, bf16[2,1,1,64,1536]{4,3,2,1,0:T(8,128)(2,1)S(1)}, u32[]{:S(2)}, u32[]{:S(2)}) collective-permute-start(bf16[2,1,1,64,1536]{4,3,2,1,0:T(8,128)(2,1)S(1)} %constant_dynamic-slice_fusion.8), channel_id=1, source_target_pairs={{0,2},{1,3},{2,0},{3,1},{4,6},{5,7},{6,4},{7,5},{8,10},{9,11},{10,... | collective-permute-start | bytes 1179656 | tf_op jit(solution)/shard_map/ppermute | solution.py:344
  835.2 55.3 %collective-permute-start.61 = (bf16[256,1024]{1,0:T(8,128)(2,1)S(1)}, bf16[256,1024]{1,0:T(8,128)(2,1)S(1)}, u32[]{:S(2)}, u32[]{:S(2)}) collective-permute-start(bf16[256,1024]{1,0:T(8,128)(2,1)S(1)} %bitcast.275), channel_id=1, source_target_pairs={{0,0},{16,8},{8,16},{24,24},{1,1},{17,9},{9,17},{25,25},{2,2},{18,... | collective-permute-start | bytes 1572872 | tf_op jit(solution)/shard_map/ppermute | solution.py:292
  842.0 47.5 %collective-permute-start.47 = (bf16[64,4096]{1,0:T(8,128)(2,1)S(1)}, bf16[64,4096]{1,0:T(8,128)(2,1)S(1)}, u32[]{:S(2)}, u32[]{:S(2)}) collective-permute-start(bf16[64,4096]{1,0:T(8,128)(2,1)S(1)} %bitcast.274), channel_id=1, source_target_pairs={{0,0},{16,8},{8,16},{24,24},{1,1},{17,9},{9,17},{25,25},{2,2},{18,... | collective-permute-start | bytes 1572872 | tf_op jit(solution)/shard_map/ppermute | solution.py:292
  845.7 39.2 %collective-permute-start.56 = (bf16[1,1,1,64,1536]{4,3,2,1,0:T(8,128)(2,1)S(1)}, bf16[1,1,1,64,1536]{4,3,2,1,0:T(8,128)(2,1)}, u32[]{:S(2)}, u32[]{:S(2)}) collective-permute-start(bf16[1,1,1,64,1536]{4,3,2,1,0:T(8,128)(2,1)S(1)} %constant_dynamic-slice_fusion.2), channel_id=1, source_target_pairs={{0,4},{1,5},{2,6},{3,7},{4,0},{5,1},{6,2},{7,3},{8,12},{9,13},{10,... | collective-permute-start | bytes 589832 | tf_op jit(solution)/shard_map/ppermute | solution.py:344
  845.8 40.1 %collective-permute-start.57 = (bf16[1,1,1,64,1536]{4,3,2,1,0:T(8,128)(2,1)S(1)}, bf16[1,1,1,64,1536]{4,3,2,1,0:T(8,128)(2,1)}, u32[]{:S(2)}, u32[]{:S(2)}) collective-permute-start(bf16[1,1,1,64,1536]{4,3,2,1,0:T(8,128)(2,1)S(1)} %constant_dynamic-slice_fusion.1), channel_id=1, source_target_pairs={{0,1},{1,0},{2,3},{3,2},{4,5},{5,4},{6,7},{7,6},{8,9},{9,8},{10,11... | collective-permute-start | bytes 589832 | tf_op jit(solution)/shard_map/ppermute | solution.py:344
  847.7 9.7 %collective-permute-start.54 = (f32[1,1,1,1,1665]{4,2,1,0,3:T(1,128)S(1)}, f32[1,1,1,1,1665]{4,2,1,0,3:T(1,128)S(1)}, u32[]{:S(2)}, u32[]{:S(2)}) collective-permute-start(f32[1,1,1,1,1665]{4,2,1,0,3:T(1,128)S(1)} %constant_dynamic-slice_fusion.3), channel_id=1, source_target_pairs={{0,4},{1,5},{2,6},{3,7},{4,0},{5,1},{6,2},{7,3},{8,12},{9,13},{10,... | collective-permute-start | bytes 19988 | tf_op jit(solution)/shard_map/ppermute | solution.py:344
  865.1 14.2 %collective-permute-start.60 = (f32[768]{0:T(1024)S(1)}, f32[768]{0:T(1024)S(1)}, u32[]{:S(2)}, u32[]{:S(2)}) collective-permute-start(f32[768]{0:T(1024)S(1)} %slice_reduce_fusion.4), channel_id=1, source_target_pairs={{0,0},{16,8},{8,16},{24,24},{1,1},{17,9},{9,17},{25,25},{2,2},{18,... | collective-permute-start | bytes 9224 | tf_op jit(solution)/shard_map/ppermute | solution.py:292
  879.2 4.8 collective-permute-start.58
  887.0 16.0 %collective-permute-start.59 = (bf16[64,4096]{1,0:T(8,128)(2,1)S(1)}, bf16[64,4096]{1,0:T(8,128)(2,1)S(1)}, u32[]{:S(2)}, u32[]{:S(2)}) collective-permute-start(bf16[64,4096]{1,0:T(8,128)(2,1)S(1)} %pad_maximum_fusion.13), channel_id=1, source_target_pairs={{0,0},{16,8},{8,16},{24,24},{1,1},{17,9},{9,17},{25,25},{2,2},{18,... | collective-permute-start | bytes 1572872 | tf_op jit(solution)/shard_map/ppermute | solution.py:292
  (136 other events, 1764.4 us)
Sparse Core Ops, SparseCore 0:
  86.9 91.4 all-gather.3
  209.7 103.6 all-gather.5
  496.8 103.7 all-gather.7

commit v2 on v1

--- a/solution.py
+++ b/solution.py
@@ -266,8 +266,7 @@
         for p in (grad_scores, chances_bf)
     ]
     seen = jnp.concatenate(seen, axis=2).astype(BF).reshape(-1, 2 * width)
-    flat = jnp.concatenate(factors, axis=1).reshape(seen.shape[0], -1)
-    mats = jnp.concatenate([seen, flat], axis=1)
+    mats = (jnp.concatenate(factors, axis=1), seen)
     smalls = (
         jnp.concatenate([colsum(grad_q), colsum(grad_kv[:, width:])]),
         colsum(grad_one_bf),
@@ -310,6 +309,13 @@
         pairs = []
         for i in range(h):
             pairs += [(i, i), (n + i, i + h)]
+        return self.all_pairs(value, pairs)
+
+    def home_dec(self, value):
+        n, h = self.n, self.half
+        pairs = []
+        for i in range(h):
+            pairs += [(n + i + h, n + i + h), (i + h, n + i)]
         return self.all_pairs(value, pairs)
 
     def push_dec(self, value):
@@ -372,6 +378,21 @@
         own = mm_lt(self.half_of(left, self.core), right) + got.astype(F32)
         shard = left.shape[1] // self.n
         return own.astype(BF).reshape((2,) * self.bits + (shard, right.shape[1]))
+
+    def reduce_steps(self, jobs):
+        keeps, gots = [], []
+        for value, turn, step, who, lead in jobs:
+            bit = self.order(turn)[step]
+            mine = (self.dp >> bit) & 1
+            axis = lead + self.bits - 1 - bit
+            send = lax.dynamic_slice_in_dim(value, 1 - mine, 1, axis)
+            keeps.append(lax.dynamic_slice_in_dim(value, mine, 1, axis))
+            gots.append(self.hop(send, bit, who))
+        gots = lax.optimization_barrier(tuple(gots))
+        return [
+            (keep.astype(F32) + got.astype(F32)).astype(keep.dtype)
+            for keep, got in zip(keeps, gots)
+        ]
 
     def reduce_step(self, value, turn, step, who="both", lead=0):
         bit = self.order(turn)[step]
@@ -553,8 +574,7 @@
     labels = held[0][:, joint_w + width :].reshape(1, -1)[:, n_role : n_role + total]
     labels = labels.astype(jnp.int32).reshape(micro, rows)
     held = [v[None] for v in held]
-    tokens_in, held = stage(token_vectors[0].reshape(total, width), held)
-    stream_bf = links.swap(tokens_in)
+    tokens_in = token_vectors[0].reshape(total, width)
     adjoint_own = generation_result_adjoint.reshape(total, width)
     query_in = jnp.concatenate(
         [retriever_triple_map, retriever_mixing_result_map, retriever_widen_map]
@@ -589,26 +609,20 @@
     )
     q_own = inquiry_vectors.reshape(-1, q_width)
     last = links.bits - 1
+    cross_full = lax.all_gather(cross_in, everyone, axis=0, tiled=True)
     for step in range(last):
         held = [
             jnp.concatenate([v, links.gather_hop(v, turn, step)], axis=0)
             for turn, v in enumerate(held)
         ]
         if step == 0:
-            held, stream_bf, adjoint_own, cross_in, doc_own, q_own = stage(
-                held, stream_bf, adjoint_own, cross_in, doc_own, q_own
-            )
-            cross_full = lax.all_gather(cross_in, everyone, axis=0, tiled=True)
+            (held,) = stage(held)
         else:
-            (held,) = stage(held)
+            held, cross_full = stage(held, cross_full)
     recv = [links.gather_hop(v, turn, last) for turn, v in enumerate(held)]
     theirs = [links.flip(v) for v in held]
-    adjoint_bf = links.push_dec(adjoint_own)
-    doc_packet = links.pull_enc(doc_own)
-    q_block_rows = links.pull_enc(q_own)
-    recv, theirs, adjoint_bf, query_in, doc_packet, q_block_rows = stage(
-        recv, theirs, adjoint_bf, query_in, doc_packet, q_block_rows
-    )
+    recv, theirs, query_in, tokens_in = stage(recv, theirs, query_in, tokens_in)
+    stream_bf = links.swap(tokens_in)
     query_full = lax.all_gather(query_in, everyone, axis=0, tiled=True)
     got = [links.flip(v) for v in recv]
     w_joint, w_out, w_small, w_up, w_down = weave(
@@ -625,9 +639,16 @@
     bias_joint = jnp.concatenate([b_joint[:width], jnp.zeros((width,), F32), b_joint[width:]])
     joint = (mm(stream_bf, w_joint) + bias_joint).astype(BF)
     self_off = (0, width, 2 * width)
+    joint, adjoint_own, doc_own, q_own = stage(joint, adjoint_own, doc_own, q_own)
+    adjoint_bf = links.push_dec(adjoint_own)
+    doc_packet = links.pull_enc(doc_own)
+    q_block_rows = links.pull_enc(q_own)
     mixed = attend(joint, joint, joint, self_off, width, labels, causal)
     first, kept_one = norm_fwd(stream + mm(mixed, w_out) + b_out, gains[0], shifts[0], EPS_MODEL)
     first_bf = first.astype(BF)
+    first, first_bf, kept_one, adjoint_bf, doc_packet, q_block_rows = stage(
+        first, first_bf, kept_one, adjoint_bf, doc_packet, q_block_rows
+    )
 
     def feed(stream_one, stream_one_bf):
         active, slope = gelu_pair(mm(stream_one_bf, w_up) + b_up)
@@ -709,7 +730,9 @@
     (
         layer_rows, grad_memory, feed_in, active, dec_f, dec_h, dec_norm, cross_small_grads, cross_kept
     ) = dec
-    grad_memory, cross_kept, query_full = stage(grad_memory, cross_kept, query_full)
+    grad_memory, cross_kept, query_full, layer_rows = stage(
+        grad_memory, cross_kept, query_full, layer_rows
+    )
 
     passages = document_vectors.shape[1]
     n_span, n_pick = micro * asked, micro * asked * chosen_count
@@ -741,6 +764,18 @@
 
     queried = when(is_enc, query_branch)
     memory_grad = links.to_enc(grad_memory)
+    queried, layer_rows = stage(queried, layer_rows)
+    factors_got = [links.to_dec(g[g.shape[0] // 2 :]) for g in queried[3]]
+    enc_home = links.home_enc(layer_rows)
+    memory_grad, queried, cross_kept, factors_got, enc_home, layer_rows = stage(
+        memory_grad, queried, cross_kept, factors_got, enc_home, layer_rows
+    )
+    factors = [
+        lax.all_gather(
+            jnp.where(is_enc, g[: g.shape[0] // 2], got), everyone, axis=0, tiled=True
+        )
+        for g, got in zip(queried[3], factors_got)
+    ]
 
     def cross_late():
         grad_cross, grad_cross_bf, cmixed, grad_cq, grad_ckv = cross_kept
@@ -760,14 +795,6 @@
         cross_late,
     )
     scored, q_grad_rows, grad_heat, query_grads, query_small_grads = queried
-    half_rows = query_grads.shape[0] // 2
-    factors_got = links.to_dec(query_grads[half_rows:])
-    memory_grad, cross_grads, dec_first, query_grads, factors_got = stage(
-        memory_grad, cross_grads, dec_first, query_grads, factors_got
-    )
-    factors = lax.all_gather(
-        jnp.where(is_enc, query_grads[:half_rows], factors_got), everyone, axis=0, tiled=True
-    )
 
     def enc_back():
         grad_f, grad_h, grad_first, gain_two, shift_two = feed_back(
@@ -780,7 +807,7 @@
     )
 
     grad_h, grad_f, grad_first, layer_rows = stage(grad_h, grad_f, grad_first, layer_rows)
-    layer_home = links.swap(layer_rows)
+    dec_home = links.home_dec(layer_rows)
     up_got = links.reduce_open(feed_in, grad_h)
     down_got = links.reduce_open(active, grad_f)
     cross_pair = cross_grads.reshape(2, width // 2, 4 * width)
@@ -790,66 +817,33 @@
     grad_one, gain_one, shift_one = norm_bwd(grad_first, kept_one, gains[0])
     grad_one_bf = grad_one.astype(BF)
     grad_mixed = mm_rt(grad_one_bf, w_out).astype(BF)
-    up_got, down_got, cross_got, grad_mixed, layer_home = stage(
-        up_got, down_got, cross_got, grad_mixed, layer_home
+    up_got, down_got, cross_got, grad_mixed, dec_home = stage(
+        up_got, down_got, cross_got, grad_mixed, dec_home
     )
     cross_sum = lax.dynamic_index_in_dim(cross_pair, core, 0, keepdims=False)
     cross_sum = (cross_sum.astype(F32) + cross_got.astype(F32)).astype(BF)
     cross_sum = cross_sum.reshape((2,) + (2,) * links.bits + (cross_rows, 4 * width))
-    cross_sum = links.reduce_step(cross_sum, 0, 0, "dec", 1)
-    up_sum = links.reduce_step(links.reduce_own(feed_in, grad_h, up_got), 1, 0)
-    down_sum = links.reduce_step(links.reduce_own(active, grad_f, down_got), 2, 0)
+    up_sum = links.reduce_own(feed_in, grad_h, up_got)
+    down_sum = links.reduce_own(active, grad_f, down_got)
+
+    def feed_steps(step):
+        return [
+            (up_sum, 1, step, "both", 0),
+            (down_sum, 2, step, "both", 0),
+            (cross_sum, 0, step, "dec", 1),
+        ]
+
+    up_sum, down_sum, cross_sum = links.reduce_steps(feed_steps(0))
     grad_joint = attend_back(
         joint, joint, joint, self_off, width, labels, causal, grad_mixed, True
     )
-    up_sum, down_sum, cross_sum, grad_joint, factors = stage(
-        up_sum, down_sum, cross_sum, grad_joint, factors
-    )
-    device = core * n + links.dp
-
-    def own_columns(matrix, count):
-        wide = matrix.shape[1]
-        lines = lax.broadcasted_iota(jnp.int32, (wide, count), 0)
-        places = lax.broadcasted_iota(jnp.int32, (wide, count), 1) + device * count
-        return mm(matrix, (lines == places).astype(BF)).astype(BF)
-
-    all_asked = 2 * n * asked
-    seen_keys = own_columns(factors[:, :q_width], q_rows).reshape(all_asked, QHEADS, q_rows)
-    seen_values = own_columns(factors[:, q_width : 2 * q_width], q_rows)
-    seen_values = seen_values.reshape(all_asked, QHEADS, q_rows)
-    factors = factors[:, 2 * q_width :].reshape(all_asked, -1)
-    sizes, at, cols = [q_width] * 5 + [q_ff, q_ff] + [q_width] * 3, 0, []
-    for size in sizes:
-        cols.append(factors[:, at : at + size])
-        at += size
-    f_head, f_q, f_mixed, f_one, f_middle, f_hidden, f_active, f_two, f_asks, f_gmix = cols
-
-    def by_head(seen, other, scale):
-        per_head = jnp.einsum(
-            "qhd,qhe->hde", seen, heads_of(other, QHEADS), preferred_element_type=F32
-        )
-        return per_head.transpose(1, 0, 2).reshape(q_rows, q_width) * scale
-
-    query_k_own = by_head(seen_keys, f_asks, (q_width // QHEADS) ** (-0.5))
-    query_v_own = by_head(seen_values, f_gmix, 1.0)
-    query_q_own = mm_lt(own_columns(f_head, q_rows), f_q)
-    query_out_own = mm_lt(own_columns(f_mixed, q_rows), f_one)
-    query_up_own = mm_lt(own_columns(f_middle, q_rows), f_hidden)
-    query_down_own = mm_lt(own_columns(f_active, q_rows * q_folds), f_two)
-    cross_sum = links.reduce_step(cross_sum, 0, 1, "dec", 1)
+    up_sum, down_sum, cross_sum, grad_joint = stage(up_sum, down_sum, cross_sum, grad_joint)
     split_joint = [(0, joint_w // 2), (joint_w // 2, joint_w)]
     attn_jobs = [(stream_bf, grad_joint[:, a:b]) for a, b in split_joint]
     attn_jobs += [(mixed, grad_one_bf)]
     attn_got = [links.reduce_open(left, right) for left, right in attn_jobs]
     grad_rows = (grad_one + mm_rt(grad_joint, w_joint)).astype(BF)
-    query_own_mats = [
-        jnp.concatenate([query_q_own, query_k_own, query_v_own], axis=1),
-        query_out_own,
-        query_up_own,
-        query_down_own,
-    ]
-    up_sum = links.reduce_step(up_sum, 1, 1)
-    down_sum = links.reduce_step(down_sum, 2, 1)
+    up_sum, down_sum, cross_sum = links.reduce_steps(feed_steps(1))
 
     def role_rows(vec):
         return vec.reshape(n, -1)
@@ -904,8 +898,11 @@
         for turn, ((left, right), got) in enumerate(zip(attn_jobs, attn_got))
     ]
     small_sum = links.reduce_step(small_sum, 0, 0)
-    attn_sum, up_sum, down_sum, rows_home, small_sum, cross_sum, query_own_mats = stage(
-        attn_sum, up_sum, down_sum, rows_home, small_sum, cross_sum, query_own_mats
+    per_block = inquiry_vectors.shape[1]
+    score_row = jnp.pad(scored.reshape(1, -1), ((0, 0), (0, q_width - scored.size))).astype(BF)
+    q_packet = jnp.concatenate([q_grad_rows.astype(BF), score_row])
+    attn_sum, up_sum, down_sum, rows_home, small_sum, cross_sum, factors, q_packet = stage(
+        attn_sum, up_sum, down_sum, rows_home, small_sum, cross_sum, factors, q_packet
     )
     up_own = links.swap(up_sum.reshape(-1, ff)).astype(F32)
     down_own = links.swap(down_sum.reshape(-1, width)).astype(F32)
@@ -913,7 +910,44 @@
         attn_sum = [links.reduce_step(v, turn, step) for turn, v in enumerate(attn_sum)]
         small_sum = links.reduce_step(small_sum, 0, step)
         if step + 1 < links.bits:
-            attn_sum, small_sum = stage(attn_sum, small_sum)
+            attn_sum, small_sum, factors = stage(attn_sum, small_sum, factors)
+    device = core * n + links.dp
+
+    def own_columns(matrix, count):
+        wide = matrix.shape[1]
+        lines = lax.broadcasted_iota(jnp.int32, (wide, count), 0)
+        places = lax.broadcasted_iota(jnp.int32, (wide, count), 1) + device * count
+        return mm(matrix, (lines == places).astype(BF)).astype(BF)
+
+    sizes, at, cols = [q_width] * 5 + [q_ff, q_ff] + [q_width] * 3, 0, []
+    for size in sizes:
+        cols.append(factors[0][:, at : at + size])
+        at += size
+    f_head, f_q, f_mixed, f_one, f_middle, f_hidden, f_active, f_two, f_asks, f_gmix = cols
+
+    table = factors[1]
+    all_asked, all_seen = factors[0].shape[0], table.shape[0]
+    lines = lax.broadcasted_iota(jnp.int32, (all_seen, all_asked), 0) // QHEADS
+    spread = (lines == lax.broadcasted_iota(jnp.int32, (all_seen, all_asked), 1)).astype(BF)
+    row_head = lax.broadcasted_iota(jnp.int32, (all_seen, q_width), 0) % QHEADS
+    col_head = lax.broadcasted_iota(jnp.int32, (all_seen, q_width), 1) // (q_width // QHEADS)
+
+    def by_head(seen, other):
+        wide = jnp.where(row_head == col_head, mm(spread, other), 0.0).astype(BF)
+        return mm_lt(own_columns(seen, q_rows), wide)
+
+    query_k_own = by_head(table[:, :q_width], f_asks) * (q_width // QHEADS) ** (-0.5)
+    query_v_own = by_head(table[:, q_width:], f_gmix)
+    query_q_own = mm_lt(own_columns(f_head, q_rows), f_q)
+    query_out_own = mm_lt(own_columns(f_mixed, q_rows), f_one)
+    query_up_own = mm_lt(own_columns(f_middle, q_rows), f_hidden)
+    query_down_own = mm_lt(own_columns(f_active, q_rows * q_folds), f_two)
+    query_own_mats = [
+        jnp.concatenate([query_q_own, query_k_own, query_v_own], axis=1),
+        query_out_own,
+        query_up_own,
+        query_down_own,
+    ]
     attn_home = jnp.concatenate([v.reshape(-1, v.shape[-1]) for v in attn_sum], axis=1)
     attn_home = links.swap(attn_home).astype(F32)
     joint_own, out_own = attn_home[:, :joint_w], attn_home[:, joint_w:]
@@ -936,13 +970,9 @@
     query_own = side_own[n_cross : n_cross + n_query]
     heat_total = side_own[-1:]
 
-    layer_out = layer_home.reshape(1, micro, rows, width)
+    layer_out = jnp.where(core == 0, enc_home, dec_home).reshape(1, micro, rows, width)
     input_grad = rows_home.astype(F32).reshape(1, micro, rows, width)
 
-    per_block = inquiry_vectors.shape[1]
-    score_row = jnp.pad(scored.reshape(1, -1), ((0, 0), (0, q_width - scored.size))).astype(BF)
-    q_packet = jnp.concatenate([q_grad_rows.astype(BF), score_row])
-    up_mark, q_packet = stage(up_own, q_packet)
     q_home = links.home_enc(q_packet)
     q_mats = q_home[: micro * per_block].reshape(micro, per_block, q_width)
     s_mats = q_home[micro * per_block :, : scored.size].reshape(micro, 1, -1)

time: 927 us -> 877 us (0.946)
  waiting for transfers between devices: 311 us -> 261 us
  local copies, waits for them, and re-layouts: 119 us -> 95.3 us
  starting transfers between devices: 167 us -> 190 us
    ppermute x27 -> x28, waiting for transfers between devices: 145 us -> 91.5 us  [all_pairs(): return lax.ppermute(value, ('phase', 'dp'), pairs)]
    ppermute x27 -> x28, starting transfers between devices: 85.4 us -> 124 us  [all_pairs(): return lax.ppermute(value, ('phase', 'dp'), pairs)]
    ppermute x2 -> x3, starting transfers between devices: 46.1 us -> 8.51 us  [to_dec(): lax.ppermute(value, 'dp', [(i, i + self.half) for i in range(self.half)])]
    ppermute x30, starting transfers between devices: 32 us -> 50 us  [hop(): lax.ppermute(value, 'dp', [(i, i ^ 1 << bit) for i in range(first, last)])]
    convert_element_type x0 -> x6, other arithmetic: none -> 17.4 us  [reduce_steps(): (keep.astype(F32) + got.astype(F32)).astype(keep.dtype)]
    reshape x7 -> x1, local copies, waits for them, and re-layouts: 19.1 us -> 4.34 us  [local(): cross_pair = cross_grads.reshape(2, width // 2, 4 * width)]
    ppermute x30, waiting for transfers between devices: 106 us -> 121 us  [hop(): lax.ppermute(value, 'dp', [(i, i ^ 1 << bit) for i in range(first, last)])]
    ppermute x2, waiting for transfers between devices: 25.4 us -> 10.9 us  [to_enc(): lax.ppermute(value, 'dp', [(i + self.half, i) for i in range(self.half)])]
  transfers between devices with their start and end apart: 66 -> 69, of which waited for: 23 -> 23; matrix products, arithmetic and copies ran while one was open for 37% -> 26% of each run, Pallas kernels for 6% -> 7%
where the time goes in v2:
time: 877 us; the launch traced here: 864 us
  waiting for transfers between devices  261 us (30%)
  starting transfers between devices  190 us (22%)
  matrix products  147 us (17%)
  local copies, waits for them, and re-layouts  95.3 us (11%)
  other arithmetic  90.3 us (10%)
  Pallas kernels  57.4 us (7%)
  between operations  16.1 us (2%)
    ppermute x28, starting transfers between devices, all_pairs(): return lax.ppermute(value, ('phase', 'dp'), pairs)  124 us
    ppermute x30, waiting for transfers between devices, hop(): lax.ppermute(value, 'dp', [(i, i ^ 1 << bit) for i in range(first, last)])  121 us
    ppermute x28, waiting for transfers between devices, all_pairs(): return lax.ppermute(value, ('phase', 'dp'), pairs)  91.5 us
    ppermute x30, starting transfers between devices, hop(): lax.ppermute(value, 'dp', [(i, i ^ 1 << bit) for i in range(first, last)])  50 us
    dot_general x15, matrix products, mm(): return jnp.dot(left, right, preferred_element_type=F32)  49.8 us
    dot_general x12, matrix products, mm_rt(): lax.dot_general(left, right, (((1,), (1,)), ((), ())), preferred_element_...  46.5 us
    dot_general x16, matrix products, mm_lt(): lax.dot_general(left, right, (((0,), (0,)), ((), ())), preferred_element_...  46.3 us
    ppermute x3, waiting for transfers between devices, to_dec(): lax.ppermute(value, 'dp', [(i, i + self.half) for i in range(self.half)])  37.4 us
  transfers between devices with their start and end apart: 69, of which 23 were waited for; matrix products, arithmetic and copies ran while one was open for 26% of the time, Pallas kernels for 7%

profile of v2, /device:TPU:1, one launch (start us, length us, event | category | flops | bytes accessed | tf_op | source)
XLA Modules:
  0.0 864.3 jit_solution(13611694731004622824)
XLA Ops:
  14.0 5.6 collective-permute-start
  21.5 4.5 collective-permute-start.2
  26.1 39.7 %collective-permute-done.1 = bf16[64,4096]{1,0:T(8,128)(2,1)S(1)} collective-permute-done((bf16[64,4096]{1,0:T(8,128)(2,1)}, bf16[64,4096]{1,0:T(8,128)(2,1)S(1)}, u32[]{:S(2)}, u32[]{:S(2)}) %collective-permute-start.1) | collective-permute-done | bytes 524320 | tf_op jit(solution)/shard_map/ppermute | solution.py:291
  65.8 6.5 collective-permute-done.2
  75.3 23.6 %collective-permute-done.5 = bf16[1,256,1024]{2,1,0:T(8,128)(2,1)S(1)} collective-permute-done((bf16[1,256,1024]{2,1,0:T(8,128)(2,1)S(1)}, bf16[1,256,1024]{2,1,0:T(8,128)(2,1)S(1)}, u32[]{:S(2)}, u32[]{:S(2)}) %collective-permute-start.5) | collective-permute-done | bytes 524320 | tf_op jit(solution)/shard_map/ppermute | solution.py:350
  100.8 12.2 %collective-permute-done.8 = bf16[2,256,1024]{2,1,0:T(8,128)(2,1)S(1)} collective-permute-done((bf16[2,256,1024]{2,1,0:T(8,128)(2,1)S(1)}, bf16[2,256,1024]{2,1,0:T(8,128)(2,1)S(1)}, u32[]{:S(2)}, u32[]{:S(2)}) %collective-permute-start.8) | collective-permute-done | bytes 1048608 | tf_op jit(solution)/shard_map/ppermute | solution.py:350
  114.5 4.1 collective-permute-done.7
  123.0 36.6 %collective-permute-done.10.refs_5_ = bf16[4,64,4096]{2,1,0:T(8,128)(2,1)S(1)} collective-permute-done((bf16[4,64,4096]{2,1,0:T(8,128)(2,1)S(1)}, bf16[4,64,4096]{2,1,0:T(8,128)(2,1)S(1)}, u32[]{:S(2)}, u32[]{:S(2)}) %collective-permute-start.10) | collective-permute-done | bytes 2097184 | tf_op jit(solution)/shard_map/ppermute | solution.py:350
  161.4 8.8 %collective-permute-done.11.refs_9_ = bf16[4,256,1024]{2,1,0:T(8,128)(2,1)} collective-permute-done((bf16[4,256,1024]{2,1,0:T(8,128)(2,1)}, bf16[4,256,1024]{2,1,0:T(8,128)(2,1)}, u32[]{:S(2)}, u32[]{:S(2)}) %collective-permute-start.11) | collective-permute-done | bytes 2097184 | tf_op jit(solution)/shard_map/ppermute | solution.py:350
  174.1 4.9 collective-permute-start.15
  181.4 22.8 %weave.1 = (bf16[1024,3072]{1,0:T(8,128)(2,1)}, bf16[1024,1024]{1,0:T(8,128)(2,1)S(1)}, bf16[1024,128]{1,0:T(8,128)(2,1)S(1)}, bf16[1024,4096]{1,0:T(8,128)(2,1)}, bf16[4096,1024]{1,0:T(8,128)(2,1)}) custom-call(s32[3,16]{1,0:T(4,128)S(1)} %pad_add_fusion.place_ref, bf16[4,64,4224]{2,1,0:T(8,128)(2,1)} %pad_maximum_fusion.6.refs_0_, ...), custom_call_target="tpu_custom_call" | custom-call | bytes 50855936 | tf_op jit(solution)/shard_map/weave/pallas_call | solution.py:442
  205.8 6.9 collective-permute-done.15
  212.6 6.5 add_convert_fusion.6.q_ref.k_ref.v_ref
  223.1 2.9 collective-permute-start.19
  228.5 13.2 %attend_fwd.3 = bf16[512,1024]{1,0:T(8,128)(2,1)S(1)} custom-call(s32[1]{0:T(128)} %bitcast.47.causal_ref, s32[2,256,1]{2,1,0:T(8,128)S(1)} %broadcast_in_dim_reshape.19.key_ref, s32[2,1,256]{2,1,0:T(1,128)S(1)} %bitcast.286, bf16[512,3072]{1,0:T(8,128)(2,1)S(1)} %add_convert_fusion.6.q_ref.k_ref.v_ref, ...), custom_call_target="tpu_custom_call" | custom-call | flops 536870912 | bytes 4194304 | tf_op jit(solution)/shard_map/attend_fwd/pallas_call | solution.py:154
  241.8 2.9 fusion.162
  246.5 4.2 fusion.246
  252.9 23.1 %conditional.5 = (bf16[512,1024]{1,0:T(8,128)(2,1)S(1)}, bf16[512,4096]{1,0:T(8,128)(2,1)}, bf16[512,4096]{1,0:T(8,128)(2,1)}, f32[512,1024]{1,0:T(8,128)S(1)}, f32[512,1]{0,1:T(1,128)}) conditional(s32[]{:T(128)} %convert_element_type.566, () %tuple.96, (bf16[512,1024]{1,0:T(8,128)(2,1)}, bf16[1024,4096]{1,0:T(8,128)(2,1)}, f32[16,256]{1,0:T(8,128)S(1)}, ...), branch_computations={%region_2.3_spmd, %region_3.6_spmd} | conditional | flops 8620868608 | bytes 50518168 | solution.py:670
  253.1 12.2 %fusion.4 = (bf16[512,4096]{1,0:T(8,128)(2,1)}, bf16[512,4096]{1,0:T(8,128)(2,1)}) fusion(f32[4096]{0:T(1024)S(1)} %bitcast.303, bf16[512,1024]{1,0:T(8,128)(2,1)} %get-tuple-element.126, bf16[1024,4096]{1,0:T(8,128)(2,1)} %get-tuple-element.127), kind=kOutput, calls=%fused_computation.6 | convolution fusion | flops 4320133120 | bytes 17842176 | tf_op jit(solution)/shard_map/cond/branch_1_fun/dot_general | solution.py:20
  265.4 8.4 fusion.247
  278.3 34.7 %collective-permute-done.22 = bf16[512,1024]{1,0:T(8,128)(2,1)} collective-permute-done((bf16[512,1024]{1,0:T(8,128)(2,1)S(1)}, bf16[512,1024]{1,0:T(8,128)(2,1)}, u32[]{:S(2)}, u32[]{:S(2)}) %collective-permute-start.22) | collective-permute-done | bytes 1048608 | tf_op jit(solution)/shard_map/ppermute | solution.py:329
  313.0 16.9 %conditional.6 = (bf16[512,1024]{1,0:T(8,128)(2,1)}, bf16[512,1024]{1,0:T(8,128)(2,1)S(1)}, bf16[512,1024]{1,0:T(8,128)(2,1)}, bf16[512,4096]{1,0:T(8,128)(2,1)}...) conditional(s32[]{:T(128)} %convert_element_type.566, ...), branch_computations={%region_6.22_spmd, %region_22.23_spmd} | conditional | flops 26658598912 | bytes 209142640 | solution.py:725
  330.9 61.5 %conditional.7 = (bf16[8,5]{1,0:T(8,128)(2,1)S(1)}, bf16[256,768]{1,0:T(8,128)(2,1)S(1)}, f32[]{:T(128)}, bf16[8,12288]{1,0:T(8,128)(2,1)}, bf16[96,1536]{1,0:T(...) conditional(s32[]{:T(128)} %convert_element_type.566, ...), branch_computations={%region_23.24_spmd, %region_24.49_spmd} | conditional | flops 1519001600 | bytes 49347288 | solution.py:670
  344.7 3.1 multiply_convert_fusion.6
  368.2 3.8 multiply_reduce_fusion.11
  393.1 59.6 %collective-permute-start.26 = (bf16[512,1024]{1,0:T(8,128)(2,1)}, bf16[512,1024]{1,0:T(8,128)(2,1)S(1)}, u32[]{:S(2)}, u32[]{:S(2)}) collective-permute-start(bf16[512,1024]{1,0:T(8,128)(2,1)} %get-tuple-element.461), channel_id=1, source_target_pairs={{0,0},{16,8},{1,1},{17,9},{2,2},{18,10},{3,3},{19,11},{4,4},{20,12... | collective-permute-start | bytes 3145736 | tf_op jit(solution)/shard_map/ppermute | solution.py:291
  457.8 5.0 collective-permute-start.25
  469.8 7.4 collective-permute-done.23
  477.2 6.0 conditional.8
  477.2 4.3 reshape.759
  483.1 23.8 %conditional.9 = ((bf16[512,1024]{1,0:T(8,128)(2,1)}, bf16[512,4096]{1,0:T(8,128)(2,1)}, f32[512,1024]{1,0:T(8,128)}, f32[1024]{0:T(1024)}, f32[1024]{0:T(1024)})) conditional(s32[]{:T(128)} %convert_element_type.566, (bf16[512,1024]{1,0:T(8,128)(2,1)}, bf16[512,4096]{1,0:T(8,128)(2,1)}, f32[512,1024]{1,0:T(8,128)}, f32[1024]{0:T(1024)}, ...), branch_computations={%region_51.52_spmd, %region_52.57_spmd} | conditional | flops 8607758336 | bytes 72405152 | solution.py:805
  486.4 9.2 %multiply_convert_fusion.1 = bf16[512,4096]{1,0:T(8,128)(2,1)S(1)} fusion(bf16[512,4096]{1,0:T(8,128)(2,1)} %get-tuple-element.167, bf16[512,1024]{1,0:T(8,128)(2,1)S(1)} %fusion.17, bf16[4096,1024]{1,0:T(8,128)(2,1)} %get-tuple-element.166), kind=kOutput, calls=%fused_computation.22 | convolution fusion | flops 4301258752 | bytes 17825792 | tf_op jit(solution)/shard_map/cond/branch_1_fun/dot_general | solution.py:28
  495.6 10.9 %convolution_add_fusion = f32[512,1024]{1,0:T(8,128)} fusion(bf16[512,4096]{1,0:T(8,128)(2,1)S(1)} %multiply_convert_fusion.1, bf16[1024,4096]{1,0:T(8,128)(2,1)} %get-tuple-element.168, f32[512,1024]{1,0:T(8,128)S(1)} %get-tuple-element.165, f32[512]{0:T(512)S(1)} %get-tuple-element.590, f32[512]{0:T(512)S(1)} %get-tuple-element.591, ...), kind=kOutput, calls=%fused_computation.33 | convolution fusion | flops 4298637312 | bytes 17836032 | tf_op jit(solution)/shard_map/cond/branch_1_fun/dot_general | solution.py:28
  507.0 6.4 convolution_convert_fusion.10
  513.4 4.4 convolution_convert_fusion.9
  518.4 4.9 dynamic-slice_bitcast_fusion
  531.7 2.8 convert_reduce_fusion.15
  536.8 10.7 %collective-permute-done.30 = bf16[512,1024]{1,0:T(8,128)(2,1)S(1)} collective-permute-done((bf16[512,1024]{1,0:T(8,128)(2,1)}, bf16[512,1024]{1,0:T(8,128)(2,1)S(1)}, u32[]{:S(2)}, u32[]{:S(2)}) %collective-permute-start.30) | collective-permute-done | bytes 1048608 | tf_op jit(solution)/shard_map/ppermute | solution.py:291
  548.5 5.0 fusion.125
  558.4 5.3 add_convert_fusion.4
  566.8 27.6 %collective-permute-start.32 = (bf16[1,2,2,256,1024]{4,3,2,1,0:T(8,128)(2,1)}, bf16[1,2,2,256,1024]{4,3,2,1,0:T(8,128)(2,1)}, u32[]{:S(2)}, u32[]{:S(2)}) collective-permute-start(bf16[1,2,2,256,1024]{4,3,2,1,0:T(8,128)(2,1)} %constant_dynamic-slice_fusion.20), channel_id=1, source_target_pairs={{0,4},{1,5},{2,6},{3,7},{4,0},{5,1},{6,2},{7,3},{8,12},{9,13},{10,... | collective-permute-start | bytes 6291464 | tf_op jit(solution)/shard_map/ppermute | solution.py:350
  594.4 4.6 add_convert_fusion.5
  603.8 3.3 convert_reduce_fusion.12
  612.8 21.4 %attend_bwd.3 = bf16[512,3072]{1,0:T(8,128)(2,1)S(1)} custom-call(s32[1]{0:T(128)} %bitcast.47.causal_ref, s32[2,256,1]{2,1,0:T(8,128)S(1)} %broadcast_in_dim_reshape.19.key_ref, s32[2,1,256]{2,1,0:T(1,128)S(1)} %bitcast.287, bf16[512,3072]{1,0:T(8,128)(2,1)} %copy-done, bf16[512,3072]{1,0:T(8,128)(2,1)} %copy-done, bf16[512,3072]{1,0:T(8,128)(2,1)} %copy-done, ...), custom_call_target="tpu_custom_call" | custom-call | flops 1342177280 | bytes 7340032 | tf_op jit(solution)/shard_map/attend_bwd/pallas_call | solution.py:170
  635.3 5.7 reshape.890
  643.7 4.4 add_convert_fusion.7
  648.1 4.2 add_convert_fusion.8
  652.3 3.7 add_convert_fusion.9
  657.7 7.8 add_convert_fusion.11
  673.1 3.3 convolution_convert_fusion.11
  676.4 3.2 convolution_convert_fusion.12
  680.6 19.7 %collective-permute-done.35 = bf16[1,2,1,256,1024]{4,3,2,1,0:T(8,128)(2,1)} collective-permute-done((bf16[1,2,1,256,1024]{4,3,2,1,0:T(8,128)(2,1)}, bf16[1,2,1,256,1024]{4,3,2,1,0:T(8,128)(2,1)}, u32[]{:S(2)}, u32[]{:S(2)}) %collective-permute-start.35) | collective-permute-done | bytes 1048608 | tf_op jit(solution)/shard_map/ppermute | solution.py:350
  701.0 3.6 collective-permute-done.34
  722.5 3.8 collective-permute-done.44
  726.3 8.9 %collective-permute-start.46 = (bf16[512,1024]{1,0:T(8,128)(2,1)S(1)}, bf16[512,1024]{1,0:T(8,128)(2,1)}, u32[]{:S(2)}, u32[]{:S(2)}) collective-permute-start(bf16[512,1024]{1,0:T(8,128)(2,1)S(1)} %copy-done.127), channel_id=1, source_target_pairs={{0,0},{16,8},{8,16},{24,24},{1,1},{17,9},{9,17},{25,25},{2,2},{18,... | collective-permute-start | bytes 3145736 | tf_op jit(solution)/shard_map/ppermute | solution.py:291
  737.4 4.4 collective-permute-done.42
  743.4 15.8 %collective-permute-done.46 = bf16[512,1024]{1,0:T(8,128)(2,1)} collective-permute-done((bf16[512,1024]{1,0:T(8,128)(2,1)S(1)}, bf16[512,1024]{1,0:T(8,128)(2,1)}, u32[]{:S(2)}, u32[]{:S(2)}) %collective-permute-start.46) | collective-permute-done | bytes 1048608 | tf_op jit(solution)/shard_map/ppermute | solution.py:291
  765.4 7.1 collective-permute-start.49
  773.1 3.6 collective-permute-done.64
  780.9 3.6 collective-permute-start.62
  794.3 3.2 fusion.145
  812.1 3.5 collective-permute-start.56
  816.6 8.5 collective-permute-start.61
  846.0 9.6 %collective-permute-done.60 = bf16[64,4096]{1,0:T(8,128)(2,1)S(1)} collective-permute-done((bf16[64,4096]{1,0:T(8,128)(2,1)S(1)}, bf16[64,4096]{1,0:T(8,128)(2,1)S(1)}, u32[]{:S(2)}, u32[]{:S(2)}) %collective-permute-start.60) | collective-permute-done | bytes 524320 | tf_op jit(solution)/shard_map/ppermute | solution.py:291
  (701 shorter events, 252.7 us)
Async XLA Ops:
  7.2 113.3 %all-gather.6.cloned.1.call-start = ((), (), s32[]{:S(2)}) async-start(), calls=%async_computation | async-start | bytes 8921088 | tf_op jit(solution)/shard_map/all_gather | solution.py:612
  9.8 320.1 %all-gather.8.cloned.1.call-start = ((), (), s32[]{:S(2)}) async-start(), calls=%async_computation.1 | async-start | bytes 14800896 | tf_op jit(solution)/shard_map/all_gather | solution.py:626
  14.0 58.3 %collective-permute-start = (bf16[64,4224]{1,0:T(8,128)(2,1)S(1)}, bf16[64,4224]{1,0:T(8,128)(2,1)S(1)}, u32[]{:S(2)}, u32[]{:S(2)}) collective-permute-start(bf16[64,4224]{1,0:T(8,128)(2,1)S(1)} %pad_maximum_fusion.12), channel_id=1, source_target_pairs={{0,0},{16,8},{8,16},{24,24},{1,1},{17,9},{9,17},{25,25},{2,2},{18,... | collective-permute-start | bytes 1622024 | tf_op jit(solution)/shard_map/ppermute | solution.py:291
  19.6 46.2 %collective-permute-start.1 = (bf16[64,4096]{1,0:T(8,128)(2,1)}, bf16[64,4096]{1,0:T(8,128)(2,1)S(1)}, u32[]{:S(2)}, u32[]{:S(2)}) collective-permute-start(bf16[64,4096]{1,0:T(8,128)(2,1)} %bitcast.323), channel_id=1, source_target_pairs={{0,0},{16,8},{8,16},{24,24},{1,1},{17,9},{9,17},{25,25},{2,2},{18,... | collective-permute-start | bytes 1572872 | tf_op jit(solution)/shard_map/ppermute | solution.py:291
  21.5 50.8 %collective-permute-start.2 = (bf16[256,1024]{1,0:T(8,128)(2,1)}, bf16[256,1024]{1,0:T(8,128)(2,1)S(1)}, u32[]{:S(2)}, u32[]{:S(2)}) collective-permute-start(bf16[256,1024]{1,0:T(8,128)(2,1)} %bitcast.324), channel_id=1, source_target_pairs={{0,0},{16,8},{8,16},{24,24},{1,1},{17,9},{9,17},{25,25},{2,2},{18,... | collective-permute-start | bytes 1572872 | tf_op jit(solution)/shard_map/ppermute | solution.py:291
  72.3 26.6 %collective-permute-start.5 = (bf16[1,256,1024]{2,1,0:T(8,128)(2,1)S(1)}, bf16[1,256,1024]{2,1,0:T(8,128)(2,1)S(1)}, u32[]{:S(2)}, u32[]{:S(2)}) collective-permute-start(bf16[1,256,1024]{2,1,0:T(8,128)(2,1)S(1)} %bitcast.267), channel_id=1, source_target_pairs={{0,4},{1,5},{2,6},{3,7},{4,0},{5,1},{6,2},{7,3},{8,12},{9,13},{10,... | collective-permute-start | bytes 1572872 | tf_op jit(solution)/shard_map/ppermute | solution.py:350
  72.8 26.2 %collective-permute-start.4 = (bf16[1,64,4096]{2,1,0:T(8,128)(2,1)S(1)}, bf16[1,64,4096]{2,1,0:T(8,128)(2,1)S(1)}, u32[]{:S(2)}, u32[]{:S(2)}) collective-permute-start(bf16[1,64,4096]{2,1,0:T(8,128)(2,1)S(1)} %bitcast.265), channel_id=1, source_target_pairs={{0,2},{1,3},{2,0},{3,1},{4,6},{5,7},{6,4},{7,5},{8,10},{9,11},{10,... | collective-permute-start | bytes 1572872 | tf_op jit(solution)/shard_map/ppermute | solution.py:350
  74.0 25.1 %collective-permute-start.3 = (bf16[1,64,4224]{2,1,0:T(8,128)(2,1)S(1)}, bf16[1,64,4224]{2,1,0:T(8,128)(2,1)S(1)}, u32[]{:S(2)}, u32[]{:S(2)}) collective-permute-start(bf16[1,64,4224]{2,1,0:T(8,128)(2,1)S(1)} %bitcast.263), channel_id=1, source_target_pairs={{0,1},{1,0},{2,3},{3,2},{4,5},{5,4},{6,7},{7,6},{8,9},{9,8},{10,11... | collective-permute-start | bytes 1622024 | tf_op jit(solution)/shard_map/ppermute | solution.py:350
  99.2 13.7 %collective-permute-start.8 = (bf16[2,256,1024]{2,1,0:T(8,128)(2,1)S(1)}, bf16[2,256,1024]{2,1,0:T(8,128)(2,1)S(1)}, u32[]{:S(2)}, u32[]{:S(2)}) collective-permute-start(bf16[2,256,1024]{2,1,0:T(8,128)(2,1)S(1)} %pad_maximum_fusion.11), channel_id=1, source_target_pairs={{0,1},{1,0},{2,3},{3,2},{4,5},{5,4},{6,7},{7,6},{8,9},{9,8},{10,11... | collective-permute-start | bytes 3145736 | tf_op jit(solution)/shard_map/ppermute | solution.py:350
  99.6 19.0 %collective-permute-start.7 = (bf16[2,64,4096]{2,1,0:T(8,128)(2,1)S(1)}, bf16[2,64,4096]{2,1,0:T(8,128)(2,1)S(1)}, u32[]{:S(2)}, u32[]{:S(2)}) collective-permute-start(bf16[2,64,4096]{2,1,0:T(8,128)(2,1)S(1)} %pad_maximum_fusion.10), channel_id=1, source_target_pairs={{0,4},{1,5},{2,6},{3,7},{4,0},{5,1},{6,2},{7,3},{8,12},{9,13},{10,... | collective-permute-start | bytes 3145736 | tf_op jit(solution)/shard_map/ppermute | solution.py:350
  99.6 19.3 %collective-permute-start.6 = (bf16[2,64,4224]{2,1,0:T(8,128)(2,1)S(1)}, bf16[2,64,4224]{2,1,0:T(8,128)(2,1)S(1)}, u32[]{:S(2)}, u32[]{:S(2)}) collective-permute-start(bf16[2,64,4224]{2,1,0:T(8,128)(2,1)S(1)} %pad_maximum_fusion.9), channel_id=1, source_target_pairs={{0,2},{1,3},{2,0},{3,1},{4,6},{5,7},{6,4},{7,5},{8,10},{9,11},{10,... | collective-permute-start | bytes 3244040 | tf_op jit(solution)/shard_map/ppermute | solution.py:350
  120.5 39.1 %collective-permute-start.10 = (bf16[4,64,4096]{2,1,0:T(8,128)(2,1)S(1)}, bf16[4,64,4096]{2,1,0:T(8,128)(2,1)S(1)}, u32[]{:S(2)}, u32[]{:S(2)}) collective-permute-start(bf16[4,64,4096]{2,1,0:T(8,128)(2,1)S(1)} %pad_maximum_fusion.7.refs_4_), channel_id=1, source_target_pairs={{0,1},{1,0},{2,3},{3,2},{4,5},{5,4},{6,7},{7,6},{8,9},{9,8},{10,11... | collective-permute-start | bytes 6291464 | tf_op jit(solution)/shard_map/ppermute | solution.py:350
  121.3 48.9 %collective-permute-start.12 = (bf16[4,64,4224]{2,1,0:T(8,128)(2,1)}, bf16[4,64,4224]{2,1,0:T(8,128)(2,1)}, u32[]{:S(2)}, u32[]{:S(2)}) collective-permute-start(bf16[4,64,4224]{2,1,0:T(8,128)(2,1)} %pad_maximum_fusion.6.refs_0_), channel_id=1, source_target_pairs={{0,16},{16,0},{1,17},{17,1},{2,18},{18,2},{3,19},{19,3},{4,20},{20... | collective-permute-start | bytes 6488072 | tf_op jit(solution)/shard_map/ppermute | solution.py:291
  121.3 48.9 %collective-permute-start.9 = (bf16[4,64,4224]{2,1,0:T(8,128)(2,1)}, bf16[4,64,4224]{2,1,0:T(8,128)(2,1)}, u32[]{:S(2)}, u32[]{:S(2)}) collective-permute-start(bf16[4,64,4224]{2,1,0:T(8,128)(2,1)} %pad_maximum_fusion.6.refs_0_), channel_id=1, source_target_pairs={{0,4},{1,5},{2,6},{3,7},{4,0},{5,1},{6,2},{7,3},{8,12},{9,13},{10,... | collective-permute-start | bytes 6488072 | tf_op jit(solution)/shard_map/ppermute | solution.py:350
  121.8 48.4 %collective-permute-start.13 = (bf16[4,64,4096]{2,1,0:T(8,128)(2,1)S(1)}, bf16[4,64,4096]{2,1,0:T(8,128)(2,1)}, u32[]{:S(2)}, u32[]{:S(2)}) collective-permute-start(bf16[4,64,4096]{2,1,0:T(8,128)(2,1)S(1)} %pad_maximum_fusion.7.refs_4_), channel_id=1, source_target_pairs={{0,16},{16,0},{1,17},{17,1},{2,18},{18,2},{3,19},{19,3},{4,20},{20... | collective-permute-start | bytes 6291464 | tf_op jit(solution)/shard_map/ppermute | solution.py:291
  122.6 47.6 %collective-permute-start.11 = (bf16[4,256,1024]{2,1,0:T(8,128)(2,1)}, bf16[4,256,1024]{2,1,0:T(8,128)(2,1)}, u32[]{:S(2)}, u32[]{:S(2)}) collective-permute-start(bf16[4,256,1024]{2,1,0:T(8,128)(2,1)} %pad_maximum_fusion.8.refs_8_), channel_id=1, source_target_pairs={{0,2},{1,3},{2,0},{3,1},{4,6},{5,7},{6,4},{7,5},{8,10},{9,11},{10,... | collective-permute-start | bytes 6291464 | tf_op jit(solution)/shard_map/ppermute | solution.py:350
  160.9 9.3 %collective-permute-start.14 = (bf16[4,256,1024]{2,1,0:T(8,128)(2,1)}, bf16[4,256,1024]{2,1,0:T(8,128)(2,1)}, u32[]{:S(2)}, u32[]{:S(2)}) collective-permute-start(bf16[4,256,1024]{2,1,0:T(8,128)(2,1)} %pad_maximum_fusion.8.refs_8_), channel_id=1, source_target_pairs={{0,16},{16,0},{1,17},{17,1},{2,18},{18,2},{3,19},{19,3},{4,20},{20... | collective-permute-start | bytes 6291464 | tf_op jit(solution)/shard_map/ppermute | solution.py:291
  170.2 465.1 %all-gather.12.cloned.1.call-start = ((), (), s32[]{:S(2)}) async-start(), calls=%async_computation.3 | async-start | bytes 3244032 | tf_op jit(solution)/shard_map/all_gather | solution.py:774
  170.3 11.1 %collective-permute-start.16 = (bf16[4,64,4224]{2,1,0:T(8,128)(2,1)}, bf16[4,64,4224]{2,1,0:T(8,128)(2,1)}, u32[]{:S(2)}, u32[]{:S(2)}) collective-permute-start(bf16[4,64,4224]{2,1,0:T(8,128)(2,1)} %collective-permute-done.9.refs_1_), channel_id=1, source_target_pairs={{0,16},{16,0},{1,17},{17,1},{2,18},{18,2},{3,19},{19,3},{4,20},{20... | collective-permute-start | bytes 6488072 | tf_op jit(solution)/shard_map/ppermute | solution.py:291
  171.2 8.0 collective-permute-start.17
  171.3 10.1 %collective-permute-start.18 = (bf16[4,256,1024]{2,1,0:T(8,128)(2,1)}, bf16[4,256,1024]{2,1,0:T(8,128)(2,1)}, u32[]{:S(2)}, u32[]{:S(2)}) collective-permute-start(bf16[4,256,1024]{2,1,0:T(8,128)(2,1)} %collective-permute-done.11.refs_9_), channel_id=1, source_target_pairs={{0,16},{16,0},{1,17},{17,1},{2,18},{18,2},{3,19},{19,3},{4,20},{20... | collective-permute-start | bytes 6291464 | tf_op jit(solution)/shard_map/ppermute | solution.py:291
  174.1 38.6 %collective-permute-start.15 = (bf16[512,1024]{1,0:T(8,128)(2,1)}, bf16[512,1024]{1,0:T(8,128)(2,1)}, u32[]{:S(2)}, u32[]{:S(2)}) collective-permute-start(bf16[512,1024]{1,0:T(8,128)(2,1)} %bitcast.321), channel_id=1, source_target_pairs={{0,0},{16,8},{8,16},{24,24},{1,1},{17,9},{9,17},{25,25},{2,2},{18,... | collective-permute-start | bytes 3145736 | tf_op jit(solution)/shard_map/ppermute | solution.py:291
  223.1 29.8 %collective-permute-start.19 = (bf16[512,1024]{1,0:T(8,128)(2,1)}, bf16[512,1024]{1,0:T(8,128)(2,1)}, u32[]{:S(2)}, u32[]{:S(2)}) collective-permute-start(bf16[512,1024]{1,0:T(8,128)(2,1)} %bitcast.322), channel_id=1, source_target_pairs={{24,24},{16,8},{25,25},{17,9},{26,26},{18,10},{27,27},{19,11},{28,... | collective-permute-start | bytes 3145736 | tf_op jit(solution)/shard_map/ppermute | solution.py:291
  225.9 26.9 %collective-permute-start.21 = (bf16[256,768]{1,0:T(8,128)(2,1)}, bf16[256,768]{1,0:T(8,128)(2,1)}, u32[]{:S(2)}, u32[]{:S(2)}) collective-permute-start(bf16[256,768]{1,0:T(8,128)(2,1)} %bitcast.325), channel_id=1, source_target_pairs={{0,0},{8,16},{1,1},{9,17},{2,2},{10,18},{3,3},{11,19},{4,4},{12,20... | collective-permute-start | bytes 1179656 | tf_op jit(solution)/shard_map/ppermute | solution.py:291
  227.2 25.6 %collective-permute-start.20 = (f32[33,768]{1,0:T(8,128)}, f32[33,768]{1,0:T(8,128)S(1)}, u32[]{:S(2)}, u32[]{:S(2)}) collective-permute-start(f32[33,768]{1,0:T(8,128)} %pad_maximum_fusion.16), channel_id=1, source_target_pairs={{0,0},{8,16},{1,1},{9,17},{2,2},{10,18},{3,3},{11,19},{4,4},{12,20... | collective-permute-start | bytes 304136 | tf_op jit(solution)/shard_map/ppermute | solution.py:291
  276.0 37.0 %collective-permute-start.22 = (bf16[512,1024]{1,0:T(8,128)(2,1)S(1)}, bf16[512,1024]{1,0:T(8,128)(2,1)}, u32[]{:S(2)}, u32[]{:S(2)}) collective-permute-start(bf16[512,1024]{1,0:T(8,128)(2,1)S(1)} %get-tuple-element.390), channel_id=1, source_target_pairs={{0,8},{1,9},{2,10},{3,11},{4,12},{5,13},{6,14},{7,15},{16,24},{17,... | collective-permute-start | bytes 3145736 | tf_op jit(solution)/shard_map/ppermute | solution.py:329
  393.1 76.7 %collective-permute-start.26 = (bf16[512,1024]{1,0:T(8,128)(2,1)}, bf16[512,1024]{1,0:T(8,128)(2,1)S(1)}, u32[]{:S(2)}, u32[]{:S(2)}) collective-permute-start(bf16[512,1024]{1,0:T(8,128)(2,1)} %get-tuple-element.461), channel_id=1, source_target_pairs={{0,0},{16,8},{1,1},{17,9},{2,2},{18,10},{3,3},{19,11},{4,4},{20,12... | collective-permute-start | bytes 3145736 | tf_op jit(solution)/shard_map/ppermute | solution.py:291
  452.6 24.5 %collective-permute-start.23 = (bf16[512,1024]{1,0:T(8,128)(2,1)}, bf16[512,1024]{1,0:T(8,128)(2,1)S(1)}, u32[]{:S(2)}, u32[]{:S(2)}) collective-permute-start(bf16[512,1024]{1,0:T(8,128)(2,1)} %copy-done.128), channel_id=1, source_target_pairs={{8,0},{9,1},{10,2},{11,3},{12,4},{13,5},{14,6},{15,7},{24,16},{25,... | collective-permute-start | bytes 3145736 | tf_op jit(solution)/shard_map/ppermute | solution.py:332
  457.8 11.9 %collective-permute-start.25 = (bf16[48,1536]{1,0:T(8,128)(2,1)S(1)}, bf16[48,1536]{1,0:T(8,128)(2,1)S(1)}, u32[]{:S(2)}, u32[]{:S(2)}) collective-permute-start(bf16[48,1536]{1,0:T(8,128)(2,1)S(1)} %slice.488), channel_id=1, source_target_pairs={{0,8},{1,9},{2,10},{3,11},{4,12},{5,13},{6,14},{7,15},{16,24},{17,... | collective-permute-start | bytes 442376 | tf_op jit(solution)/shard_map/ppermute | solution.py:329
  513.4 34.2 %collective-permute-start.28 = (bf16[2048,1024]{1,0:T(8,128)(2,1)}, bf16[2048,1024]{1,0:T(8,128)(2,1)}, u32[]{:S(2)}, u32[]{:S(2)}) collective-permute-start(bf16[2048,1024]{1,0:T(8,128)(2,1)} %convolution_convert_fusion.10), channel_id=1, source_target_pairs={{0,16},{16,0},{1,17},{17,1},{2,18},{18,2},{3,19},{19,3},{4,20},{20... | collective-permute-start | bytes 12582920 | tf_op jit(solution)/shard_map/ppermute | solution.py:291
  517.8 29.7 %collective-permute-start.27 = (bf16[512,4096]{1,0:T(8,128)(2,1)}, bf16[512,4096]{1,0:T(8,128)(2,1)}, u32[]{:S(2)}, u32[]{:S(2)}) collective-permute-start(bf16[512,4096]{1,0:T(8,128)(2,1)} %convolution_convert_fusion.9), channel_id=1, source_target_pairs={{0,16},{16,0},{1,17},{17,1},{2,18},{18,2},{3,19},{19,3},{4,20},{20... | collective-permute-start | bytes 12582920 | tf_op jit(solution)/shard_map/ppermute | solution.py:291
  523.3 25.3 %collective-permute-start.29 = (bf16[512,4096]{1,0:T(8,128)(2,1)}, bf16[512,4096]{1,0:T(8,128)(2,1)}, u32[]{:S(2)}, u32[]{:S(2)}) collective-permute-start(bf16[512,4096]{1,0:T(8,128)(2,1)} %dynamic-slice_bitcast_fusion), channel_id=1, source_target_pairs={{8,24},{24,8},{9,25},{25,9},{10,26},{26,10},{11,27},{27,11},{12,28... | collective-permute-start | bytes 12582920 | tf_op jit(solution)/shard_map/ppermute | solution.py:291
  527.7 231.5 %all-gather.10.cloned.1.call-start = ((), (), s32[]{:S(2)}) async-start(), calls=%async_computation.2 | async-start | bytes 4866048 | tf_op jit(solution)/shard_map/all_gather | solution.py:774
  530.3 17.2 %collective-permute-start.30 = (bf16[512,1024]{1,0:T(8,128)(2,1)}, bf16[512,1024]{1,0:T(8,128)(2,1)S(1)}, u32[]{:S(2)}, u32[]{:S(2)}) collective-permute-start(bf16[512,1024]{1,0:T(8,128)(2,1)} %get-tuple-element.461), channel_id=1, source_target_pairs={{24,24},{8,16},{25,25},{9,17},{26,26},{10,18},{27,27},{11,19},{28,... | collective-permute-start | bytes 3145736 | tf_op jit(solution)/shard_map/ppermute | solution.py:291
  556.2 84.8 %collective-permute-start.33 = (bf16[2,2,2,1,32,4096]{5,4,3,2,1,0:T(8,128)(2,1)}, bf16[2,2,2,1,32,4096]{5,4,3,2,1,0:T(8,128)(2,1)}, u32[]{:S(2)}, u32[]{:S(2)}) collective-permute-start(bf16[2,2,2,1,32,4096]{5,4,3,2,1,0:T(8,128)(2,1)} %constant_dynamic-slice_fusion.19), channel_id=1, source_target_pairs={{8,9},{9,8},{10,11},{11,10},{12,13},{13,12},{14,15},{15,14},{24,25... | collective-permute-start | bytes 6291464 | tf_op jit(solution)/shard_map/ppermute | solution.py:350
  566.8 74.2 %collective-permute-start.32 = (bf16[1,2,2,256,1024]{4,3,2,1,0:T(8,128)(2,1)}, bf16[1,2,2,256,1024]{4,3,2,1,0:T(8,128)(2,1)}, u32[]{:S(2)}, u32[]{:S(2)}) collective-permute-start(bf16[1,2,2,256,1024]{4,3,2,1,0:T(8,128)(2,1)} %constant_dynamic-slice_fusion.20), channel_id=1, source_target_pairs={{0,4},{1,5},{2,6},{3,7},{4,0},{5,1},{6,2},{7,3},{8,12},{9,13},{10,... | collective-permute-start | bytes 6291464 | tf_op jit(solution)/shard_map/ppermute | solution.py:350
  601.7 42.0 %collective-permute-start.31 = (bf16[2,1,2,64,4096]{4,3,2,1,0:T(8,128)(2,1)}, bf16[2,1,2,64,4096]{4,3,2,1,0:T(8,128)(2,1)}, u32[]{:S(2)}, u32[]{:S(2)}) collective-permute-start(bf16[2,1,2,64,4096]{4,3,2,1,0:T(8,128)(2,1)} %constant_dynamic-slice_fusion.21), channel_id=1, source_target_pairs={{0,2},{1,3},{2,0},{3,1},{4,6},{5,7},{6,4},{7,5},{8,10},{9,11},{10,... | collective-permute-start | bytes 6291464 | tf_op jit(solution)/shard_map/ppermute | solution.py:350
  609.1 100.8 %collective-permute-start.39 = (bf16[512,1024]{1,0:T(8,128)(2,1)}, bf16[512,1024]{1,0:T(8,128)(2,1)}, u32[]{:S(2)}, u32[]{:S(2)}) collective-permute-start(bf16[512,1024]{1,0:T(8,128)(2,1)} %convolution_convert_fusion.14), channel_id=1, source_target_pairs={{0,16},{16,0},{1,17},{17,1},{2,18},{18,2},{3,19},{19,3},{4,20},{20... | collective-permute-start | bytes 3145736 | tf_op jit(solution)/shard_map/ppermute | solution.py:291
  665.6 14.0 %collective-permute-start.40 = (f32[8,1665]{1,0:T(8,128)S(1)}, f32[8,1665]{1,0:T(8,128)S(1)}, u32[]{:S(2)}, u32[]{:S(2)}) collective-permute-start(f32[8,1665]{1,0:T(8,128)S(1)} %dynamic-slice_bitcast_fusion.1), channel_id=1, source_target_pairs={{0,16},{16,0},{1,17},{17,1},{2,18},{18,2},{3,19},{19,3},{4,20},{20... | collective-permute-start | bytes 159848 | tf_op jit(solution)/shard_map/ppermute | solution.py:291
  668.1 32.2 %collective-permute-start.35 = (bf16[1,2,1,256,1024]{4,3,2,1,0:T(8,128)(2,1)}, bf16[1,2,1,256,1024]{4,3,2,1,0:T(8,128)(2,1)}, u32[]{:S(2)}, u32[]{:S(2)}) collective-permute-start(bf16[1,2,1,256,1024]{4,3,2,1,0:T(8,128)(2,1)} %constant_dynamic-slice_fusion.17), channel_id=1, source_target_pairs={{0,1},{1,0},{2,3},{3,2},{4,5},{5,4},{6,7},{7,6},{8,9},{9,8},{10,11... | collective-permute-start | bytes 3145736 | tf_op jit(solution)/shard_map/ppermute | solution.py:350
  669.3 31.7 %collective-permute-start.36 = (bf16[2,2,1,1,32,4096]{5,4,3,2,1,0:T(8,128)(2,1)}, bf16[2,2,1,1,32,4096]{5,4,3,2,1,0:T(8,128)(2,1)}, u32[]{:S(2)}, u32[]{:S(2)}) collective-permute-start(bf16[2,2,1,1,32,4096]{5,4,3,2,1,0:T(8,128)(2,1)} %constant_dynamic-slice_fusion.16), channel_id=1, source_target_pairs={{8,10},{9,11},{10,8},{11,9},{12,14},{13,15},{14,12},{15,13},{24,26... | collective-permute-start | bytes 3145736 | tf_op jit(solution)/shard_map/ppermute | solution.py:350
  672.1 32.6 %collective-permute-start.34 = (bf16[1,1,2,64,4096]{4,3,2,1,0:T(8,128)(2,1)}, bf16[1,1,2,64,4096]{4,3,2,1,0:T(8,128)(2,1)}, u32[]{:S(2)}, u32[]{:S(2)}) collective-permute-start(bf16[1,1,2,64,4096]{4,3,2,1,0:T(8,128)(2,1)} %constant_dynamic-slice_fusion.18), channel_id=1, source_target_pairs={{0,4},{1,5},{2,6},{3,7},{4,0},{5,1},{6,2},{7,3},{8,12},{9,13},{10,... | collective-permute-start | bytes 3145736 | tf_op jit(solution)/shard_map/ppermute | solution.py:350
  679.6 30.3 %collective-permute-start.38 = (bf16[512,1536]{1,0:T(8,128)(2,1)}, bf16[512,1536]{1,0:T(8,128)(2,1)}, u32[]{:S(2)}, u32[]{:S(2)}) collective-permute-start(bf16[512,1536]{1,0:T(8,128)(2,1)} %convolution_convert_fusion.11), channel_id=1, source_target_pairs={{0,16},{16,0},{1,17},{17,1},{2,18},{18,2},{3,19},{19,3},{4,20},{20... | collective-permute-start | bytes 4718600 | tf_op jit(solution)/shard_map/ppermute | solution.py:291
  700.3 9.6 %collective-permute-start.37 = (bf16[512,1536]{1,0:T(8,128)(2,1)}, bf16[512,1536]{1,0:T(8,128)(2,1)S(1)}, u32[]{:S(2)}, u32[]{:S(2)}) collective-permute-start(bf16[512,1536]{1,0:T(8,128)(2,1)} %convolution_convert_fusion.12), channel_id=1, source_target_pairs={{0,16},{16,0},{1,17},{17,1},{2,18},{18,2},{3,19},{19,3},{4,20},{20... | collective-permute-start | bytes 4718600 | tf_op jit(solution)/shard_map/ppermute | solution.py:291
  710.0 11.2 %collective-permute-start.48 = (bf16[2,1,1,1,32,4096]{5,4,3,2,1,0:T(8,128)(2,1)S(1)}, bf16[2,1,1,1,32,4096]{5,4,3,2,1,0:T(8,128)(2,1)S(1)}, u32[]{:S(2)}, u32[]{:S(2)}) collective-permute-start(bf16[2,1,1,1,32,4096]{5,4,3,2,1,0:T(8,128)(2,1)S(1)} %constant_dynamic-slice_fusion.9), channel_id=1, source_target_pairs={{8,12},{9,13},{10,14},{11,15},{12,8},{13,9},{14,10},{15,11},{24,28... | collective-permute-start | bytes 1572872 | tf_op jit(solution)/shard_map/ppermute | solution.py:350
  711.1 9.8 %collective-permute-start.47 = (f32[2,2,1,1,1665]{4,2,1,0,3:T(1,128)S(1)}, f32[2,2,1,1,1665]{4,2,1,0,3:T(1,128)S(1)}, u32[]{:S(2)}, u32[]{:S(2)}) collective-permute-start(f32[2,2,1,1,1665]{4,2,1,0,3:T(1,128)S(1)} %constant_dynamic-slice_fusion.10), channel_id=1, source_target_pairs={{0,1},{1,0},{2,3},{3,2},{4,5},{5,4},{6,7},{7,6},{8,9},{9,8},{10,11... | collective-permute-start | bytes 79928 | tf_op jit(solution)/shard_map/ppermute | solution.py:350
  712.4 23.7 %collective-permute-start.45 = (bf16[1,1,1,256,1024]{4,3,2,1,0:T(8,128)(2,1)S(1)}, bf16[1,1,1,256,1024]{4,3,2,1,0:T(8,128)(2,1)S(1)}, u32[]{:S(2)}, u32[]{:S(2)}) collective-permute-start(bf16[1,1,1,256,1024]{4,3,2,1,0:T(8,128)(2,1)S(1)} %constant_dynamic-slice_fusion.11), channel_id=1, source_target_pairs={{0,2},{1,3},{2,0},{3,1},{4,6},{5,7},{6,4},{7,5},{8,10},{9,11},{10,... | collective-permute-start | bytes 1572872 | tf_op jit(solution)/shard_map/ppermute | solution.py:350
  713.9 12.4 %collective-permute-start.44 = (bf16[1,1,1,64,4096]{4,3,2,1,0:T(8,128)(2,1)S(1)}, bf16[1,1,1,64,4096]{4,3,2,1,0:T(8,128)(2,1)S(1)}, u32[]{:S(2)}, u32[]{:S(2)}) collective-permute-start(bf16[1,1,1,64,4096]{4,3,2,1,0:T(8,128)(2,1)S(1)} %constant_dynamic-slice_fusion.12), channel_id=1, source_target_pairs={{0,1},{1,0},{2,3},{3,2},{4,5},{5,4},{6,7},{7,6},{8,9},{9,8},{10,11... | collective-permute-start | bytes 1572872 | tf_op jit(solution)/shard_map/ppermute | solution.py:350
  715.9 21.2 %collective-permute-start.43 = (bf16[1,2,2,64,1024]{4,3,2,1,0:T(8,128)(2,1)S(1)}, bf16[1,2,2,64,1024]{4,3,2,1,0:T(8,128)(2,1)S(1)}, u32[]{:S(2)}, u32[]{:S(2)}) collective-permute-start(bf16[1,2,2,64,1024]{4,3,2,1,0:T(8,128)(2,1)S(1)} %constant_dynamic-slice_fusion.13), channel_id=1, source_target_pairs={{0,4},{1,5},{2,6},{3,7},{4,0},{5,1},{6,2},{7,3},{8,12},{9,13},{10,... | collective-permute-start | bytes 1572872 | tf_op jit(solution)/shard_map/ppermute | solution.py:350
  720.8 20.9 %collective-permute-start.42 = (bf16[2,1,2,64,1536]{4,3,2,1,0:T(8,128)(2,1)S(1)}, bf16[2,1,2,64,1536]{4,3,2,1,0:T(8,128)(2,1)S(1)}, u32[]{:S(2)}, u32[]{:S(2)}) collective-permute-start(bf16[2,1,2,64,1536]{4,3,2,1,0:T(8,128)(2,1)S(1)} %constant_dynamic-slice_fusion.14), channel_id=1, source_target_pairs={{0,2},{1,3},{2,0},{3,1},{4,6},{5,7},{6,4},{7,5},{8,10},{9,11},{10,... | collective-permute-start | bytes 2359304 | tf_op jit(solution)/shard_map/ppermute | solution.py:350
  721.1 22.0 %collective-permute-start.41 = (bf16[2,2,1,64,1536]{4,3,2,1,0:T(8,128)(2,1)S(1)}, bf16[2,2,1,64,1536]{4,3,2,1,0:T(8,128)(2,1)S(1)}, u32[]{:S(2)}, u32[]{:S(2)}) collective-permute-start(bf16[2,2,1,64,1536]{4,3,2,1,0:T(8,128)(2,1)S(1)} %constant_dynamic-slice_fusion.15), channel_id=1, source_target_pairs={{0,1},{1,0},{2,3},{3,2},{4,5},{5,4},{6,7},{7,6},{8,9},{9,8},{10,11... | collective-permute-start | bytes 2359304 | tf_op jit(solution)/shard_map/ppermute | solution.py:350
  726.3 32.9 %collective-permute-start.46 = (bf16[512,1024]{1,0:T(8,128)(2,1)S(1)}, bf16[512,1024]{1,0:T(8,128)(2,1)}, u32[]{:S(2)}, u32[]{:S(2)}) collective-permute-start(bf16[512,1024]{1,0:T(8,128)(2,1)S(1)} %copy-done.127), channel_id=1, source_target_pairs={{0,0},{16,8},{8,16},{24,24},{1,1},{17,9},{9,17},{25,25},{2,2},{18,... | collective-permute-start | bytes 3145736 | tf_op jit(solution)/shard_map/ppermute | solution.py:291
  759.2 21.7 %collective-permute-start.53 = (bf16[1,2,1,64,1024]{4,3,2,1,0:T(8,128)(2,1)S(1)}, bf16[1,2,1,64,1024]{4,3,2,1,0:T(8,128)(2,1)S(1)}, u32[]{:S(2)}, u32[]{:S(2)}) collective-permute-start(bf16[1,2,1,64,1024]{4,3,2,1,0:T(8,128)(2,1)S(1)} %constant_dynamic-slice_fusion.6), channel_id=1, source_target_pairs={{0,1},{1,0},{2,3},{3,2},{4,5},{5,4},{6,7},{7,6},{8,9},{9,8},{10,11... | collective-permute-start | bytes 786440 | tf_op jit(solution)/shard_map/ppermute | solution.py:350
  759.3 25.3 %collective-permute-start.52 = (bf16[1,1,2,64,1536]{4,3,2,1,0:T(8,128)(2,1)S(1)}, bf16[1,1,2,64,1536]{4,3,2,1,0:T(8,128)(2,1)S(1)}, u32[]{:S(2)}, u32[]{:S(2)}) collective-permute-start(bf16[1,1,2,64,1536]{4,3,2,1,0:T(8,128)(2,1)S(1)} %constant_dynamic-slice_fusion.7), channel_id=1, source_target_pairs={{0,4},{1,5},{2,6},{3,7},{4,0},{5,1},{6,2},{7,3},{8,12},{9,13},{10,... | collective-permute-start | bytes 1179656 | tf_op jit(solution)/shard_map/ppermute | solution.py:350
  759.7 25.8 %collective-permute-start.51 = (bf16[2,1,1,64,1536]{4,3,2,1,0:T(8,128)(2,1)S(1)}, bf16[2,1,1,64,1536]{4,3,2,1,0:T(8,128)(2,1)S(1)}, u32[]{:S(2)}, u32[]{:S(2)}) collective-permute-start(bf16[2,1,1,64,1536]{4,3,2,1,0:T(8,128)(2,1)S(1)} %constant_dynamic-slice_fusion.8), channel_id=1, source_target_pairs={{0,2},{1,3},{2,0},{3,1},{4,6},{5,7},{6,4},{7,5},{8,10},{9,11},{10,... | collective-permute-start | bytes 1179656 | tf_op jit(solution)/shard_map/ppermute | solution.py:350
  761.2 15.4 %collective-permute-start.64 = (bf16[32,4096]{1,0:T(8,128)(2,1)S(1)}, bf16[32,4096]{1,0:T(8,128)(2,1)S(1)}, u32[]{:S(2)}, u32[]{:S(2)}) collective-permute-start(bf16[32,4096]{1,0:T(8,128)(2,1)S(1)} %slice_bitcast_fusion.2), channel_id=1, source_target_pairs={{8,0},{9,1},{10,2},{11,3},{12,4},{13,5},{14,6},{15,7},{24,16},{25,... | collective-permute-start | bytes 786440 | tf_op jit(solution)/shard_map/ppermute | solution.py:332
  765.4 41.2 %collective-permute-start.49 = (bf16[257,768]{1,0:T(8,128)(2,1)}, bf16[257,768]{1,0:T(8,128)(2,1)}, u32[]{:S(2)}, u32[]{:S(2)}) collective-permute-start(bf16[257,768]{1,0:T(8,128)(2,1)} %fusion.176), channel_id=1, source_target_pairs={{0,0},{16,8},{1,1},{17,9},{2,2},{18,10},{3,3},{19,11},{4,4},{20,12... | collective-permute-start | bytes 1184264 | tf_op jit(solution)/shard_map/ppermute | solution.py:291
  776.6 64.2 %collective-permute-start.63 = (bf16[256,1024]{1,0:T(8,128)(2,1)}, bf16[256,1024]{1,0:T(8,128)(2,1)}, u32[]{:S(2)}, u32[]{:S(2)}) collective-permute-start(bf16[256,1024]{1,0:T(8,128)(2,1)} %bitcast.103), channel_id=1, source_target_pairs={{0,0},{16,8},{8,16},{24,24},{1,1},{17,9},{9,17},{25,25},{2,2},{18,... | collective-permute-start | bytes 1572872 | tf_op jit(solution)/shard_map/ppermute | solution.py:291
  780.9 52.1 %collective-permute-start.62 = (bf16[64,4096]{1,0:T(8,128)(2,1)}, bf16[64,4096]{1,0:T(8,128)(2,1)}, u32[]{:S(2)}, u32[]{:S(2)}) collective-permute-start(bf16[64,4096]{1,0:T(8,128)(2,1)} %bitcast.100), channel_id=1, source_target_pairs={{0,0},{16,8},{8,16},{24,24},{1,1},{17,9},{9,17},{25,25},{2,2},{18,... | collective-permute-start | bytes 1572872 | tf_op jit(solution)/shard_map/ppermute | solution.py:291
  799.2 37.3 %collective-permute-start.57 = (bf16[1,1,1,64,1536]{4,3,2,1,0:T(8,128)(2,1)}, bf16[1,1,1,64,1536]{4,3,2,1,0:T(8,128)(2,1)}, u32[]{:S(2)}, u32[]{:S(2)}) collective-permute-start(bf16[1,1,1,64,1536]{4,3,2,1,0:T(8,128)(2,1)} %constant_dynamic-slice_fusion.2), channel_id=1, source_target_pairs={{0,4},{1,5},{2,6},{3,7},{4,0},{5,1},{6,2},{7,3},{8,12},{9,13},{10,... | collective-permute-start | bytes 589832 | tf_op jit(solution)/shard_map/ppermute | solution.py:350
  800.8 36.7 %collective-permute-start.58 = (bf16[1,1,1,64,1536]{4,3,2,1,0:T(8,128)(2,1)}, bf16[1,1,1,64,1536]{4,3,2,1,0:T(8,128)(2,1)}, u32[]{:S(2)}, u32[]{:S(2)}) collective-permute-start(bf16[1,1,1,64,1536]{4,3,2,1,0:T(8,128)(2,1)} %constant_dynamic-slice_fusion.1), channel_id=1, source_target_pairs={{0,1},{1,0},{2,3},{3,2},{4,5},{5,4},{6,7},{7,6},{8,9},{9,8},{10,11... | collective-permute-start | bytes 589832 | tf_op jit(solution)/shard_map/ppermute | solution.py:350
  816.6 13.5 %collective-permute-start.61 = (f32[768]{0:T(1024)S(1)}, f32[768]{0:T(1024)S(1)}, u32[]{:S(2)}, u32[]{:S(2)}) collective-permute-start(f32[768]{0:T(1024)S(1)} %slice_reduce_fusion.4), channel_id=1, source_target_pairs={{0,0},{16,8},{8,16},{24,24},{1,1},{17,9},{9,17},{25,25},{2,2},{18,... | collective-permute-start | bytes 9224 | tf_op jit(solution)/shard_map/ppermute | solution.py:291
  833.1 9.8 %collective-permute-start.50 = (bf16[129,768]{1,0:T(8,128)(2,1)S(1)}, bf16[129,768]{1,0:T(8,128)(2,1)S(1)}, u32[]{:S(2)}, u32[]{:S(2)}) collective-permute-start(bf16[129,768]{1,0:T(8,128)(2,1)S(1)} %fusion.190), channel_id=1, source_target_pairs={{0,16},{1,17},{2,18},{3,19},{4,20},{5,21},{6,22},{7,23},{8,24},{9,... | collective-permute-start | bytes 594440 | tf_op jit(solution)/shard_map/ppermute | solution.py:982
  838.5 17.0 %collective-permute-start.60 = (bf16[64,4096]{1,0:T(8,128)(2,1)S(1)}, bf16[64,4096]{1,0:T(8,128)(2,1)S(1)}, u32[]{:S(2)}, u32[]{:S(2)}) collective-permute-start(bf16[64,4096]{1,0:T(8,128)(2,1)S(1)} %pad_maximum_fusion.13), channel_id=1, source_target_pairs={{0,0},{16,8},{8,16},{24,24},{1,1},{17,9},{9,17},{25,25},{2,2},{18,... | collective-permute-start | bytes 1572872 | tf_op jit(solution)/shard_map/ppermute | solution.py:291
  (110 other events, 1805.2 us)
Sparse Core Ops, SparseCore 0:
  11.5 99.5 all-gather.5
  170.4 135.6 all-gather.7
  527.8 90.5 all-gather.11
  621.7 75.2 all-gather.9

commit v3 on v2

--- a/solution.py
+++ b/solution.py
@@ -907,8 +907,10 @@
     up_own = links.swap(up_sum.reshape(-1, ff)).astype(F32)
     down_own = links.swap(down_sum.reshape(-1, width)).astype(F32)
     for step in range(1, links.bits):
-        attn_sum = [links.reduce_step(v, turn, step) for turn, v in enumerate(attn_sum)]
-        small_sum = links.reduce_step(small_sum, 0, step)
+        *attn_sum, small_sum = links.reduce_steps(
+            [(v, turn, step, "both", 0) for turn, v in enumerate(attn_sum)]
+            + [(small_sum, 0, step, "both", 0)]
+        )
         if step + 1 < links.bits:
             attn_sum, small_sum, factors = stage(attn_sum, small_sum, factors)
     device = core * n + links.dp

time: 877 us -> 875 us (level)
    convert_element_type x6 -> x9, other arithmetic: 17.4 us -> 19.1 us  [reduce_steps(): (keep.astype(F32) + got.astype(F32)).astype(keep.dtype)]
  transfers between devices with their start and end apart: 69 -> 69, of which waited for: 23 -> 22; matrix products, arithmetic and copies ran while one was open for 26% -> 26% of each run, Pallas kernels for 7% -> 7%
where the time goes in v3:
time: 875 us; the launch traced here: 862 us
  waiting for transfers between devices  262 us (30%)
  starting transfers between devices  187 us (21%)
  matrix products  147 us (17%)
  local copies, waits for them, and re-layouts  96 us (11%)
  other arithmetic  89.6 us (10%)
  Pallas kernels  57.4 us (7%)
  between operations  16.1 us (2%)
    ppermute x28, starting transfers between devices, all_pairs(): return lax.ppermute(value, ('phase', 'dp'), pairs)  123 us
    ppermute x30, waiting for transfers between devices, hop(): lax.ppermute(value, 'dp', [(i, i ^ 1 << bit) for i in range(first, last)])  120 us
    ppermute x28, waiting for transfers between devices, all_pairs(): return lax.ppermute(value, ('phase', 'dp'), pairs)  87.4 us
    ppermute x30, starting transfers between devices, hop(): lax.ppermute(value, 'dp', [(i, i ^ 1 << bit) for i in range(first, last)])  50 us
    dot_general x15, matrix products, mm(): return jnp.dot(left, right, preferred_element_type=F32)  49.8 us
    dot_general x12, matrix products, mm_rt(): lax.dot_general(left, right, (((1,), (1,)), ((), ())), preferred_element_...  46.6 us
    dot_general x16, matrix products, mm_lt(): lax.dot_general(left, right, (((0,), (0,)), ((), ())), preferred_element_...  46.4 us
    ppermute x3, waiting for transfers between devices, to_dec(): lax.ppermute(value, 'dp', [(i, i + self.half) for i in range(self.half)])  37.5 us
  transfers between devices with their start and end apart: 69, of which 22 were waited for; matrix products, arithmetic and copies ran while one was open for 26% of the time, Pallas kernels for 7%

profile of v3, /device:TPU:1, one launch (start us, length us, event | category | flops | bytes accessed | tf_op | source)
XLA Modules:
  0.0 862.1 jit_solution(5011642923617534919)
XLA Ops:
  14.0 5.6 collective-permute-start
  21.5 4.5 collective-permute-start.2
  26.1 39.7 %collective-permute-done.1 = bf16[64,4096]{1,0:T(8,128)(2,1)S(1)} collective-permute-done((bf16[64,4096]{1,0:T(8,128)(2,1)}, bf16[64,4096]{1,0:T(8,128)(2,1)S(1)}, u32[]{:S(2)}, u32[]{:S(2)}) %collective-permute-start.1) | collective-permute-done | bytes 524320 | tf_op jit(solution)/shard_map/ppermute | solution.py:291
  65.8 6.5 collective-permute-done.2
  75.3 23.6 %collective-permute-done.5 = bf16[1,256,1024]{2,1,0:T(8,128)(2,1)S(1)} collective-permute-done((bf16[1,256,1024]{2,1,0:T(8,128)(2,1)S(1)}, bf16[1,256,1024]{2,1,0:T(8,128)(2,1)S(1)}, u32[]{:S(2)}, u32[]{:S(2)}) %collective-permute-start.5) | collective-permute-done | bytes 524320 | tf_op jit(solution)/shard_map/ppermute | solution.py:350
  100.8 12.2 %collective-permute-done.8 = bf16[2,256,1024]{2,1,0:T(8,128)(2,1)S(1)} collective-permute-done((bf16[2,256,1024]{2,1,0:T(8,128)(2,1)S(1)}, bf16[2,256,1024]{2,1,0:T(8,128)(2,1)S(1)}, u32[]{:S(2)}, u32[]{:S(2)}) %collective-permute-start.8) | collective-permute-done | bytes 1048608 | tf_op jit(solution)/shard_map/ppermute | solution.py:350
  114.5 4.1 collective-permute-done.7
  123.0 36.6 %collective-permute-done.10.refs_5_ = bf16[4,64,4096]{2,1,0:T(8,128)(2,1)S(1)} collective-permute-done((bf16[4,64,4096]{2,1,0:T(8,128)(2,1)S(1)}, bf16[4,64,4096]{2,1,0:T(8,128)(2,1)S(1)}, u32[]{:S(2)}, u32[]{:S(2)}) %collective-permute-start.10) | collective-permute-done | bytes 2097184 | tf_op jit(solution)/shard_map/ppermute | solution.py:350
  161.4 8.8 %collective-permute-done.11.refs_9_ = bf16[4,256,1024]{2,1,0:T(8,128)(2,1)} collective-permute-done((bf16[4,256,1024]{2,1,0:T(8,128)(2,1)}, bf16[4,256,1024]{2,1,0:T(8,128)(2,1)}, u32[]{:S(2)}, u32[]{:S(2)}) %collective-permute-start.11) | collective-permute-done | bytes 2097184 | tf_op jit(solution)/shard_map/ppermute | solution.py:350
  174.1 4.9 collective-permute-start.15
  181.4 22.8 %weave.1 = (bf16[1024,3072]{1,0:T(8,128)(2,1)}, bf16[1024,1024]{1,0:T(8,128)(2,1)S(1)}, bf16[1024,128]{1,0:T(8,128)(2,1)S(1)}, bf16[1024,4096]{1,0:T(8,128)(2,1)}, bf16[4096,1024]{1,0:T(8,128)(2,1)}) custom-call(s32[3,16]{1,0:T(4,128)S(1)} %pad_add_fusion.place_ref, bf16[4,64,4224]{2,1,0:T(8,128)(2,1)} %pad_maximum_fusion.6.refs_0_, ...), custom_call_target="tpu_custom_call" | custom-call | bytes 50855936 | tf_op jit(solution)/shard_map/weave/pallas_call | solution.py:442
  205.7 6.9 collective-permute-done.15
  212.6 6.5 add_convert_fusion.6.q_ref.k_ref.v_ref
  223.0 2.9 collective-permute-start.19
  228.5 13.2 %attend_fwd.3 = bf16[512,1024]{1,0:T(8,128)(2,1)S(1)} custom-call(s32[1]{0:T(128)} %bitcast.47.causal_ref, s32[2,256,1]{2,1,0:T(8,128)S(1)} %broadcast_in_dim_reshape.19.key_ref, s32[2,1,256]{2,1,0:T(1,128)S(1)} %bitcast.286, bf16[512,3072]{1,0:T(8,128)(2,1)S(1)} %add_convert_fusion.6.q_ref.k_ref.v_ref, ...), custom_call_target="tpu_custom_call" | custom-call | flops 536870912 | bytes 4194304 | tf_op jit(solution)/shard_map/attend_fwd/pallas_call | solution.py:154
  241.8 2.9 fusion.162
  246.5 4.2 fusion.246
  252.9 23.1 %conditional.5 = (bf16[512,1024]{1,0:T(8,128)(2,1)S(1)}, bf16[512,4096]{1,0:T(8,128)(2,1)}, bf16[512,4096]{1,0:T(8,128)(2,1)}, f32[512,1024]{1,0:T(8,128)S(1)}, f32[512,1]{0,1:T(1,128)}) conditional(s32[]{:T(128)} %convert_element_type.566, () %tuple.98, (bf16[512,1024]{1,0:T(8,128)(2,1)}, bf16[1024,4096]{1,0:T(8,128)(2,1)}, f32[16,256]{1,0:T(8,128)S(1)}, ...), branch_computations={%region_2.3_spmd, %region_3.6_spmd} | conditional | flops 8620868608 | bytes 50518168 | solution.py:670
  253.1 12.2 %fusion.4 = (bf16[512,4096]{1,0:T(8,128)(2,1)}, bf16[512,4096]{1,0:T(8,128)(2,1)}) fusion(f32[4096]{0:T(1024)S(1)} %bitcast.303, bf16[512,1024]{1,0:T(8,128)(2,1)} %get-tuple-element.126, bf16[1024,4096]{1,0:T(8,128)(2,1)} %get-tuple-element.127), kind=kOutput, calls=%fused_computation.6 | convolution fusion | flops 4320133120 | bytes 17842176 | tf_op jit(solution)/shard_map/cond/branch_1_fun/dot_general | solution.py:20
  265.4 8.4 fusion.247
  278.2 34.9 %collective-permute-done.22 = bf16[512,1024]{1,0:T(8,128)(2,1)} collective-permute-done((bf16[512,1024]{1,0:T(8,128)(2,1)S(1)}, bf16[512,1024]{1,0:T(8,128)(2,1)}, u32[]{:S(2)}, u32[]{:S(2)}) %collective-permute-start.22) | collective-permute-done | bytes 1048608 | tf_op jit(solution)/shard_map/ppermute | solution.py:329
  313.1 16.9 %conditional.6 = (bf16[512,1024]{1,0:T(8,128)(2,1)}, bf16[512,1024]{1,0:T(8,128)(2,1)S(1)}, bf16[512,1024]{1,0:T(8,128)(2,1)}, bf16[512,4096]{1,0:T(8,128)(2,1)}...) conditional(s32[]{:T(128)} %convert_element_type.566, ...), branch_computations={%region_6.22_spmd, %region_22.23_spmd} | conditional | flops 26658598912 | bytes 209142640 | solution.py:725
  331.0 61.5 %conditional.7 = (bf16[8,5]{1,0:T(8,128)(2,1)S(1)}, bf16[256,768]{1,0:T(8,128)(2,1)S(1)}, f32[]{:T(128)}, bf16[8,12288]{1,0:T(8,128)(2,1)}, bf16[96,1536]{1,0:T(...) conditional(s32[]{:T(128)} %convert_element_type.566, ...), branch_computations={%region_23.24_spmd, %region_24.49_spmd} | conditional | flops 1519001600 | bytes 49347288 | solution.py:670
  344.9 3.1 multiply_convert_fusion.6
  368.3 3.8 multiply_reduce_fusion.11
  393.2 59.6 %collective-permute-start.26 = (bf16[512,1024]{1,0:T(8,128)(2,1)}, bf16[512,1024]{1,0:T(8,128)(2,1)S(1)}, u32[]{:S(2)}, u32[]{:S(2)}) collective-permute-start(bf16[512,1024]{1,0:T(8,128)(2,1)} %get-tuple-element.469), channel_id=1, source_target_pairs={{0,0},{16,8},{1,1},{17,9},{2,2},{18,10},{3,3},{19,11},{4,4},{20,12... | collective-permute-start | bytes 3145736 | tf_op jit(solution)/shard_map/ppermute | solution.py:291
  458.1 5.0 collective-permute-start.25
  470.0 7.4 collective-permute-done.23
  477.4 6.0 conditional.8
  477.4 4.4 reshape.759
  483.4 23.8 %conditional.9 = ((bf16[512,1024]{1,0:T(8,128)(2,1)}, bf16[512,4096]{1,0:T(8,128)(2,1)}, f32[512,1024]{1,0:T(8,128)}, f32[1024]{0:T(1024)}, f32[1024]{0:T(1024)})) conditional(s32[]{:T(128)} %convert_element_type.566, (bf16[512,1024]{1,0:T(8,128)(2,1)}, bf16[512,4096]{1,0:T(8,128)(2,1)}, f32[512,1024]{1,0:T(8,128)}, f32[1024]{0:T(1024)}, ...), branch_computations={%region_51.52_spmd, %region_52.57_spmd} | conditional | flops 8607758336 | bytes 72405152 | solution.py:805
  486.7 9.2 %multiply_convert_fusion.1 = bf16[512,4096]{1,0:T(8,128)(2,1)S(1)} fusion(bf16[512,4096]{1,0:T(8,128)(2,1)} %get-tuple-element.167, bf16[512,1024]{1,0:T(8,128)(2,1)S(1)} %fusion.17, bf16[4096,1024]{1,0:T(8,128)(2,1)} %get-tuple-element.166), kind=kOutput, calls=%fused_computation.22 | convolution fusion | flops 4301258752 | bytes 17825792 | tf_op jit(solution)/shard_map/cond/branch_1_fun/dot_general | solution.py:28
  495.9 10.9 %convolution_add_fusion = f32[512,1024]{1,0:T(8,128)} fusion(bf16[512,4096]{1,0:T(8,128)(2,1)S(1)} %multiply_convert_fusion.1, bf16[1024,4096]{1,0:T(8,128)(2,1)} %get-tuple-element.168, f32[512,1024]{1,0:T(8,128)S(1)} %get-tuple-element.165, f32[512]{0:T(512)S(1)} %get-tuple-element.606, f32[512]{0:T(512)S(1)} %get-tuple-element.607, ...), kind=kOutput, calls=%fused_computation.33 | convolution fusion | flops 4298637312 | bytes 17836032 | tf_op jit(solution)/shard_map/cond/branch_1_fun/dot_general | solution.py:28
  507.2 6.4 convolution_convert_fusion.10
  513.7 4.4 convolution_convert_fusion.9
  518.6 4.9 dynamic-slice_bitcast_fusion
  532.0 2.8 convert_reduce_fusion.15
  537.1 10.7 %collective-permute-done.30 = bf16[512,1024]{1,0:T(8,128)(2,1)S(1)} collective-permute-done((bf16[512,1024]{1,0:T(8,128)(2,1)}, bf16[512,1024]{1,0:T(8,128)(2,1)S(1)}, u32[]{:S(2)}, u32[]{:S(2)}) %collective-permute-start.30) | collective-permute-done | bytes 1048608 | tf_op jit(solution)/shard_map/ppermute | solution.py:291
  548.8 5.0 fusion.125
  558.7 5.3 add_convert_fusion.4
  567.1 27.5 %collective-permute-start.32 = (bf16[1,2,2,256,1024]{4,3,2,1,0:T(8,128)(2,1)}, bf16[1,2,2,256,1024]{4,3,2,1,0:T(8,128)(2,1)}, u32[]{:S(2)}, u32[]{:S(2)}) collective-permute-start(bf16[1,2,2,256,1024]{4,3,2,1,0:T(8,128)(2,1)} %constant_dynamic-slice_fusion.20), channel_id=1, source_target_pairs={{0,4},{1,5},{2,6},{3,7},{4,0},{5,1},{6,2},{7,3},{8,12},{9,13},{10,... | collective-permute-start | bytes 6291464 | tf_op jit(solution)/shard_map/ppermute | solution.py:350
  594.6 4.7 add_convert_fusion.5
  603.9 3.3 convert_reduce_fusion.12
  612.9 21.4 %attend_bwd.3 = bf16[512,3072]{1,0:T(8,128)(2,1)S(1)} custom-call(s32[1]{0:T(128)} %bitcast.47.causal_ref, s32[2,256,1]{2,1,0:T(8,128)S(1)} %broadcast_in_dim_reshape.19.key_ref, s32[2,1,256]{2,1,0:T(1,128)S(1)} %bitcast.287, bf16[512,3072]{1,0:T(8,128)(2,1)} %copy-done, bf16[512,3072]{1,0:T(8,128)(2,1)} %copy-done, bf16[512,3072]{1,0:T(8,128)(2,1)} %copy-done, ...), custom_call_target="tpu_custom_call" | custom-call | flops 1342177280 | bytes 7340032 | tf_op jit(solution)/shard_map/attend_bwd/pallas_call | solution.py:170
  635.4 5.7 reshape.890
  643.8 4.4 add_convert_fusion.7
  648.2 4.2 add_convert_fusion.8
  652.4 3.7 add_convert_fusion.9
  657.8 7.8 add_convert_fusion.11
  673.2 3.3 convolution_convert_fusion.11
  676.5 3.3 convolution_convert_fusion.12
  680.7 19.6 %collective-permute-done.35 = bf16[1,2,1,256,1024]{4,3,2,1,0:T(8,128)(2,1)} collective-permute-done((bf16[1,2,1,256,1024]{4,3,2,1,0:T(8,128)(2,1)}, bf16[1,2,1,256,1024]{4,3,2,1,0:T(8,128)(2,1)}, u32[]{:S(2)}, u32[]{:S(2)}) %collective-permute-start.35) | collective-permute-done | bytes 1048608 | tf_op jit(solution)/shard_map/ppermute | solution.py:350
  701.1 3.4 collective-permute-done.34
  722.3 3.8 collective-permute-done.44
  726.1 9.3 %collective-permute-start.46 = (bf16[512,1024]{1,0:T(8,128)(2,1)S(1)}, bf16[512,1024]{1,0:T(8,128)(2,1)}, u32[]{:S(2)}, u32[]{:S(2)}) collective-permute-start(bf16[512,1024]{1,0:T(8,128)(2,1)S(1)} %copy-done.128), channel_id=1, source_target_pairs={{0,0},{16,8},{8,16},{24,24},{1,1},{17,9},{9,17},{25,25},{2,2},{18,... | collective-permute-start | bytes 3145736 | tf_op jit(solution)/shard_map/ppermute | solution.py:291
  737.5 3.8 collective-permute-done.42
  743.1 16.2 %collective-permute-done.46 = bf16[512,1024]{1,0:T(8,128)(2,1)} collective-permute-done((bf16[512,1024]{1,0:T(8,128)(2,1)S(1)}, bf16[512,1024]{1,0:T(8,128)(2,1)}, u32[]{:S(2)}, u32[]{:S(2)}) %collective-permute-start.46) | collective-permute-done | bytes 1048608 | tf_op jit(solution)/shard_map/ppermute | solution.py:291
  762.7 2.8 convert.38
  765.6 10.1 %collective-permute-done.64 = bf16[32,4096]{1,0:T(8,128)(2,1)S(1)} collective-permute-done((bf16[32,4096]{1,0:T(8,128)(2,1)S(1)}, bf16[32,4096]{1,0:T(8,128)(2,1)S(1)}, u32[]{:S(2)}, u32[]{:S(2)}) %collective-permute-start.64) | collective-permute-done | bytes 262176 | tf_op jit(solution)/shard_map/ppermute | solution.py:332
  775.7 3.1 collective-permute-start.49
  782.3 4.5 collective-permute-start.62
  797.2 3.2 fusion.145
  824.0 11.3 %collective-permute-start.60 = (bf16[64,4096]{1,0:T(8,128)(2,1)S(1)}, bf16[64,4096]{1,0:T(8,128)(2,1)S(1)}, u32[]{:S(2)}, u32[]{:S(2)}) collective-permute-start(bf16[64,4096]{1,0:T(8,128)(2,1)S(1)} %pad_maximum_fusion.13), channel_id=1, source_target_pairs={{0,0},{16,8},{8,16},{24,24},{1,1},{17,9},{9,17},{25,25},{2,2},{18,... | collective-permute-start | bytes 1572872 | tf_op jit(solution)/shard_map/ppermute | solution.py:291
  842.2 5.1 collective-permute-done.61
  (703 shorter events, 249.4 us)
Async XLA Ops:
  7.2 113.3 %all-gather.6.cloned.1.call-start = ((), (), s32[]{:S(2)}) async-start(), calls=%async_computation | async-start | bytes 8921088 | tf_op jit(solution)/shard_map/all_gather | solution.py:612
  9.8 320.3 %all-gather.8.cloned.1.call-start = ((), (), s32[]{:S(2)}) async-start(), calls=%async_computation.1 | async-start | bytes 14800896 | tf_op jit(solution)/shard_map/all_gather | solution.py:626
  14.0 58.3 %collective-permute-start = (bf16[64,4224]{1,0:T(8,128)(2,1)S(1)}, bf16[64,4224]{1,0:T(8,128)(2,1)S(1)}, u32[]{:S(2)}, u32[]{:S(2)}) collective-permute-start(bf16[64,4224]{1,0:T(8,128)(2,1)S(1)} %pad_maximum_fusion.12), channel_id=1, source_target_pairs={{0,0},{16,8},{8,16},{24,24},{1,1},{17,9},{9,17},{25,25},{2,2},{18,... | collective-permute-start | bytes 1622024 | tf_op jit(solution)/shard_map/ppermute | solution.py:291
  19.6 46.2 %collective-permute-start.1 = (bf16[64,4096]{1,0:T(8,128)(2,1)}, bf16[64,4096]{1,0:T(8,128)(2,1)S(1)}, u32[]{:S(2)}, u32[]{:S(2)}) collective-permute-start(bf16[64,4096]{1,0:T(8,128)(2,1)} %bitcast.323), channel_id=1, source_target_pairs={{0,0},{16,8},{8,16},{24,24},{1,1},{17,9},{9,17},{25,25},{2,2},{18,... | collective-permute-start | bytes 1572872 | tf_op jit(solution)/shard_map/ppermute | solution.py:291
  21.5 50.8 %collective-permute-start.2 = (bf16[256,1024]{1,0:T(8,128)(2,1)}, bf16[256,1024]{1,0:T(8,128)(2,1)S(1)}, u32[]{:S(2)}, u32[]{:S(2)}) collective-permute-start(bf16[256,1024]{1,0:T(8,128)(2,1)} %bitcast.324), channel_id=1, source_target_pairs={{0,0},{16,8},{8,16},{24,24},{1,1},{17,9},{9,17},{25,25},{2,2},{18,... | collective-permute-start | bytes 1572872 | tf_op jit(solution)/shard_map/ppermute | solution.py:291
  72.3 26.6 %collective-permute-start.5 = (bf16[1,256,1024]{2,1,0:T(8,128)(2,1)S(1)}, bf16[1,256,1024]{2,1,0:T(8,128)(2,1)S(1)}, u32[]{:S(2)}, u32[]{:S(2)}) collective-permute-start(bf16[1,256,1024]{2,1,0:T(8,128)(2,1)S(1)} %bitcast.267), channel_id=1, source_target_pairs={{0,4},{1,5},{2,6},{3,7},{4,0},{5,1},{6,2},{7,3},{8,12},{9,13},{10,... | collective-permute-start | bytes 1572872 | tf_op jit(solution)/shard_map/ppermute | solution.py:350
  72.8 26.2 %collective-permute-start.4 = (bf16[1,64,4096]{2,1,0:T(8,128)(2,1)S(1)}, bf16[1,64,4096]{2,1,0:T(8,128)(2,1)S(1)}, u32[]{:S(2)}, u32[]{:S(2)}) collective-permute-start(bf16[1,64,4096]{2,1,0:T(8,128)(2,1)S(1)} %bitcast.265), channel_id=1, source_target_pairs={{0,2},{1,3},{2,0},{3,1},{4,6},{5,7},{6,4},{7,5},{8,10},{9,11},{10,... | collective-permute-start | bytes 1572872 | tf_op jit(solution)/shard_map/ppermute | solution.py:350
  74.0 25.1 %collective-permute-start.3 = (bf16[1,64,4224]{2,1,0:T(8,128)(2,1)S(1)}, bf16[1,64,4224]{2,1,0:T(8,128)(2,1)S(1)}, u32[]{:S(2)}, u32[]{:S(2)}) collective-permute-start(bf16[1,64,4224]{2,1,0:T(8,128)(2,1)S(1)} %bitcast.263), channel_id=1, source_target_pairs={{0,1},{1,0},{2,3},{3,2},{4,5},{5,4},{6,7},{7,6},{8,9},{9,8},{10,11... | collective-permute-start | bytes 1622024 | tf_op jit(solution)/shard_map/ppermute | solution.py:350
  99.2 13.7 %collective-permute-start.8 = (bf16[2,256,1024]{2,1,0:T(8,128)(2,1)S(1)}, bf16[2,256,1024]{2,1,0:T(8,128)(2,1)S(1)}, u32[]{:S(2)}, u32[]{:S(2)}) collective-permute-start(bf16[2,256,1024]{2,1,0:T(8,128)(2,1)S(1)} %pad_maximum_fusion.11), channel_id=1, source_target_pairs={{0,1},{1,0},{2,3},{3,2},{4,5},{5,4},{6,7},{7,6},{8,9},{9,8},{10,11... | collective-permute-start | bytes 3145736 | tf_op jit(solution)/shard_map/ppermute | solution.py:350
  99.6 19.0 %collective-permute-start.7 = (bf16[2,64,4096]{2,1,0:T(8,128)(2,1)S(1)}, bf16[2,64,4096]{2,1,0:T(8,128)(2,1)S(1)}, u32[]{:S(2)}, u32[]{:S(2)}) collective-permute-start(bf16[2,64,4096]{2,1,0:T(8,128)(2,1)S(1)} %pad_maximum_fusion.10), channel_id=1, source_target_pairs={{0,4},{1,5},{2,6},{3,7},{4,0},{5,1},{6,2},{7,3},{8,12},{9,13},{10,... | collective-permute-start | bytes 3145736 | tf_op jit(solution)/shard_map/ppermute | solution.py:350
  99.6 19.3 %collective-permute-start.6 = (bf16[2,64,4224]{2,1,0:T(8,128)(2,1)S(1)}, bf16[2,64,4224]{2,1,0:T(8,128)(2,1)S(1)}, u32[]{:S(2)}, u32[]{:S(2)}) collective-permute-start(bf16[2,64,4224]{2,1,0:T(8,128)(2,1)S(1)} %pad_maximum_fusion.9), channel_id=1, source_target_pairs={{0,2},{1,3},{2,0},{3,1},{4,6},{5,7},{6,4},{7,5},{8,10},{9,11},{10,... | collective-permute-start | bytes 3244040 | tf_op jit(solution)/shard_map/ppermute | solution.py:350
  120.5 39.1 %collective-permute-start.10 = (bf16[4,64,4096]{2,1,0:T(8,128)(2,1)S(1)}, bf16[4,64,4096]{2,1,0:T(8,128)(2,1)S(1)}, u32[]{:S(2)}, u32[]{:S(2)}) collective-permute-start(bf16[4,64,4096]{2,1,0:T(8,128)(2,1)S(1)} %pad_maximum_fusion.7.refs_4_), channel_id=1, source_target_pairs={{0,1},{1,0},{2,3},{3,2},{4,5},{5,4},{6,7},{7,6},{8,9},{9,8},{10,11... | collective-permute-start | bytes 6291464 | tf_op jit(solution)/shard_map/ppermute | solution.py:350
  121.3 48.9 %collective-permute-start.12 = (bf16[4,64,4224]{2,1,0:T(8,128)(2,1)}, bf16[4,64,4224]{2,1,0:T(8,128)(2,1)}, u32[]{:S(2)}, u32[]{:S(2)}) collective-permute-start(bf16[4,64,4224]{2,1,0:T(8,128)(2,1)} %pad_maximum_fusion.6.refs_0_), channel_id=1, source_target_pairs={{0,16},{16,0},{1,17},{17,1},{2,18},{18,2},{3,19},{19,3},{4,20},{20... | collective-permute-start | bytes 6488072 | tf_op jit(solution)/shard_map/ppermute | solution.py:291
  121.3 48.9 %collective-permute-start.9 = (bf16[4,64,4224]{2,1,0:T(8,128)(2,1)}, bf16[4,64,4224]{2,1,0:T(8,128)(2,1)}, u32[]{:S(2)}, u32[]{:S(2)}) collective-permute-start(bf16[4,64,4224]{2,1,0:T(8,128)(2,1)} %pad_maximum_fusion.6.refs_0_), channel_id=1, source_target_pairs={{0,4},{1,5},{2,6},{3,7},{4,0},{5,1},{6,2},{7,3},{8,12},{9,13},{10,... | collective-permute-start | bytes 6488072 | tf_op jit(solution)/shard_map/ppermute | solution.py:350
  121.8 48.4 %collective-permute-start.13 = (bf16[4,64,4096]{2,1,0:T(8,128)(2,1)S(1)}, bf16[4,64,4096]{2,1,0:T(8,128)(2,1)}, u32[]{:S(2)}, u32[]{:S(2)}) collective-permute-start(bf16[4,64,4096]{2,1,0:T(8,128)(2,1)S(1)} %pad_maximum_fusion.7.refs_4_), channel_id=1, source_target_pairs={{0,16},{16,0},{1,17},{17,1},{2,18},{18,2},{3,19},{19,3},{4,20},{20... | collective-permute-start | bytes 6291464 | tf_op jit(solution)/shard_map/ppermute | solution.py:291
  122.6 47.6 %collective-permute-start.11 = (bf16[4,256,1024]{2,1,0:T(8,128)(2,1)}, bf16[4,256,1024]{2,1,0:T(8,128)(2,1)}, u32[]{:S(2)}, u32[]{:S(2)}) collective-permute-start(bf16[4,256,1024]{2,1,0:T(8,128)(2,1)} %pad_maximum_fusion.8.refs_8_), channel_id=1, source_target_pairs={{0,2},{1,3},{2,0},{3,1},{4,6},{5,7},{6,4},{7,5},{8,10},{9,11},{10,... | collective-permute-start | bytes 6291464 | tf_op jit(solution)/shard_map/ppermute | solution.py:350
  170.2 465.2 %all-gather.12.cloned.1.call-start = ((), (), s32[]{:S(2)}) async-start(), calls=%async_computation.3 | async-start | bytes 3244032 | tf_op jit(solution)/shard_map/all_gather | solution.py:774
  170.3 11.1 %collective-permute-start.16 = (bf16[4,64,4224]{2,1,0:T(8,128)(2,1)}, bf16[4,64,4224]{2,1,0:T(8,128)(2,1)}, u32[]{:S(2)}, u32[]{:S(2)}) collective-permute-start(bf16[4,64,4224]{2,1,0:T(8,128)(2,1)} %collective-permute-done.9.refs_1_), channel_id=1, source_target_pairs={{0,16},{16,0},{1,17},{17,1},{2,18},{18,2},{3,19},{19,3},{4,20},{20... | collective-permute-start | bytes 6488072 | tf_op jit(solution)/shard_map/ppermute | solution.py:291
  171.3 10.1 %collective-permute-start.18 = (bf16[4,256,1024]{2,1,0:T(8,128)(2,1)}, bf16[4,256,1024]{2,1,0:T(8,128)(2,1)}, u32[]{:S(2)}, u32[]{:S(2)}) collective-permute-start(bf16[4,256,1024]{2,1,0:T(8,128)(2,1)} %collective-permute-done.11.refs_9_), channel_id=1, source_target_pairs={{0,16},{16,0},{1,17},{17,1},{2,18},{18,2},{3,19},{19,3},{4,20},{20... | collective-permute-start | bytes 6291464 | tf_op jit(solution)/shard_map/ppermute | solution.py:291
  174.1 38.6 %collective-permute-start.15 = (bf16[512,1024]{1,0:T(8,128)(2,1)}, bf16[512,1024]{1,0:T(8,128)(2,1)}, u32[]{:S(2)}, u32[]{:S(2)}) collective-permute-start(bf16[512,1024]{1,0:T(8,128)(2,1)} %bitcast.321), channel_id=1, source_target_pairs={{0,0},{16,8},{8,16},{24,24},{1,1},{17,9},{9,17},{25,25},{2,2},{18,... | collective-permute-start | bytes 3145736 | tf_op jit(solution)/shard_map/ppermute | solution.py:291
  223.0 29.8 %collective-permute-start.19 = (bf16[512,1024]{1,0:T(8,128)(2,1)}, bf16[512,1024]{1,0:T(8,128)(2,1)}, u32[]{:S(2)}, u32[]{:S(2)}) collective-permute-start(bf16[512,1024]{1,0:T(8,128)(2,1)} %bitcast.322), channel_id=1, source_target_pairs={{24,24},{16,8},{25,25},{17,9},{26,26},{18,10},{27,27},{19,11},{28,... | collective-permute-start | bytes 3145736 | tf_op jit(solution)/shard_map/ppermute | solution.py:291
  225.9 26.9 %collective-permute-start.21 = (bf16[256,768]{1,0:T(8,128)(2,1)}, bf16[256,768]{1,0:T(8,128)(2,1)}, u32[]{:S(2)}, u32[]{:S(2)}) collective-permute-start(bf16[256,768]{1,0:T(8,128)(2,1)} %bitcast.325), channel_id=1, source_target_pairs={{0,0},{8,16},{1,1},{9,17},{2,2},{10,18},{3,3},{11,19},{4,4},{12,20... | collective-permute-start | bytes 1179656 | tf_op jit(solution)/shard_map/ppermute | solution.py:291
  227.2 25.6 %collective-permute-start.20 = (f32[33,768]{1,0:T(8,128)}, f32[33,768]{1,0:T(8,128)S(1)}, u32[]{:S(2)}, u32[]{:S(2)}) collective-permute-start(f32[33,768]{1,0:T(8,128)} %pad_maximum_fusion.16), channel_id=1, source_target_pairs={{0,0},{8,16},{1,1},{9,17},{2,2},{10,18},{3,3},{11,19},{4,4},{12,20... | collective-permute-start | bytes 304136 | tf_op jit(solution)/shard_map/ppermute | solution.py:291
  276.0 37.1 %collective-permute-start.22 = (bf16[512,1024]{1,0:T(8,128)(2,1)S(1)}, bf16[512,1024]{1,0:T(8,128)(2,1)}, u32[]{:S(2)}, u32[]{:S(2)}) collective-permute-start(bf16[512,1024]{1,0:T(8,128)(2,1)S(1)} %get-tuple-element.398), channel_id=1, source_target_pairs={{0,8},{1,9},{2,10},{3,11},{4,12},{5,13},{6,14},{7,15},{16,24},{17,... | collective-permute-start | bytes 3145736 | tf_op jit(solution)/shard_map/ppermute | solution.py:329
  393.2 76.8 %collective-permute-start.26 = (bf16[512,1024]{1,0:T(8,128)(2,1)}, bf16[512,1024]{1,0:T(8,128)(2,1)S(1)}, u32[]{:S(2)}, u32[]{:S(2)}) collective-permute-start(bf16[512,1024]{1,0:T(8,128)(2,1)} %get-tuple-element.469), channel_id=1, source_target_pairs={{0,0},{16,8},{1,1},{17,9},{2,2},{18,10},{3,3},{19,11},{4,4},{20,12... | collective-permute-start | bytes 3145736 | tf_op jit(solution)/shard_map/ppermute | solution.py:291
  452.9 24.5 %collective-permute-start.23 = (bf16[512,1024]{1,0:T(8,128)(2,1)}, bf16[512,1024]{1,0:T(8,128)(2,1)S(1)}, u32[]{:S(2)}, u32[]{:S(2)}) collective-permute-start(bf16[512,1024]{1,0:T(8,128)(2,1)} %copy-done.129), channel_id=1, source_target_pairs={{8,0},{9,1},{10,2},{11,3},{12,4},{13,5},{14,6},{15,7},{24,16},{25,... | collective-permute-start | bytes 3145736 | tf_op jit(solution)/shard_map/ppermute | solution.py:332
  458.1 11.9 %collective-permute-start.25 = (bf16[48,1536]{1,0:T(8,128)(2,1)S(1)}, bf16[48,1536]{1,0:T(8,128)(2,1)S(1)}, u32[]{:S(2)}, u32[]{:S(2)}) collective-permute-start(bf16[48,1536]{1,0:T(8,128)(2,1)S(1)} %slice.488), channel_id=1, source_target_pairs={{0,8},{1,9},{2,10},{3,11},{4,12},{5,13},{6,14},{7,15},{16,24},{17,... | collective-permute-start | bytes 442376 | tf_op jit(solution)/shard_map/ppermute | solution.py:329
  513.7 34.2 %collective-permute-start.28 = (bf16[2048,1024]{1,0:T(8,128)(2,1)}, bf16[2048,1024]{1,0:T(8,128)(2,1)}, u32[]{:S(2)}, u32[]{:S(2)}) collective-permute-start(bf16[2048,1024]{1,0:T(8,128)(2,1)} %convolution_convert_fusion.10), channel_id=1, source_target_pairs={{0,16},{16,0},{1,17},{17,1},{2,18},{18,2},{3,19},{19,3},{4,20},{20... | collective-permute-start | bytes 12582920 | tf_op jit(solution)/shard_map/ppermute | solution.py:291
  518.1 29.7 %collective-permute-start.27 = (bf16[512,4096]{1,0:T(8,128)(2,1)}, bf16[512,4096]{1,0:T(8,128)(2,1)}, u32[]{:S(2)}, u32[]{:S(2)}) collective-permute-start(bf16[512,4096]{1,0:T(8,128)(2,1)} %convolution_convert_fusion.9), channel_id=1, source_target_pairs={{0,16},{16,0},{1,17},{17,1},{2,18},{18,2},{3,19},{19,3},{4,20},{20... | collective-permute-start | bytes 12582920 | tf_op jit(solution)/shard_map/ppermute | solution.py:291
  523.5 25.3 %collective-permute-start.29 = (bf16[512,4096]{1,0:T(8,128)(2,1)}, bf16[512,4096]{1,0:T(8,128)(2,1)}, u32[]{:S(2)}, u32[]{:S(2)}) collective-permute-start(bf16[512,4096]{1,0:T(8,128)(2,1)} %dynamic-slice_bitcast_fusion), channel_id=1, source_target_pairs={{8,24},{24,8},{9,25},{25,9},{10,26},{26,10},{11,27},{27,11},{12,28... | collective-permute-start | bytes 12582920 | tf_op jit(solution)/shard_map/ppermute | solution.py:291
  527.9 231.3 %all-gather.10.cloned.1.call-start = ((), (), s32[]{:S(2)}) async-start(), calls=%async_computation.2 | async-start | bytes 4866048 | tf_op jit(solution)/shard_map/all_gather | solution.py:774
  530.6 17.2 %collective-permute-start.30 = (bf16[512,1024]{1,0:T(8,128)(2,1)}, bf16[512,1024]{1,0:T(8,128)(2,1)S(1)}, u32[]{:S(2)}, u32[]{:S(2)}) collective-permute-start(bf16[512,1024]{1,0:T(8,128)(2,1)} %get-tuple-element.469), channel_id=1, source_target_pairs={{24,24},{8,16},{25,25},{9,17},{26,26},{10,18},{27,27},{11,19},{28,... | collective-permute-start | bytes 3145736 | tf_op jit(solution)/shard_map/ppermute | solution.py:291
  556.5 84.7 %collective-permute-start.33 = (bf16[2,2,2,1,32,4096]{5,4,3,2,1,0:T(8,128)(2,1)}, bf16[2,2,2,1,32,4096]{5,4,3,2,1,0:T(8,128)(2,1)}, u32[]{:S(2)}, u32[]{:S(2)}) collective-permute-start(bf16[2,2,2,1,32,4096]{5,4,3,2,1,0:T(8,128)(2,1)} %constant_dynamic-slice_fusion.19), channel_id=1, source_target_pairs={{8,9},{9,8},{10,11},{11,10},{12,13},{13,12},{14,15},{15,14},{24,25... | collective-permute-start | bytes 6291464 | tf_op jit(solution)/shard_map/ppermute | solution.py:350
  567.1 74.1 %collective-permute-start.32 = (bf16[1,2,2,256,1024]{4,3,2,1,0:T(8,128)(2,1)}, bf16[1,2,2,256,1024]{4,3,2,1,0:T(8,128)(2,1)}, u32[]{:S(2)}, u32[]{:S(2)}) collective-permute-start(bf16[1,2,2,256,1024]{4,3,2,1,0:T(8,128)(2,1)} %constant_dynamic-slice_fusion.20), channel_id=1, source_target_pairs={{0,4},{1,5},{2,6},{3,7},{4,0},{5,1},{6,2},{7,3},{8,12},{9,13},{10,... | collective-permute-start | bytes 6291464 | tf_op jit(solution)/shard_map/ppermute | solution.py:350
  601.8 42.0 %collective-permute-start.31 = (bf16[2,1,2,64,4096]{4,3,2,1,0:T(8,128)(2,1)}, bf16[2,1,2,64,4096]{4,3,2,1,0:T(8,128)(2,1)}, u32[]{:S(2)}, u32[]{:S(2)}) collective-permute-start(bf16[2,1,2,64,4096]{4,3,2,1,0:T(8,128)(2,1)} %constant_dynamic-slice_fusion.21), channel_id=1, source_target_pairs={{0,2},{1,3},{2,0},{3,1},{4,6},{5,7},{6,4},{7,5},{8,10},{9,11},{10,... | collective-permute-start | bytes 6291464 | tf_op jit(solution)/shard_map/ppermute | solution.py:350
  609.2 100.5 %collective-permute-start.39 = (bf16[512,1024]{1,0:T(8,128)(2,1)}, bf16[512,1024]{1,0:T(8,128)(2,1)}, u32[]{:S(2)}, u32[]{:S(2)}) collective-permute-start(bf16[512,1024]{1,0:T(8,128)(2,1)} %convolution_convert_fusion.14), channel_id=1, source_target_pairs={{0,16},{16,0},{1,17},{17,1},{2,18},{18,2},{3,19},{19,3},{4,20},{20... | collective-permute-start | bytes 3145736 | tf_op jit(solution)/shard_map/ppermute | solution.py:291
  665.7 14.1 %collective-permute-start.40 = (f32[8,1665]{1,0:T(8,128)S(1)}, f32[8,1665]{1,0:T(8,128)S(1)}, u32[]{:S(2)}, u32[]{:S(2)}) collective-permute-start(f32[8,1665]{1,0:T(8,128)S(1)} %dynamic-slice_bitcast_fusion.1), channel_id=1, source_target_pairs={{0,16},{16,0},{1,17},{17,1},{2,18},{18,2},{3,19},{19,3},{4,20},{20... | collective-permute-start | bytes 159848 | tf_op jit(solution)/shard_map/ppermute | solution.py:291
  668.2 32.1 %collective-permute-start.35 = (bf16[1,2,1,256,1024]{4,3,2,1,0:T(8,128)(2,1)}, bf16[1,2,1,256,1024]{4,3,2,1,0:T(8,128)(2,1)}, u32[]{:S(2)}, u32[]{:S(2)}) collective-permute-start(bf16[1,2,1,256,1024]{4,3,2,1,0:T(8,128)(2,1)} %constant_dynamic-slice_fusion.17), channel_id=1, source_target_pairs={{0,1},{1,0},{2,3},{3,2},{4,5},{5,4},{6,7},{7,6},{8,9},{9,8},{10,11... | collective-permute-start | bytes 3145736 | tf_op jit(solution)/shard_map/ppermute | solution.py:350
  669.5 31.6 %collective-permute-start.36 = (bf16[2,2,1,1,32,4096]{5,4,3,2,1,0:T(8,128)(2,1)}, bf16[2,2,1,1,32,4096]{5,4,3,2,1,0:T(8,128)(2,1)}, u32[]{:S(2)}, u32[]{:S(2)}) collective-permute-start(bf16[2,2,1,1,32,4096]{5,4,3,2,1,0:T(8,128)(2,1)} %constant_dynamic-slice_fusion.16), channel_id=1, source_target_pairs={{8,10},{9,11},{10,8},{11,9},{12,14},{13,15},{14,12},{15,13},{24,26... | collective-permute-start | bytes 3145736 | tf_op jit(solution)/shard_map/ppermute | solution.py:350
  672.2 32.2 %collective-permute-start.34 = (bf16[1,1,2,64,4096]{4,3,2,1,0:T(8,128)(2,1)}, bf16[1,1,2,64,4096]{4,3,2,1,0:T(8,128)(2,1)}, u32[]{:S(2)}, u32[]{:S(2)}) collective-permute-start(bf16[1,1,2,64,4096]{4,3,2,1,0:T(8,128)(2,1)} %constant_dynamic-slice_fusion.18), channel_id=1, source_target_pairs={{0,4},{1,5},{2,6},{3,7},{4,0},{5,1},{6,2},{7,3},{8,12},{9,13},{10,... | collective-permute-start | bytes 3145736 | tf_op jit(solution)/shard_map/ppermute | solution.py:350
  679.8 29.9 %collective-permute-start.38 = (bf16[512,1536]{1,0:T(8,128)(2,1)}, bf16[512,1536]{1,0:T(8,128)(2,1)}, u32[]{:S(2)}, u32[]{:S(2)}) collective-permute-start(bf16[512,1536]{1,0:T(8,128)(2,1)} %convolution_convert_fusion.11), channel_id=1, source_target_pairs={{0,16},{16,0},{1,17},{17,1},{2,18},{18,2},{3,19},{19,3},{4,20},{20... | collective-permute-start | bytes 4718600 | tf_op jit(solution)/shard_map/ppermute | solution.py:291
  709.8 11.6 %collective-permute-start.48 = (bf16[2,1,1,1,32,4096]{5,4,3,2,1,0:T(8,128)(2,1)S(1)}, bf16[2,1,1,1,32,4096]{5,4,3,2,1,0:T(8,128)(2,1)S(1)}, u32[]{:S(2)}, u32[]{:S(2)}) collective-permute-start(bf16[2,1,1,1,32,4096]{5,4,3,2,1,0:T(8,128)(2,1)S(1)} %constant_dynamic-slice_fusion.9), channel_id=1, source_target_pairs={{8,12},{9,13},{10,14},{11,15},{12,8},{13,9},{14,10},{15,11},{24,28... | collective-permute-start | bytes 1572872 | tf_op jit(solution)/shard_map/ppermute | solution.py:350
  710.9 9.9 %collective-permute-start.47 = (f32[2,2,1,1,1665]{4,2,1,0,3:T(1,128)S(1)}, f32[2,2,1,1,1665]{4,2,1,0,3:T(1,128)S(1)}, u32[]{:S(2)}, u32[]{:S(2)}) collective-permute-start(f32[2,2,1,1,1665]{4,2,1,0,3:T(1,128)S(1)} %constant_dynamic-slice_fusion.10), channel_id=1, source_target_pairs={{0,1},{1,0},{2,3},{3,2},{4,5},{5,4},{6,7},{7,6},{8,9},{9,8},{10,11... | collective-permute-start | bytes 79928 | tf_op jit(solution)/shard_map/ppermute | solution.py:350
  712.3 24.0 %collective-permute-start.45 = (bf16[1,1,1,256,1024]{4,3,2,1,0:T(8,128)(2,1)S(1)}, bf16[1,1,1,256,1024]{4,3,2,1,0:T(8,128)(2,1)S(1)}, u32[]{:S(2)}, u32[]{:S(2)}) collective-permute-start(bf16[1,1,1,256,1024]{4,3,2,1,0:T(8,128)(2,1)S(1)} %constant_dynamic-slice_fusion.11), channel_id=1, source_target_pairs={{0,2},{1,3},{2,0},{3,1},{4,6},{5,7},{6,4},{7,5},{8,10},{9,11},{10,... | collective-permute-start | bytes 1572872 | tf_op jit(solution)/shard_map/ppermute | solution.py:350
  713.8 12.2 %collective-permute-start.44 = (bf16[1,1,1,64,4096]{4,3,2,1,0:T(8,128)(2,1)S(1)}, bf16[1,1,1,64,4096]{4,3,2,1,0:T(8,128)(2,1)S(1)}, u32[]{:S(2)}, u32[]{:S(2)}) collective-permute-start(bf16[1,1,1,64,4096]{4,3,2,1,0:T(8,128)(2,1)S(1)} %constant_dynamic-slice_fusion.12), channel_id=1, source_target_pairs={{0,1},{1,0},{2,3},{3,2},{4,5},{5,4},{6,7},{7,6},{8,9},{9,8},{10,11... | collective-permute-start | bytes 1572872 | tf_op jit(solution)/shard_map/ppermute | solution.py:350
  715.9 21.4 %collective-permute-start.43 = (bf16[1,2,2,64,1024]{4,3,2,1,0:T(8,128)(2,1)S(1)}, bf16[1,2,2,64,1024]{4,3,2,1,0:T(8,128)(2,1)S(1)}, u32[]{:S(2)}, u32[]{:S(2)}) collective-permute-start(bf16[1,2,2,64,1024]{4,3,2,1,0:T(8,128)(2,1)S(1)} %constant_dynamic-slice_fusion.13), channel_id=1, source_target_pairs={{0,4},{1,5},{2,6},{3,7},{4,0},{5,1},{6,2},{7,3},{8,12},{9,13},{10,... | collective-permute-start | bytes 1572872 | tf_op jit(solution)/shard_map/ppermute | solution.py:350
  720.8 20.5 %collective-permute-start.42 = (bf16[2,1,2,64,1536]{4,3,2,1,0:T(8,128)(2,1)S(1)}, bf16[2,1,2,64,1536]{4,3,2,1,0:T(8,128)(2,1)S(1)}, u32[]{:S(2)}, u32[]{:S(2)}) collective-permute-start(bf16[2,1,2,64,1536]{4,3,2,1,0:T(8,128)(2,1)S(1)} %constant_dynamic-slice_fusion.14), channel_id=1, source_target_pairs={{0,2},{1,3},{2,0},{3,1},{4,6},{5,7},{6,4},{7,5},{8,10},{9,11},{10,... | collective-permute-start | bytes 2359304 | tf_op jit(solution)/shard_map/ppermute | solution.py:350
  721.3 21.6 %collective-permute-start.41 = (bf16[2,2,1,64,1536]{4,3,2,1,0:T(8,128)(2,1)S(1)}, bf16[2,2,1,64,1536]{4,3,2,1,0:T(8,128)(2,1)S(1)}, u32[]{:S(2)}, u32[]{:S(2)}) collective-permute-start(bf16[2,2,1,64,1536]{4,3,2,1,0:T(8,128)(2,1)S(1)} %constant_dynamic-slice_fusion.15), channel_id=1, source_target_pairs={{0,1},{1,0},{2,3},{3,2},{4,5},{5,4},{6,7},{7,6},{8,9},{9,8},{10,11... | collective-permute-start | bytes 2359304 | tf_op jit(solution)/shard_map/ppermute | solution.py:350
  726.1 33.2 %collective-permute-start.46 = (bf16[512,1024]{1,0:T(8,128)(2,1)S(1)}, bf16[512,1024]{1,0:T(8,128)(2,1)}, u32[]{:S(2)}, u32[]{:S(2)}) collective-permute-start(bf16[512,1024]{1,0:T(8,128)(2,1)S(1)} %copy-done.128), channel_id=1, source_target_pairs={{0,0},{16,8},{8,16},{24,24},{1,1},{17,9},{9,17},{25,25},{2,2},{18,... | collective-permute-start | bytes 3145736 | tf_op jit(solution)/shard_map/ppermute | solution.py:291
  759.3 27.5 %collective-permute-start.51 = (bf16[2,1,1,64,1536]{4,3,2,1,0:T(8,128)(2,1)S(1)}, bf16[2,1,1,64,1536]{4,3,2,1,0:T(8,128)(2,1)S(1)}, u32[]{:S(2)}, u32[]{:S(2)}) collective-permute-start(bf16[2,1,1,64,1536]{4,3,2,1,0:T(8,128)(2,1)S(1)} %constant_dynamic-slice_fusion.8), channel_id=1, source_target_pairs={{0,2},{1,3},{2,0},{3,1},{4,6},{5,7},{6,4},{7,5},{8,10},{9,11},{10,... | collective-permute-start | bytes 1179656 | tf_op jit(solution)/shard_map/ppermute | solution.py:350
  759.4 27.4 %collective-permute-start.52 = (bf16[1,1,2,64,1536]{4,3,2,1,0:T(8,128)(2,1)S(1)}, bf16[1,1,2,64,1536]{4,3,2,1,0:T(8,128)(2,1)S(1)}, u32[]{:S(2)}, u32[]{:S(2)}) collective-permute-start(bf16[1,1,2,64,1536]{4,3,2,1,0:T(8,128)(2,1)S(1)} %constant_dynamic-slice_fusion.7), channel_id=1, source_target_pairs={{0,4},{1,5},{2,6},{3,7},{4,0},{5,1},{6,2},{7,3},{8,12},{9,13},{10,... | collective-permute-start | bytes 1179656 | tf_op jit(solution)/shard_map/ppermute | solution.py:350
  759.8 15.9 %collective-permute-start.64 = (bf16[32,4096]{1,0:T(8,128)(2,1)S(1)}, bf16[32,4096]{1,0:T(8,128)(2,1)S(1)}, u32[]{:S(2)}, u32[]{:S(2)}) collective-permute-start(bf16[32,4096]{1,0:T(8,128)(2,1)S(1)} %slice_bitcast_fusion.2), channel_id=1, source_target_pairs={{8,0},{9,1},{10,2},{11,3},{12,4},{13,5},{14,6},{15,7},{24,16},{25,... | collective-permute-start | bytes 786440 | tf_op jit(solution)/shard_map/ppermute | solution.py:332
  761.3 21.0 %collective-permute-start.53 = (bf16[1,2,1,64,1024]{4,3,2,1,0:T(8,128)(2,1)S(1)}, bf16[1,2,1,64,1024]{4,3,2,1,0:T(8,128)(2,1)S(1)}, u32[]{:S(2)}, u32[]{:S(2)}) collective-permute-start(bf16[1,2,1,64,1024]{4,3,2,1,0:T(8,128)(2,1)S(1)} %constant_dynamic-slice_fusion.6), channel_id=1, source_target_pairs={{0,1},{1,0},{2,3},{3,2},{4,5},{5,4},{6,7},{7,6},{8,9},{9,8},{10,11... | collective-permute-start | bytes 786440 | tf_op jit(solution)/shard_map/ppermute | solution.py:350
  761.4 19.0 %collective-permute-start.54 = (f32[2,1,1,1,1665]{4,2,1,0,3:T(1,128)S(1)}, f32[2,1,1,1,1665]{4,2,1,0,3:T(1,128)S(1)}, u32[]{:S(2)}, u32[]{:S(2)}) collective-permute-start(f32[2,1,1,1,1665]{4,2,1,0,3:T(1,128)S(1)} %constant_dynamic-slice_fusion.5), channel_id=1, source_target_pairs={{0,2},{1,3},{2,0},{3,1},{4,6},{5,7},{6,4},{7,5},{8,10},{9,11},{10,... | collective-permute-start | bytes 39968 | tf_op jit(solution)/shard_map/ppermute | solution.py:350
  775.7 33.0 %collective-permute-start.49 = (bf16[257,768]{1,0:T(8,128)(2,1)}, bf16[257,768]{1,0:T(8,128)(2,1)}, u32[]{:S(2)}, u32[]{:S(2)}) collective-permute-start(bf16[257,768]{1,0:T(8,128)(2,1)} %fusion.176), channel_id=1, source_target_pairs={{0,0},{16,8},{1,1},{17,9},{2,2},{18,10},{3,3},{19,11},{4,4},{20,12... | collective-permute-start | bytes 1184264 | tf_op jit(solution)/shard_map/ppermute | solution.py:291
  780.3 35.1 %collective-permute-start.63 = (bf16[256,1024]{1,0:T(8,128)(2,1)}, bf16[256,1024]{1,0:T(8,128)(2,1)}, u32[]{:S(2)}, u32[]{:S(2)}) collective-permute-start(bf16[256,1024]{1,0:T(8,128)(2,1)} %bitcast.103), channel_id=1, source_target_pairs={{0,0},{16,8},{8,16},{24,24},{1,1},{17,9},{9,17},{25,25},{2,2},{18,... | collective-permute-start | bytes 1572872 | tf_op jit(solution)/shard_map/ppermute | solution.py:291
  782.3 29.6 %collective-permute-start.62 = (bf16[64,4096]{1,0:T(8,128)(2,1)}, bf16[64,4096]{1,0:T(8,128)(2,1)}, u32[]{:S(2)}, u32[]{:S(2)}) collective-permute-start(bf16[64,4096]{1,0:T(8,128)(2,1)} %bitcast.100), channel_id=1, source_target_pairs={{0,0},{16,8},{8,16},{24,24},{1,1},{17,9},{9,17},{25,25},{2,2},{18,... | collective-permute-start | bytes 1572872 | tf_op jit(solution)/shard_map/ppermute | solution.py:291
  802.0 16.9 %collective-permute-start.56 = (bf16[1,1,1,64,1536]{4,3,2,1,0:T(8,128)(2,1)}, bf16[1,1,1,64,1536]{4,3,2,1,0:T(8,128)(2,1)}, u32[]{:S(2)}, u32[]{:S(2)}) collective-permute-start(bf16[1,1,1,64,1536]{4,3,2,1,0:T(8,128)(2,1)} %constant_dynamic-slice_fusion.2), channel_id=1, source_target_pairs={{0,1},{1,0},{2,3},{3,2},{4,5},{5,4},{6,7},{7,6},{8,9},{9,8},{10,11... | collective-permute-start | bytes 589832 | tf_op jit(solution)/shard_map/ppermute | solution.py:350
  803.7 15.3 %collective-permute-start.55 = (bf16[1,1,1,64,1536]{4,3,2,1,0:T(8,128)(2,1)}, bf16[1,1,1,64,1536]{4,3,2,1,0:T(8,128)(2,1)}, u32[]{:S(2)}, u32[]{:S(2)}) collective-permute-start(bf16[1,1,1,64,1536]{4,3,2,1,0:T(8,128)(2,1)} %constant_dynamic-slice_fusion.3), channel_id=1, source_target_pairs={{0,4},{1,5},{2,6},{3,7},{4,0},{5,1},{6,2},{7,3},{8,12},{9,13},{10,... | collective-permute-start | bytes 589832 | tf_op jit(solution)/shard_map/ppermute | solution.py:350
  808.8 10.2 %collective-permute-start.57 = (bf16[1,1,1,64,1024]{4,3,2,1,0:T(8,128)(2,1)S(1)}, bf16[1,1,1,64,1024]{4,3,2,1,0:T(8,128)(2,1)S(1)}, u32[]{:S(2)}, u32[]{:S(2)}) collective-permute-start(bf16[1,1,1,64,1024]{4,3,2,1,0:T(8,128)(2,1)S(1)} %constant_dynamic-slice_fusion.1), channel_id=1, source_target_pairs={{0,2},{1,3},{2,0},{3,1},{4,6},{5,7},{6,4},{7,5},{8,10},{9,11},{10,... | collective-permute-start | bytes 393224 | tf_op jit(solution)/shard_map/ppermute | solution.py:350
  815.5 32.3 %collective-permute-start.50 = (bf16[129,768]{1,0:T(8,128)(2,1)S(1)}, bf16[129,768]{1,0:T(8,128)(2,1)S(1)}, u32[]{:S(2)}, u32[]{:S(2)}) collective-permute-start(bf16[129,768]{1,0:T(8,128)(2,1)S(1)} %fusion.190), channel_id=1, source_target_pairs={{0,16},{1,17},{2,18},{3,19},{4,20},{5,21},{6,22},{7,23},{8,24},{9,... | collective-permute-start | bytes 594440 | tf_op jit(solution)/shard_map/ppermute | solution.py:984
  822.6 14.7 %collective-permute-start.59 = (f32[449]{0:T(512)S(1)}, f32[449]{0:T(512)S(1)}, u32[]{:S(2)}, u32[]{:S(2)}) collective-permute-start(f32[449]{0:T(512)S(1)} %pad_maximum_fusion.20), channel_id=1, source_target_pairs={{0,8},{1,9},{2,10},{3,11},{4,12},{5,13},{6,14},{7,15},{8,0},{9,1},... | collective-permute-start | bytes 5396 | tf_op jit(solution)/shard_map/ppermute | solution.py:337
  824.0 29.4 %collective-permute-start.60 = (bf16[64,4096]{1,0:T(8,128)(2,1)S(1)}, bf16[64,4096]{1,0:T(8,128)(2,1)S(1)}, u32[]{:S(2)}, u32[]{:S(2)}) collective-permute-start(bf16[64,4096]{1,0:T(8,128)(2,1)S(1)} %pad_maximum_fusion.13), channel_id=1, source_target_pairs={{0,0},{16,8},{8,16},{24,24},{1,1},{17,9},{9,17},{25,25},{2,2},{18,... | collective-permute-start | bytes 1572872 | tf_op jit(solution)/shard_map/ppermute | solution.py:291
  835.3 12.0 %collective-permute-start.61 = (f32[768]{0:T(1024)S(1)}, f32[768]{0:T(1024)S(1)}, u32[]{:S(2)}, u32[]{:S(2)}) collective-permute-start(f32[768]{0:T(1024)S(1)} %slice_reduce_fusion.4), channel_id=1, source_target_pairs={{0,0},{16,8},{8,16},{24,24},{1,1},{17,9},{9,17},{25,25},{2,2},{18,... | collective-permute-start | bytes 9224 | tf_op jit(solution)/shard_map/ppermute | solution.py:291
  (111 other events, 1794.0 us)
Sparse Core Ops, SparseCore 0:
  11.5 99.5 all-gather.5
  170.4 135.6 all-gather.7
  528.0 90.3 all-gather.11
  621.8 74.8 all-gather.9
